TPU v7x, 256 devices: a whole 4x4x8 slice. The times are simulated.
256 devices in a mesh: seq: 64 (over z, y, core), tp: 4 (over x).
Axes of the slice: x: 4, y: 4, z: 8, core: 2. Of those that a mesh axis runs over, the one named last changes fastest.
Arguments:
- tokens: bfloat16 [16384, 2048], P('seq', 'tp'), may hold values from -6 to 6
- norm_gain: float32 [2048], replicated, may hold values from 0.1 to 1.9
- w_query: bfloat16 [2048, 1024], P(None, 'tp'), may hold values from -0.125 to 0.125
- w_key: bfloat16 [2048, 1024], P(None, 'tp'), may hold values from -0.125 to 0.125
- w_value: bfloat16 [2048, 2048], P(None, 'tp'), may hold values from -0.125 to 0.125
- w_gate_out: bfloat16 [2048, 2048], P(None, 'tp'), may hold values from -0.125 to 0.125
- gate_down: bfloat16 [2048, 16], replicated, may hold values from -0.09272438 to 0.09272438
- gate_up: bfloat16 [16, 1024], P(None, 'tp'), may hold values from -1 to 1.2625
- gate_bias: float32 [1024], P('tp'), may hold values from 1 to 8
- head_gain: float32 [2048], P('tp'), may hold values from 0.1 to 1.9
- w_out: bfloat16 [2048, 2048], P('tp'), may hold values from -0.125 to 0.125
- request_ids: int32 [16384], P('seq'), may hold values from 0 to 17, as said below
Outputs:
- mixed: bfloat16 [16384, 2048], P('seq', 'tp')
Inputs may be any that keep to these rules, and one draw needn't show every extreme that they name: `request_ids`: request numbers never fall along the tokens; every request of 0 to 17 holds 1 to 8192 tokens; request 0 holds fewer than 256 tokens and request 1 holds exactly 8192.
All inputs are finite; a program needn't handle non-finite values.
Results may differ from a plain program's by a relative error of at most 0.015.
Values may be sent and summed in bfloat16 or wider, within the bound.
No kernel may reach another device: no remote copies, remote signals or barrier semaphores. Data moves between devices by JAX's collectives and lax.ppermute only.
A program may use at most 128 MiB of HBM per device.

v0:
```python
import jax
import jax.numpy as jnp
from jax import lax
from jax.sharding import PartitionSpec as P

K = 256
V = 512
C = 64


def from_behind(block, axis, distance):
    devices = range(lax.axis_size(axis))
    route = [(i - distance, i) for i in devices if i - distance in devices]
    return lax.ppermute(block, axis, route)


def entering(shard, axis, combine, identity):
    count, position = (lax.axis_size(axis), lax.axis_index(axis))
    everything = jax.tree.map(lambda part: lax.all_gather(part, axis), shard)
    start = jax.tree.map(
        lambda part, zero: jnp.broadcast_to(jnp.asarray(zero, part.dtype), part.shape),
        shard,
        identity,
    )

    def turn(k, before):
        reached = k < position
        new = combine(before, jax.tree.map(lambda part: part[k], everything))
        return jax.tree.map(lambda a, b: jnp.where(reached, a, b), new, before)

    return lax.fori_loop(0, count, turn, start)


def rms(value, gain):
    return value * lax.rsqrt(jnp.mean(value * value, axis=-1, keepdims=True) + 1e-05) * gain


def group_terms(query, key, value, log_decay_rate, ids, prev):
    cum = jnp.cumsum(log_decay_rate, axis=0)
    query_decayed = (query.astype(jnp.float32) * jnp.exp(cum) * K ** (-0.5)).astype(jnp.bfloat16)
    kinv = (key.astype(jnp.float32) * jnp.exp(-cum)).astype(jnp.bfloat16)
    scores = jnp.dot(query_decayed, kinv.T, preferred_element_type=jnp.float32)
    place = jnp.arange(query.shape[0], dtype=jnp.int32)
    allowed = (place[None, :] <= place[:, None]) & (ids[None, :] == ids[:, None])
    weights = jnp.where(allowed, scores, 0.0).astype(jnp.bfloat16)
    intra = jnp.dot(weights, value, preferred_element_type=jnp.float32)
    causal_mask = ids == prev
    keep = (ids == ids[-1]).astype(jnp.float32)[:, None]
    kend = (key.astype(jnp.float32) * jnp.exp(cum[-1:] - cum) * keep).astype(jnp.bfloat16)
    fresh = jnp.dot(kend.T, value, preferred_element_type=jnp.float32)
    decay = jnp.exp(cum[-1]) * (ids[-1] == prev).astype(jnp.float32)
    return (query_decayed, intra, causal_mask, fresh, decay)


def local_pass(query, key, value, log_decay_rate, request_id_block, prev_device):

    def step(carry, item):
        state, product, prev = carry
        qc, kc, vc, gc, sc = item
        query_decayed, intra, causal_mask, fresh, decay = group_terms(qc, kc, vc, gc, sc, prev)
        return (
            (decay[:, None] * state + fresh, decay * product, sc[-1]),
            (query_decayed, intra, causal_mask, state, product),
        )

    start = (jnp.zeros((K, V), jnp.float32), jnp.ones((K,), jnp.float32), prev_device)
    (state, product, _), stacked = lax.scan(
        step, start, (query, key, value, log_decay_rate, request_id_block)
    )
    return (state, product, stacked)


def merge_results(earlier, later):
    return (earlier[0] * later[0], later[0][..., None] * earlier[1] + later[1])


def per_device(
    tokens,
    norm_gain,
    w_query,
    w_key,
    w_value,
    w_gate_out,
    gate_down,
    gate_up,
    gate_bias,
    head_gain,
    w_out,
    request_ids,
):
    whole = lax.all_gather(tokens, "tp", axis=1, tiled=True)
    rows = whole.shape[0]
    blocks = rows // C
    heads = w_value.shape[1] // V
    normed = rms(whole.astype(jnp.float32), norm_gain).astype(jnp.bfloat16)
    low = jnp.dot(normed, gate_down, preferred_element_type=jnp.float32).astype(jnp.bfloat16)
    log_decay_rate = (
        jax.nn.log_sigmoid(jnp.dot(low, gate_up, preferred_element_type=jnp.float32) + gate_bias)
        / 16.0
    )
    query = jnp.dot(normed, w_query, preferred_element_type=jnp.float32).astype(jnp.bfloat16)
    key = jnp.dot(normed, w_key, preferred_element_type=jnp.float32).astype(jnp.bfloat16)
    value = jnp.dot(normed, w_value, preferred_element_type=jnp.float32).astype(jnp.bfloat16)
    opengate = jnp.dot(normed, w_gate_out, preferred_element_type=jnp.float32)
    edge = from_behind(request_ids[-1:] + 1, "seq", 1)
    prev_device = edge[0] - 1
    request_id_block = request_ids.reshape(blocks, C)
    qh = query.reshape(blocks, C, K)
    kh = key.reshape(blocks, C, K)
    vh = value.reshape(blocks, C, V)
    gh = log_decay_rate.reshape(blocks, C, K)
    state, product, stacked = local_pass(qh, kh, vh, gh, request_id_block, prev_device)
    finals = [state]
    products = [product]
    identity = (jnp.ones((heads, K), jnp.float32), jnp.zeros((heads, K, V), jnp.float32))
    _, incoming = entering((jnp.stack(products), jnp.stack(finals)), "seq", merge_results, identity)
    query_decayed, intra, causal_mask, entry, entry_product = stacked
    entry_exact_value = entry + entry_product[:, :, None] * incoming[0][None]
    inter = jnp.einsum(
        "axo,aoe->axe",
        query_decayed.astype(jnp.float32),
        entry_exact_value,
        precision=lax.Precision.HIGHEST,
    )
    attn = (intra + jnp.where(causal_mask[..., None], inter, 0.0)).reshape(rows, V)
    gated = rms(attn, head_gain) * jax.nn.silu(opengate)
    results = gated.astype(jnp.bfloat16)
    partial_out = jnp.dot(results, w_out, preferred_element_type=jnp.float32)
    mixed = lax.psum_scatter(
        partial_out.astype(jnp.bfloat16), "tp", scatter_dimension=1, tiled=True
    )
    return mixed


def solution(mesh):
    return jax.shard_map(
        per_device,
        mesh=mesh,
        in_specs=(
            P("seq", "tp"),
            P(),
            P(None, "tp"),
            P(None, "tp"),
            P(None, "tp"),
            P(None, "tp"),
            P(),
            P(None, "tp"),
            P("tp"),
            P("tp"),
            P("tp", None),
            P("seq"),
        ),
        out_specs=P("seq", "tp"),
        check_vma=False,
    )
```

profile of v0, /device:TPU:97, one launch (start us, length us, event | category | flops | bytes accessed | tf_op | source)
XLA Modules:
  0.0 333.4 jit_solution(505680258630200465)
XLA Ops:
  7.3 1.3 slice.13
  9.2 4.5 %collective-permute-start = (s32[1]{0:T(128)}, s32[1]{0:T(128)}, u32[]{:S(2)}, u32[]{:S(2)}) collective-permute-start(s32[1]{0:T(128)} %add.82), channel_id=1, source_target_pairs={{0,4},{4,8},{8,12},{12,16},{16,20},{20,24},{24,28},{28,32},{32,36}... | collective-permute-start | bytes 20 | tf_op jit(solution)/shard_map/ppermute | solution.py:14
  15.0 21.6 %all-gather.6.cloned.1.call-done = bf16[256,2048]{1,0:T(8,128)(2,1)} async-done(((bf16[256,512]{1,0:T(8,128)(2,1)}), bf16[256,2048]{1,0:T(8,128)(2,1)}) %all-gather.6.cloned.1.call-update) | async-done | bytes 1048592 | tf_op jit(solution)/shard_map/all_gather | solution.py:91
  36.7 1.5 fusion.42
  38.2 2.8 convolution_convert_fusion.1
  43.2 2.0 fusion.58
  45.1 29.6 %while.41 = (s32[]{:T(128)}, f32[256,512]{1,0:T(8,128)S(1)}, f32[256]{0:T(256)S(1)}, s32[]{:T(128)}, bf16[4,64,256]{2,1,0:T(8,128)(2,1)}, /*index=5*/f32[4,64,51...) while((s32[]{:T(128)}, f32[256,512]{1,0:T(8,128)S(1)}, ...), condition=%wide.region_3.4_spmd.clone.clone, body=%wide.region_1.3_spmd.clone.sunk.clone | while | flops 24925124 | bytes 3067847 | solution.py:67
  48.4 1.3 dynamic_update_slice.42
  55.8 1.3 dynamic_update_slice.42
  63.2 1.3 dynamic_update_slice.42
  70.7 1.3 dynamic_update_slice.42
  75.7 45.0 %all-gather.2 = f32[64,1,256]{2,1,0:T(1,128)S(1)} all-gather(f32[1,1,256]{2,1,0:T(1,128)S(1)} %bitcast.158), channel_id=2, replica_groups=mesh['seq'=64,'tp'=4] {'seq'}, dimensions={0}, use_global_device_ids=true | all-gather | bytes 66560 | tf_op jit(solution)/shard_map/all_gather | solution.py:19
  120.7 98.8 %all-gather.8.cloned.1.call-done = f32[16384,512]{1,0:T(8,128)} async-done(((f32[256,512]{1,0:T(8,128)}), f32[16384,512]{1,0:T(8,128)}) %all-gather.8.cloned.1.call-update) | async-done | bytes 33554448 | tf_op jit(solution)/shard_map/all_gather | solution.py:19
  219.5 77.7 %while.42 = (s32[]{:T(128)}, f32[1,256,512]{2,1,0:T(8,128)S(1)}, s32[]{:T(128)}, f32[64,1,256]{2,1,0:T(1,128)S(1)}, f32[64,1,256,512]{3,2,1,0:T(8,128)}) while((s32[]{:T(128)}, f32[1,256,512]{2,1,0:T(8,128)S(1)}, s32[]{:T(128)}, f32[64,1,256]{2,1,0:T(1,128)S(1)}, f32[64,1,256,512]{3,2,1,0:T(8,128)}) %tuple.81), condition=%wide.region_5.6_spmd.clone.clone, body=%wide.region_4.5_spmd.clone.sunk.clone | while | flops 524292 | bytes 1576025 | solution.py:31
  219.5 1.2 fusion.104
  220.7 1.2 fusion.104
  223.1 1.2 fusion.104
  225.6 1.2 fusion.104
  228.0 1.2 fusion.104
  230.4 1.2 fusion.104
  297.3 2.7 fusion.48
  300.3 2.8 fusion.56
  303.0 1.7 convolution_convert_fusion
  304.8 22.1 %reduce-scatter.2.cloned.1.call-done = bf16[256,512]{1,0:T(8,128)(2,1)} async-done(((bf16[256,2048]{1,0:T(8,128)(2,1)}), bf16[256,512]{1,0:T(8,128)(2,1)}) %reduce-scatter.2.cloned.1.call-update) | async-done | bytes 262160 | tf_op jit(solution)/shard_map/reduce_scatter | solution.py:129
  (242 shorter events, 92.4 us)
Async XLA Ops:
  6.5 296.5 %copy-start = (bf16[512,2048]{1,0:T(8,128)(2,1)S(1)}, bf16[512,2048]{1,0:T(8,128)(2,1)}, u32[]{:S(2)}) copy-start(bf16[512,2048]{1,0:T(8,128)(2,1)} %param.26) | copy-start | bytes 6291460
  6.5 30.1 %all-gather.6.cloned.1.call-start = ((), (), s32[]{:S(2)}) async-start(), calls=%async_computation.1 | async-start | bytes 1310720 | tf_op jit(solution)/shard_map/all_gather | solution.py:91
  7.3 212.2 %all-gather.8.cloned.1.call-start = ((), (), s32[]{:S(2)}) async-start(), calls=%async_computation.3 | async-start | bytes 34078720 | tf_op jit(solution)/shard_map/all_gather | solution.py:19
  9.2 5.2 %collective-permute-start = (s32[1]{0:T(128)}, s32[1]{0:T(128)}, u32[]{:S(2)}, u32[]{:S(2)}) collective-permute-start(s32[1]{0:T(128)} %add.82), channel_id=1, source_target_pairs={{0,4},{4,8},{8,12},{12,16},{16,20},{20,24},{24,28},{28,32},{32,36}... | collective-permute-start | bytes 20 | tf_op jit(solution)/shard_map/ppermute | solution.py:14
  38.2 4.6 %copy-start.6 = (f32[256]{0:T(256)}, f32[256]{0:T(256)S(1)}, u32[]{:S(2)}) copy-start(f32[256]{0:T(256)S(1)} %add_rsqrt_fusion.1) | copy-start | bytes 3076
  38.2 2.9 copy-start.2
  38.2 2.9 copy-start.11
  38.2 2.9 copy-start.15
  41.1 1.2 copy-start.12
  42.3 0.8 copy-start.13
  42.3 0.8 copy-start.14
  42.3 0.8 copy-start.18
  46.6 4.7 %copy-start.8 = (pred[4,64]{1,0:T(4,128)(4,1)S(1)}, pred[4,64]{1,0:T(4,128)(4,1)}, u32[]{:S(2)}) copy-start(pred[4,64]{1,0:T(4,128)(4,1)} %get-tuple-element.489) | copy-start | bytes 772 | tf_op jit(solution)/shard_map/while
  54.0 4.7 %copy-start.8 = (pred[4,64]{1,0:T(4,128)(4,1)S(1)}, pred[4,64]{1,0:T(4,128)(4,1)}, u32[]{:S(2)}) copy-start(pred[4,64]{1,0:T(4,128)(4,1)} %get-tuple-element.489) | copy-start | bytes 772 | tf_op jit(solution)/shard_map/while
  61.4 4.7 %copy-start.8 = (pred[4,64]{1,0:T(4,128)(4,1)S(1)}, pred[4,64]{1,0:T(4,128)(4,1)}, u32[]{:S(2)}) copy-start(pred[4,64]{1,0:T(4,128)(4,1)} %get-tuple-element.489) | copy-start | bytes 772 | tf_op jit(solution)/shard_map/while
  68.8 4.7 %copy-start.8 = (pred[4,64]{1,0:T(4,128)(4,1)S(1)}, pred[4,64]{1,0:T(4,128)(4,1)}, u32[]{:S(2)}) copy-start(pred[4,64]{1,0:T(4,128)(4,1)} %get-tuple-element.489) | copy-start | bytes 772 | tf_op jit(solution)/shard_map/while
  75.6 251.3 %reduce-scatter.2.cloned.1.call-start = ((), (), s32[]{:S(2)}) async-start(), calls=%async_computation.2 | async-start | bytes 1310720 | tf_op jit(solution)/shard_map/reduce_scatter | solution.py:129
  219.4 77.7 %copy-start.4 = (bf16[4,64,256]{2,1,0:T(8,128)(2,1)S(1)}, bf16[4,64,256]{2,1,0:T(8,128)(2,1)}, u32[]{:S(2)}) copy-start(bf16[4,64,256]{2,1,0:T(8,128)(2,1)} %get-tuple-element.179) | copy-start | bytes 393220
  219.4 77.8 %copy-start.5 = (f32[4,256]{1,0:T(4,128)S(1)}, f32[4,256]{1,0:T(4,128)}, u32[]{:S(2)}) copy-start(f32[4,256]{1,0:T(4,128)} %get-tuple-element.181) | copy-start | bytes 12292
  219.4 77.8 %copy-start.10 = (pred[4,64]{1,0:T(4,128)(4,1)S(1)}, pred[4,64]{1,0:T(4,128)(4,1)}, u32[]{:S(2)}) copy-start(pred[4,64]{1,0:T(4,128)(4,1)} %get-tuple-element.178) | copy-start | bytes 772
  297.2 2.8 copy-start.3
  297.2 3.0 copy-start.7
  297.2 3.0 copy-start.16
  297.2 3.0 copy-start.17
  (5 other events, 3.2 us)
Sparse Core Ops, SparseCore 0:
  9.2 27.4 all-gather.5
  75.7 143.6 all-gather.7
  304.9 21.9 reduce-scatter.1
where the time goes:
time: 339 us; the launch traced here: 333 us
  waiting for transfers between devices  143 us (42%)
  other arithmetic  85.8 us (25%)
  blocking collectives  45 us (13%)
  matrix products  18.1 us (5%)
  local copies, waits for them, and re-layouts  14.7 us (4%)
  between operations  14.6 us (4%)
  loops' own time  7.42 us (2%)
  starting transfers between devices  4.56 us (1%)
    all_gather x1, waiting for transfers between devices, entering(): everything = jax.tree.map(lambda part: lax.all_gather(part, axis), shard)  98.8 us
    select_n x64, other arithmetic, turn(): return jax.tree.map(lambda a, b: jnp.where(reached, a, b), new, before)  75.2 us
    all_gather x1, blocking collectives, entering(): everything = jax.tree.map(lambda part: lax.all_gather(part, axis), shard)  45 us
    reduce_scatter x1, waiting for transfers between devices, per_device(): lax.psum_scatter(partial_out.astype(jnp.bfloat16), 'tp', scatter_dimensio...  22.1 us
    all_gather x1, waiting for transfers between devices, per_device(): whole = lax.all_gather(tokens, 'tp', axis=1, tiled=True)  21.6 us
  transfers between devices with their start and end apart: 4, of which 3 were waited for; matrix products, arithmetic and copies ran while one was open for 1% of the time, Pallas kernels for 0%

commit v1 on v0

v1 whole, which is shorter than its diff:
```python
import jax
import jax.numpy as jnp
from jax import lax
from jax.experimental import pallas as pl
from jax.experimental.pallas import tpu as pltpu
from jax.sharding import PartitionSpec as P

K = 256
V = 512
C = 64
F = 512
HALF = 256
QUARTER = 64
META = 16
F32 = jnp.float32
BF = jnp.bfloat16
VM = pl.BlockSpec(memory_space=pltpu.VMEM)
SM = pl.BlockSpec(memory_space=pltpu.SMEM)


def dot(a, b, dims=((1,), (0,))):
    return lax.dot_general(a, b, (dims, ((), ())), preferred_element_type=F32)


def place():
    seq = lax.axis_index("seq")
    return lax.div(seq, 8), lax.rem(lax.div(seq, 2), 4), lax.rem(seq, 2)


def at(index, size):
    return pl.ds(pl.multiple_of(index * size, size), size)


def turn(index, distance):
    return lax.rem(index + distance, 4)


def load(ref):
    rows = ref.shape[0] - META
    state = ref[0:rows].astype(F32)
    meta = ref[rows:].astype(F32)
    return state, meta[0:1] + meta[1:2], meta[2:3], meta[3:4]


def meta_of(decay, first, last):
    high = decay.astype(BF).astype(F32)
    row = lax.broadcasted_iota(jnp.int32, (META, K), 0)
    meta = jnp.where(row == 0, high, jnp.where(row == 1, decay - high, 0.0))
    meta = jnp.where(row == 2, first, jnp.where(row == 3, last, meta))
    return meta.astype(BF)


def save(ref, element):
    state, decay, first, last = element
    rows = state.shape[0]
    ref[0:rows] = state.astype(BF)
    ref[rows:] = meta_of(decay, first, last)


def joined(earlier, later):
    factor = jnp.where(later[2] == earlier[3], later[1], 0.0)
    return (later[0] + factor * earlier[0], factor * earlier[1], earlier[2], later[3])


def pick(cond, a, b):
    return jax.tree.map(lambda u, v: jnp.where(cond, u, v), a, b)


def block_cumsum(rate):
    row = lax.broadcasted_iota(jnp.int32, (4 * C, 4 * C), 0)
    col = lax.broadcasted_iota(jnp.int32, (4 * C, 4 * C), 1)
    mask = ((row >= col) & (row // C == col // C)).astype(BF)
    one = rate.astype(BF)
    rest = rate - one.astype(F32)
    two = rest.astype(BF)
    three = (rest - two.astype(F32)).astype(BF)
    return dot(mask, three) + dot(mask, two) + dot(mask, one)


def front_kernel(t0, t1, t2, t3, gain, wk, wv, gd, gu, bias, idc, ids,
                 normed, key_o, value_o, cum_o, keep_o, send_o):
    x = lax.axis_index("tp")
    _, _, c = place()
    parts = [(t0, x), (t1, turn(x, 3)), (t2, turn(x, 1)), (t3, turn(x, 2))]
    squares = 0.0
    for ref, _ in parts:
        wide = ref[...].astype(F32)
        squares = squares + jnp.sum(wide * wide, axis=1, keepdims=True)
    scale = lax.rsqrt(squares * (1.0 / 2048) + 1e-05)
    key, value, low = 0.0, 0.0, 0.0
    for ref, owner in parts:
        part = (ref[...].astype(F32) * scale * gain[owner]).astype(BF)
        normed[owner] = part
        key = key + dot(part, wk[at(owner, F), :])
        value = value + dot(part, wv[at(owner, F), :])
        low = low + dot(part, gd[:, at(owner, F)], ((1,), (1,)))
    rate = dot(low.astype(BF), gu[...]) + bias[...]
    rate = (jnp.minimum(rate, 0.0) - jnp.log1p(jnp.exp(-jnp.abs(rate)))) * (1.0 / 16)
    key = key.astype(BF)
    key_o[...] = key
    value_o[...] = value.astype(BF)
    cum = block_cumsum(rate)
    cum_o[...] = cum
    ends = [cum[C * b + C - 1:C * b + C] for b in range(4)]
    after = [ends[1] + ends[2] + ends[3], ends[2] + ends[3], ends[3], jnp.zeros_like(ends[3])]
    first, last = ids[0], ids[4 * C - 1]
    keep = (idc[...] == last).astype(F32)
    ending = []
    for b in range(4):
        rows = slice(C * b, C * b + C)
        left = jnp.exp(after[b] + (ends[b] - cum[rows]))
        ending.append((key[rows].astype(F32) * left * keep[rows]).astype(BF))
    ending = jnp.concatenate(ending, axis=0)
    decay = jnp.exp(ends[0] + after[0])
    decay = jnp.where(first == last, decay, 0.0)
    meta = meta_of(decay, first.astype(F32), last.astype(F32))
    for ref, side in ((keep_o, c), (send_o, 1 - c)):
        ref[0:HALF] = dot(value_o[:, at(side, HALF)], ending, ((0,), (0,))).astype(BF)
        ref[HALF:] = meta


def inner_kernel(normed, wq, wg, key_r, value_r, cum_r, idc, idr, head_gain,
                 query_o, attn_o, gate_o):
    query, gate = 0.0, 0.0
    for i in range(4):
        part = normed[i]
        query = query + dot(part, wq[i * F:(i + 1) * F, :])
        gate = gate + dot(part, wg[i * F:(i + 1) * F, :])
    gate_o[...] = gate / (1.0 + jnp.exp(-gate)) * head_gain[...]
    query = query.astype(BF).astype(F32) * (K ** -0.5)
    key = key_r[...].astype(F32)
    cum = cum_r[...]
    ends = [cum[C * b + C - 1:C * b + C] for b in range(4)]
    before = [jnp.zeros_like(ends[0])]
    for b in range(3):
        before.append(before[-1] + ends[b])
    total = [before[b] + cum[C * b:C * b + C] for b in range(4)]
    for b in range(4):
        rows = slice(C * b, C * b + C)
        query_o[rows] = (query[rows] * jnp.exp(total[b])).astype(BF)
        decayed = (query[rows] * jnp.exp(cum[rows])).astype(BF)
        keys = [(key[C * j:C * j + C] * jnp.exp(before[b] - total[j])).astype(BF) for j in range(b)]
        keys.append((key[rows] * jnp.exp(-cum[rows])).astype(BF))
        keys = jnp.concatenate(keys, axis=0)
        scores = dot(decayed, keys, ((1,), (1,)))
        row = lax.broadcasted_iota(jnp.int32, scores.shape, 0) + C * b
        col = lax.broadcasted_iota(jnp.int32, scores.shape, 1)
        allowed = (col <= row) & (idr[:, 0:C * b + C] == idc[rows])
        weights = jnp.where(allowed, scores, 0.0).astype(BF)
        attn_o[rows] = dot(weights, value_r[0:C * b + C])


def pair_kernel(mine, other, own, s1, s2, s3, scratch):
    _, y, c = place()
    a, b = load(mine), load(other)
    total = joined(pick(c == 0, a, b), pick(c == 0, b, a))
    scratch[...] = total[0].astype(BF)
    meta = meta_of(*total[1:])
    for ref, d in ((own, 0), (s1, 1), (s2, 3), (s3, 2)):
        ref[0:QUARTER] = scratch[at(turn(y, d), QUARTER), :]
        ref[QUARTER:] = meta


def stack_rows(parts, stack):
    _, y, _ = place()
    for ref, d in zip(parts, (0, 3, 1, 2)):
        stack[turn(y, d)] = ref[...]
    return [load(stack.at[i]) for i in range(4)]


def row_kernel(own, r1, r2, r3, total, stack):
    chips = stack_rows((own, r1, r2, r3), stack)
    run = chips[0]
    for chip in chips[1:]:
        run = joined(run, chip)
    save(total, run)


def two_rows_kernel(row, before, total):
    save(total, joined(load(before), load(row)))


def spread_kernel(own, r1, r2, r3, one, two, far, own_o, s1, s2, s3, stack):
    _, y, _ = place()
    chips = stack_rows((own, r1, r2, r3), stack)
    run = joined(joined(load(far), load(two)), load(one))
    for i in range(4):
        save(stack.at[i], run)
        run = joined(run, chips[i])
    for ref, d in ((own_o, 0), (s1, 1), (s2, 3), (s3, 2)):
        ref[...] = stack[turn(y, d)]


def unpair_kernel(own, r1, r2, r3, mine, other, keep, send, scratch):
    _, y, c = place()
    for ref, d in zip((own, r1, r2, r3), (0, 3, 1, 2)):
        scratch[at(turn(y, d), QUARTER), :] = ref[0:QUARTER]
    meta = own[QUARTER:].astype(F32)
    into = (scratch[...].astype(F32), meta[0:1] + meta[1:2], meta[2:3], meta[3:4])
    after = joined(into, pick(c == 0, load(mine), load(other)))
    save(keep, pick(c == 0, into, after))
    save(send, pick(c == 0, after, into))


def back_kernel(mine, other, query, attn_r, gate, idc, w_out, own, s1, s2, s3, attn):
    x = lax.axis_index("tp")
    _, _, c = place()
    prev = mine[HALF:].astype(F32)[3:4, 0:1]
    seen = idc[...].astype(F32) == prev
    for ref, side in ((mine, c), (other, 1 - c)):
        inter = dot(query[...], ref[0:HALF], ((1,), (1,)))
        attn[:, at(side, HALF)] = attn_r[:, at(side, HALF)] + jnp.where(seen, inter, 0.0)
    full = attn[...]
    scale = lax.rsqrt(jnp.mean(full * full, axis=1, keepdims=True) + 1e-05)
    gated = (full * scale * gate[...]).astype(BF)
    for ref, d in ((s3, 2), (s1, 1), (s2, 3), (own, 0)):
        ref[...] = dot(gated, w_out[:, at(turn(x, d), F)]).astype(ref.dtype)


def call(kernel, outs, args, specs=None, scratch=(), flops=0, name=None):
    shapes = [jax.ShapeDtypeStruct(s, d) for s, d in outs]
    bytes_accessed = sum(a.size * a.dtype.itemsize for a in list(args) + shapes)
    return pl.pallas_call(
        kernel,
        out_shape=shapes,
        in_specs=specs or [VM] * len(args),
        out_specs=[VM] * len(outs),
        scratch_shapes=list(scratch),
        compiler_params=pltpu.CompilerParams(vmem_limit_bytes=24 << 20),
        cost_estimate=pl.CostEstimate(flops=flops, bytes_accessed=bytes_accessed, transcendentals=0),
        name=name,
    )(*args)


def over_tp(block, distance):
    return lax.ppermute(block, "tp", [(i, (i + distance) % 4) for i in range(4)])


def seq_route(move):
    pairs = []
    for i in range(64):
        z, y, c = move(i // 8, i // 2 % 4, i % 2)
        if z < 8:
            pairs.append((i, z * 8 + y * 2 + c))
    return pairs


def over_seq(block, move):
    return lax.ppermute(block, "seq", seq_route(move))


def over_y(blocks):
    return [
        over_seq(b, lambda z, y, c, d=d: (z, (y + d) % 4, c)) for b, d in zip(blocks, (1, 3, 2))
    ]


def swap(block):
    return over_seq(block, lambda z, y, c: (z, y, 1 - c))


def per_device(tokens, norm_gain, w_query, w_key, w_value, w_gate_out, gate_down, gate_up,
               gate_bias, head_gain, w_out, request_ids):
    rows = tokens.shape[0]
    t3 = over_tp(tokens, 2)
    t1 = over_tp(tokens, 1)
    t2 = over_tp(tokens, 3)
    idc, idr = request_ids.reshape(rows, 1), request_ids.reshape(1, rows)
    piece = (QUARTER + META, K)
    half = (HALF + META, K)
    normed, key, value, cum, mine, send = call(
        front_kernel,
        [((4, rows, F), BF), ((rows, K), BF), ((rows, V), BF), ((rows, K), F32), (half, BF), (half, BF)],
        (tokens, t1, t2, t3, norm_gain.reshape(4, 1, F), w_key, w_value, gate_down.T, gate_up,
         gate_bias.reshape(1, K), idc, request_ids),
        specs=[VM] * 11 + [SM], flops=2 * rows * 2048 * 784, name="front")
    other = swap(send)
    query, attn, gate = call(
        inner_kernel,
        [((rows, K), BF), ((rows, V), F32), ((rows, V), F32)],
        (normed, w_query, w_gate_out, key, value, cum, idc, idr, head_gain.reshape(1, V)),
        flops=2 * rows * 2048 * 1024, name="inner")
    own, s1, s2, s3 = call(pair_kernel, [(piece, BF)] * 4, (mine, other),
                           scratch=[pltpu.VMEM((HALF, K), BF)], name="pair")
    chips = [own] + over_y((s1, s2, s3))
    row, = call(row_kernel, [(piece, BF)], chips, scratch=[pltpu.VMEM((4,) + piece, BF)], name="row")
    one = over_seq(row, lambda z, y, c: (z + 1, y, c))
    far = over_seq(row, lambda z, y, c: (4 if z == 0 else 8, y, c))
    pair, = call(two_rows_kernel, [(piece, BF)], (row, one), name="two_rows")
    two = over_seq(pair, lambda z, y, c: (z + 2, y, c))
    own, s1, s2, s3 = call(spread_kernel, [(piece, BF)] * 4, (*chips, one, two, far),
                           scratch=[pltpu.VMEM((4,) + piece, BF)], name="spread")
    keep, send = call(unpair_kernel, [(half, BF)] * 2, (own, *over_y((s1, s2, s3)), mine, other),
                      scratch=[pltpu.VMEM((HALF, K), BF)], name="unpair")
    own, s1, s2, s3 = call(
        back_kernel, [((rows, F), F32)] + [((rows, F), BF)] * 3,
        (keep, swap(send), query, attn, gate, idc, w_out),
        scratch=[pltpu.VMEM((rows, V), F32)], flops=2 * rows * V * 2304, name="back")
    p3 = over_tp(s3, 2)
    p1 = over_tp(s1, 1)
    p2 = over_tp(s2, 3)
    return (own + p1.astype(F32) + p2.astype(F32) + p3.astype(F32)).astype(BF)


def solution(mesh):
    return jax.shard_map(
        per_device,
        mesh=mesh,
        in_specs=(
            P("seq", "tp"),
            P(),
            P(None, "tp"),
            P(None, "tp"),
            P(None, "tp"),
            P(None, "tp"),
            P(),
            P(None, "tp"),
            P("tp"),
            P("tp"),
            P("tp", None),
            P("seq"),
        ),
        out_specs=P("seq", "tp"),
        check_vma=False,
    )
```

time: 339 us -> 83 us (0.24)
  the two profiles are of different devices: /device:TPU:97 before, /device:TPU:1 now
where the time goes in v1:
time: 83 us; the launch traced here: 82.5 us
  starting transfers between devices  35.8 us (43%)
  waiting for transfers between devices  31.4 us (38%)
  local copies, waits for them, and re-layouts  8.17 us (10%)
  Pallas kernels  6.19 us (7%)
  other arithmetic  0.84 us (1%)
    ppermute x11, starting transfers between devices, over_seq(): return lax.ppermute(block, 'seq', seq_route(move))  28 us
    ppermute x6, waiting for transfers between devices, over_tp(): lax.ppermute(block, 'tp', [(i, (i + distance) % 4) for i in range(4)])  22.5 us
    ppermute x11, waiting for transfers between devices, over_seq(): return lax.ppermute(block, 'seq', seq_route(move))  8.89 us
    ppermute x6, starting transfers between devices, over_tp(): lax.ppermute(block, 'tp', [(i, (i + distance) % 4) for i in range(4)])  7.79 us
    unnamed x24, local copies, waits for them, and re-layouts  7.37 us
    pallas_call x8, Pallas kernels, call(): pl.pallas_call(kernel, out_shape=shapes, in_specs=specs or [VM] * len(arg...  6.19 us
  transfers between devices with their start and end apart: 17, of which 9 were waited for; matrix products, arithmetic and copies ran while one was open for 1% of the time, Pallas kernels for 2%

profile of v1, /device:TPU:1, one launch (start us, length us, event | category | flops | bytes accessed | tf_op | source)
XLA Modules:
  0.0 82.5 jit_solution(12807374977802510456)
XLA Ops:
  0.0 3.3 %collective-permute-start.1 = (bf16[256,512]{1,0:T(8,128)(2,1)}, bf16[256,512]{1,0:T(8,128)(2,1)S(1)}, u32[]{:S(2)}, u32[]{:S(2)}) collective-permute-start(bf16[256,512]{1,0:T(8,128)(2,1)} %t0.1), channel_id=1, source_target_pairs={{0,3},{1,0},{2,1},{3,2},{4,7},{5,4},{6,5},{7,6},{8,11},{9,8},{10,9... | collective-permute-start | bytes 786440 | tf_op jit(solution)/shard_map/ppermute | solution.py:236
  3.3 1.7 %collective-permute-start.2 = (bf16[256,512]{1,0:T(8,128)(2,1)}, bf16[256,512]{1,0:T(8,128)(2,1)S(1)}, u32[]{:S(2)}, u32[]{:S(2)}) collective-permute-start(bf16[256,512]{1,0:T(8,128)(2,1)} %t0.1), channel_id=1, source_target_pairs={{0,2},{1,3},{2,0},{3,1},{4,6},{5,7},{6,4},{7,5},{8,10},{9,11},{10,... | collective-permute-start | bytes 786440 | tf_op jit(solution)/shard_map/ppermute | solution.py:236
  5.9 3.7 %collective-permute-done.1.t2 = bf16[256,512]{1,0:T(8,128)(2,1)S(1)} collective-permute-done((bf16[256,512]{1,0:T(8,128)(2,1)}, bf16[256,512]{1,0:T(8,128)(2,1)S(1)}, u32[]{:S(2)}, u32[]{:S(2)}) %collective-permute-start.1) | collective-permute-done | bytes 262176 | tf_op jit(solution)/shard_map/ppermute | solution.py:236
  9.5 3.0 %collective-permute-done.t1 = bf16[256,512]{1,0:T(8,128)(2,1)S(1)} collective-permute-done((bf16[256,512]{1,0:T(8,128)(2,1)}, bf16[256,512]{1,0:T(8,128)(2,1)S(1)}, u32[]{:S(2)}, u32[]{:S(2)}) %collective-permute-start) | collective-permute-done | bytes 262176 | tf_op jit(solution)/shard_map/ppermute | solution.py:236
  12.5 3.8 %collective-permute-done.2.t3 = bf16[256,512]{1,0:T(8,128)(2,1)S(1)} collective-permute-done((bf16[256,512]{1,0:T(8,128)(2,1)}, bf16[256,512]{1,0:T(8,128)(2,1)S(1)}, u32[]{:S(2)}, u32[]{:S(2)}) %collective-permute-start.2) | collective-permute-done | bytes 262176 | tf_op jit(solution)/shard_map/ppermute | solution.py:236
  16.3 1.6 %copy-done.2 = bf16[2048,512]{1,0:T(8,128)(2,1)S(1)} copy-done((bf16[2048,512]{1,0:T(8,128)(2,1)S(1)}, bf16[2048,512]{1,0:T(8,128)(2,1)}, u32[]{:S(2)}) %copy-start.2) | copy-done | bytes 2097176
  17.9 1.2 %copy-done.4 = bf16[2048,256]{1,0:T(8,128)(2,1)S(1)} copy-done((bf16[2048,256]{1,0:T(8,128)(2,1)S(1)}, bf16[2048,256]{1,0:T(8,128)(2,1)}, u32[]{:S(2)}) %copy-start.4) | copy-done | bytes 1048600
  23.7 3.0 %front.1 = (bf16[4,256,512]{2,1,0:T(8,128)(2,1)S(1)}, bf16[256,256]{1,0:T(8,128)(2,1)S(1)}, bf16[256,512]{1,0:T(8,128)(2,1)S(1)}, f32[256,256]{1,0:T(8,128)S(1)}...) custom-call(bf16[256,512]{1,0:T(8,128)(2,1)S(1)} %copy-done.5, ...), custom_call_target="tpu_custom_call" | custom-call | flops 822083584 | bytes 6261760 | tf_op jit(solution)/shard_map/front/pallas_call | solution.py:223
  26.7 2.8 %collective-permute-start.3 = (bf16[272,256]{1,0:T(8,128)(2,1)S(1)}, bf16[272,256]{1,0:T(8,128)(2,1)S(1)}, u32[]{:S(2)}, u32[]{:S(2)}) collective-permute-start(bf16[272,256]{1,0:T(8,128)(2,1)S(1)} %get-tuple-element.29), channel_id=1, source_target_pairs={{0,4},{4,0},{8,12},{12,8},{16,20},{20,16},{24,28},{28,24},{32,36},... | collective-permute-start | bytes 417800 | tf_op jit(solution)/shard_map/ppermute | solution.py:249
  30.6 1.4 %collective-permute-start.4 = (bf16[80,256]{1,0:T(8,128)(2,1)S(1)}, bf16[80,256]{1,0:T(8,128)(2,1)S(1)}, u32[]{:S(2)}, u32[]{:S(2)}) collective-permute-start(bf16[80,256]{1,0:T(8,128)(2,1)S(1)} %get-tuple-element.31), channel_id=1, source_target_pairs={{0,8},{4,12},{8,16},{12,20},{16,24},{20,28},{24,0},{28,4},{32,40},... | collective-permute-start | bytes 122888 | tf_op jit(solution)/shard_map/ppermute | solution.py:249
  32.0 1.5 %collective-permute-start.5 = (bf16[80,256]{1,0:T(8,128)(2,1)S(1)}, bf16[80,256]{1,0:T(8,128)(2,1)S(1)}, u32[]{:S(2)}, u32[]{:S(2)}) collective-permute-start(bf16[80,256]{1,0:T(8,128)(2,1)S(1)} %get-tuple-element.32), channel_id=1, source_target_pairs={{0,24},{4,28},{8,0},{12,4},{16,8},{20,12},{24,16},{28,20},{32,56},... | collective-permute-start | bytes 122888 | tf_op jit(solution)/shard_map/ppermute | solution.py:249
  33.5 1.6 %collective-permute-start.6 = (bf16[80,256]{1,0:T(8,128)(2,1)S(1)}, bf16[80,256]{1,0:T(8,128)(2,1)S(1)}, u32[]{:S(2)}, u32[]{:S(2)}) collective-permute-start(bf16[80,256]{1,0:T(8,128)(2,1)S(1)} %get-tuple-element.33), channel_id=1, source_target_pairs={{0,16},{4,20},{8,24},{12,28},{16,0},{20,4},{24,8},{28,12},{32,48},... | collective-permute-start | bytes 122888 | tf_op jit(solution)/shard_map/ppermute | solution.py:249
  35.1 2.8 %collective-permute-done.6.r3 = bf16[80,256]{1,0:T(8,128)(2,1)S(1)} collective-permute-done((bf16[80,256]{1,0:T(8,128)(2,1)S(1)}, bf16[80,256]{1,0:T(8,128)(2,1)S(1)}, u32[]{:S(2)}, u32[]{:S(2)}) %collective-permute-start.6) | collective-permute-done | bytes 40992 | tf_op jit(solution)/shard_map/ppermute | solution.py:249
  38.0 3.5 %collective-permute-start.7 = (bf16[80,256]{1,0:T(8,128)(2,1)S(1)}, bf16[80,256]{1,0:T(8,128)(2,1)S(1)}, u32[]{:S(2)}, u32[]{:S(2)}) collective-permute-start(bf16[80,256]{1,0:T(8,128)(2,1)S(1)} %row.1), channel_id=1, source_target_pairs={{0,32},{4,36},{8,40},{12,44},{16,48},{20,52},{24,56},{28,60},{32,6... | collective-permute-start | bytes 122888 | tf_op jit(solution)/shard_map/ppermute | solution.py:249
  41.5 7.9 %collective-permute-start.9 = (bf16[80,256]{1,0:T(8,128)(2,1)S(1)}, bf16[80,256]{1,0:T(8,128)(2,1)S(1)}, u32[]{:S(2)}, u32[]{:S(2)}) collective-permute-start(bf16[80,256]{1,0:T(8,128)(2,1)S(1)} %row.1), channel_id=1, source_target_pairs={{0,128},{4,132},{8,136},{12,140},{16,144},{20,148},{24,152},{28,15... | collective-permute-start | bytes 122888 | tf_op jit(solution)/shard_map/ppermute | solution.py:249
  49.5 1.3 %collective-permute-start.8 = (bf16[80,256]{1,0:T(8,128)(2,1)S(1)}, bf16[80,256]{1,0:T(8,128)(2,1)S(1)}, u32[]{:S(2)}, u32[]{:S(2)}) collective-permute-start(bf16[80,256]{1,0:T(8,128)(2,1)S(1)} %two_rows.1), channel_id=1, source_target_pairs={{0,64},{4,68},{8,72},{12,76},{16,80},{20,84},{24,88},{28,92},{32,9... | collective-permute-start | bytes 122888 | tf_op jit(solution)/shard_map/ppermute | solution.py:249
  50.8 1.1 %collective-permute-done.8.two = bf16[80,256]{1,0:T(8,128)(2,1)S(1)} collective-permute-done((bf16[80,256]{1,0:T(8,128)(2,1)S(1)}, bf16[80,256]{1,0:T(8,128)(2,1)S(1)}, u32[]{:S(2)}, u32[]{:S(2)}) %collective-permute-start.8) | collective-permute-done | bytes 40992 | tf_op jit(solution)/shard_map/ppermute | solution.py:249
  52.2 2.5 %collective-permute-start.11 = (bf16[80,256]{1,0:T(8,128)(2,1)S(1)}, bf16[80,256]{1,0:T(8,128)(2,1)S(1)}, u32[]{:S(2)}, u32[]{:S(2)}) collective-permute-start(bf16[80,256]{1,0:T(8,128)(2,1)S(1)} %get-tuple-element.36), channel_id=1, source_target_pairs={{0,24},{4,28},{8,0},{12,4},{16,8},{20,12},{24,16},{28,20},{32,56},... | collective-permute-start | bytes 122888 | tf_op jit(solution)/shard_map/ppermute | solution.py:249
  56.1 3.0 %collective-permute-done.12.r3 = bf16[80,256]{1,0:T(8,128)(2,1)S(1)} collective-permute-done((bf16[80,256]{1,0:T(8,128)(2,1)S(1)}, bf16[80,256]{1,0:T(8,128)(2,1)S(1)}, u32[]{:S(2)}, u32[]{:S(2)}) %collective-permute-start.12) | collective-permute-done | bytes 40992 | tf_op jit(solution)/shard_map/ppermute | solution.py:249
  59.2 4.9 %collective-permute-start.13 = (bf16[272,256]{1,0:T(8,128)(2,1)S(1)}, bf16[272,256]{1,0:T(8,128)(2,1)S(1)}, u32[]{:S(2)}, u32[]{:S(2)}) collective-permute-start(bf16[272,256]{1,0:T(8,128)(2,1)S(1)} %get-tuple-element.39), channel_id=1, source_target_pairs={{0,4},{4,0},{8,12},{12,8},{16,20},{20,16},{24,28},{28,24},{32,36},... | collective-permute-start | bytes 417800 | tf_op jit(solution)/shard_map/ppermute | solution.py:249
  64.1 1.6 %inner.1 = (bf16[256,256]{1,0:T(8,128)(2,1)S(1)}, f32[256,512]{1,0:T(8,128)S(1)}, f32[256,512]{1,0:T(8,128)S(1)}) custom-call(bf16[4,256,512]{2,1,0:T(8,128)(2,1)S(1)} %get-tuple-element.40.normed, bf16[2048,256]{1,0:T(8,128)(2,1)S(1)} %copy-done.3, bf16[2048,512]{1,0:T(8,128)(2,1)S(1)} %copy-done, bf16[256,256]{1,0:T(8,128)(2,1)S(1)} %get-tuple-element.41.key_r, ...), custom_call_target="tpu_custom_call" | custom-call | flops 1073741824 | bytes 6033408 | tf_op jit(solution)/shard_map/inner/pallas_call | solution.py:223
  65.7 1.2 %back.1 = (f32[256,512]{1,0:T(8,128)S(1)}, bf16[256,512]{1,0:T(8,128)(2,1)S(1)}, bf16[256,512]{1,0:T(8,128)(2,1)S(1)}, bf16[256,512]{1,0:T(8,128)(2,1)S(1)}) custom-call(bf16[272,256]{1,0:T(8,128)(2,1)S(1)} %get-tuple-element.38.mine, bf16[272,256]{1,0:T(8,128)(2,1)S(1)} %collective-permute-done.13.other, bf16[256,256]{1,0:T(8,128)(2,1)S(1)} %get-tuple-element.44.query, ...), custom_call_target="tpu_custom_call" | custom-call | flops 603979776 | bytes 4867072 | tf_op jit(solution)/shard_map/back/pallas_call | solution.py:223
  67.0 2.7 %collective-permute-start.15 = (bf16[256,512]{1,0:T(8,128)(2,1)S(1)}, bf16[256,512]{1,0:T(8,128)(2,1)S(1)}, u32[]{:S(2)}, u32[]{:S(2)}) collective-permute-start(bf16[256,512]{1,0:T(8,128)(2,1)S(1)} %get-tuple-element.49), channel_id=1, source_target_pairs={{0,3},{1,0},{2,1},{3,2},{4,7},{5,4},{6,5},{7,6},{8,11},{9,8},{10,9... | collective-permute-start | bytes 786440 | tf_op jit(solution)/shard_map/ppermute | solution.py:236
  69.6 12.0 %collective-permute-done.14 = bf16[256,512]{1,0:T(8,128)(2,1)S(1)} collective-permute-done((bf16[256,512]{1,0:T(8,128)(2,1)S(1)}, bf16[256,512]{1,0:T(8,128)(2,1)S(1)}, u32[]{:S(2)}, u32[]{:S(2)}) %collective-permute-start.14) | collective-permute-done | bytes 262176 | tf_op jit(solution)/shard_map/ppermute | solution.py:236
  (44 shorter events, 9.5 us)
Async XLA Ops:
  0.0 9.5 %collective-permute-start.1 = (bf16[256,512]{1,0:T(8,128)(2,1)}, bf16[256,512]{1,0:T(8,128)(2,1)S(1)}, u32[]{:S(2)}, u32[]{:S(2)}) collective-permute-start(bf16[256,512]{1,0:T(8,128)(2,1)} %t0.1), channel_id=1, source_target_pairs={{0,3},{1,0},{2,1},{3,2},{4,7},{5,4},{6,5},{7,6},{8,11},{9,8},{10,9... | collective-permute-start | bytes 786440 | tf_op jit(solution)/shard_map/ppermute | solution.py:236
  3.3 9.2 %collective-permute-start = (bf16[256,512]{1,0:T(8,128)(2,1)}, bf16[256,512]{1,0:T(8,128)(2,1)S(1)}, u32[]{:S(2)}, u32[]{:S(2)}) collective-permute-start(bf16[256,512]{1,0:T(8,128)(2,1)} %t0.1), channel_id=1, source_target_pairs={{0,1},{1,2},{2,3},{3,0},{4,5},{5,6},{6,7},{7,4},{8,9},{9,10},{10,1... | collective-permute-start | bytes 786440 | tf_op jit(solution)/shard_map/ppermute | solution.py:236
  3.3 13.0 %collective-permute-start.2 = (bf16[256,512]{1,0:T(8,128)(2,1)}, bf16[256,512]{1,0:T(8,128)(2,1)S(1)}, u32[]{:S(2)}, u32[]{:S(2)}) collective-permute-start(bf16[256,512]{1,0:T(8,128)(2,1)} %t0.1), channel_id=1, source_target_pairs={{0,2},{1,3},{2,0},{3,1},{4,6},{5,7},{6,4},{7,5},{8,10},{9,11},{10,... | collective-permute-start | bytes 786440 | tf_op jit(solution)/shard_map/ppermute | solution.py:236
  16.3 1.6 %copy-start.2 = (bf16[2048,512]{1,0:T(8,128)(2,1)S(1)}, bf16[2048,512]{1,0:T(8,128)(2,1)}, u32[]{:S(2)}) copy-start(bf16[2048,512]{1,0:T(8,128)(2,1)} %wv.1) | copy-start | bytes 6291460
  17.9 1.2 %copy-start.4 = (bf16[2048,256]{1,0:T(8,128)(2,1)S(1)}, bf16[2048,256]{1,0:T(8,128)(2,1)}, u32[]{:S(2)}) copy-start(bf16[2048,256]{1,0:T(8,128)(2,1)} %wk.1) | copy-start | bytes 3145732
  19.1 0.9 %copy-start.5 = (bf16[256,512]{1,0:T(8,128)(2,1)S(1)}, bf16[256,512]{1,0:T(8,128)(2,1)}, u32[]{:S(2)}) copy-start(bf16[256,512]{1,0:T(8,128)(2,1)} %t0.1) | copy-start | bytes 786436
  23.7 40.4 %copy-start = (bf16[2048,512]{1,0:T(8,128)(2,1)S(1)}, bf16[2048,512]{1,0:T(8,128)(2,1)}, u32[]{:S(2)}) copy-start(bf16[2048,512]{1,0:T(8,128)(2,1)} %wg.1) | copy-start | bytes 6291460
  23.7 40.4 %copy-start.3 = (bf16[2048,256]{1,0:T(8,128)(2,1)S(1)}, bf16[2048,256]{1,0:T(8,128)(2,1)}, u32[]{:S(2)}) copy-start(bf16[2048,256]{1,0:T(8,128)(2,1)} %wq.1) | copy-start | bytes 3145732
  23.7 40.4 %copy-start.10 = (f32[512]{0:T(512)S(1)}, f32[512]{0:T(512)}, u32[]{:S(2)}) copy-start(f32[512]{0:T(512)} %param.21) | copy-start | bytes 6148
  26.7 3.8 %collective-permute-start.3 = (bf16[272,256]{1,0:T(8,128)(2,1)S(1)}, bf16[272,256]{1,0:T(8,128)(2,1)S(1)}, u32[]{:S(2)}, u32[]{:S(2)}) collective-permute-start(bf16[272,256]{1,0:T(8,128)(2,1)S(1)} %get-tuple-element.29), channel_id=1, source_target_pairs={{0,4},{4,0},{8,12},{12,8},{16,20},{20,16},{24,28},{28,24},{32,36},... | collective-permute-start | bytes 417800 | tf_op jit(solution)/shard_map/ppermute | solution.py:249
  30.6 4.5 %collective-permute-start.4 = (bf16[80,256]{1,0:T(8,128)(2,1)S(1)}, bf16[80,256]{1,0:T(8,128)(2,1)S(1)}, u32[]{:S(2)}, u32[]{:S(2)}) collective-permute-start(bf16[80,256]{1,0:T(8,128)(2,1)S(1)} %get-tuple-element.31), channel_id=1, source_target_pairs={{0,8},{4,12},{8,16},{12,20},{16,24},{20,28},{24,0},{28,4},{32,40},... | collective-permute-start | bytes 122888 | tf_op jit(solution)/shard_map/ppermute | solution.py:249
  32.0 3.1 %collective-permute-start.5 = (bf16[80,256]{1,0:T(8,128)(2,1)S(1)}, bf16[80,256]{1,0:T(8,128)(2,1)S(1)}, u32[]{:S(2)}, u32[]{:S(2)}) collective-permute-start(bf16[80,256]{1,0:T(8,128)(2,1)S(1)} %get-tuple-element.32), channel_id=1, source_target_pairs={{0,24},{4,28},{8,0},{12,4},{16,8},{20,12},{24,16},{28,20},{32,56},... | collective-permute-start | bytes 122888 | tf_op jit(solution)/shard_map/ppermute | solution.py:249
  33.5 4.4 %collective-permute-start.6 = (bf16[80,256]{1,0:T(8,128)(2,1)S(1)}, bf16[80,256]{1,0:T(8,128)(2,1)S(1)}, u32[]{:S(2)}, u32[]{:S(2)}) collective-permute-start(bf16[80,256]{1,0:T(8,128)(2,1)S(1)} %get-tuple-element.33), channel_id=1, source_target_pairs={{0,16},{4,20},{8,24},{12,28},{16,0},{20,4},{24,8},{28,12},{32,48},... | collective-permute-start | bytes 122888 | tf_op jit(solution)/shard_map/ppermute | solution.py:249
  38.0 11.5 %collective-permute-start.7 = (bf16[80,256]{1,0:T(8,128)(2,1)S(1)}, bf16[80,256]{1,0:T(8,128)(2,1)S(1)}, u32[]{:S(2)}, u32[]{:S(2)}) collective-permute-start(bf16[80,256]{1,0:T(8,128)(2,1)S(1)} %row.1), channel_id=1, source_target_pairs={{0,32},{4,36},{8,40},{12,44},{16,48},{20,52},{24,56},{28,60},{32,6... | collective-permute-start | bytes 122888 | tf_op jit(solution)/shard_map/ppermute | solution.py:249
  41.5 9.3 %collective-permute-start.9 = (bf16[80,256]{1,0:T(8,128)(2,1)S(1)}, bf16[80,256]{1,0:T(8,128)(2,1)S(1)}, u32[]{:S(2)}, u32[]{:S(2)}) collective-permute-start(bf16[80,256]{1,0:T(8,128)(2,1)S(1)} %row.1), channel_id=1, source_target_pairs={{0,128},{4,132},{8,136},{12,140},{16,144},{20,148},{24,152},{28,15... | collective-permute-start | bytes 122888 | tf_op jit(solution)/shard_map/ppermute | solution.py:249
  49.5 2.4 %collective-permute-start.8 = (bf16[80,256]{1,0:T(8,128)(2,1)S(1)}, bf16[80,256]{1,0:T(8,128)(2,1)S(1)}, u32[]{:S(2)}, u32[]{:S(2)}) collective-permute-start(bf16[80,256]{1,0:T(8,128)(2,1)S(1)} %two_rows.1), channel_id=1, source_target_pairs={{0,64},{4,68},{8,72},{12,76},{16,80},{20,84},{24,88},{28,92},{32,9... | collective-permute-start | bytes 122888 | tf_op jit(solution)/shard_map/ppermute | solution.py:249
  51.9 4.1 %collective-permute-start.10 = (bf16[80,256]{1,0:T(8,128)(2,1)S(1)}, bf16[80,256]{1,0:T(8,128)(2,1)S(1)}, u32[]{:S(2)}, u32[]{:S(2)}) collective-permute-start(bf16[80,256]{1,0:T(8,128)(2,1)S(1)} %get-tuple-element.35), channel_id=1, source_target_pairs={{0,8},{4,12},{8,16},{12,20},{16,24},{20,28},{24,0},{28,4},{32,40},... | collective-permute-start | bytes 122888 | tf_op jit(solution)/shard_map/ppermute | solution.py:249
  52.2 3.8 %collective-permute-start.11 = (bf16[80,256]{1,0:T(8,128)(2,1)S(1)}, bf16[80,256]{1,0:T(8,128)(2,1)S(1)}, u32[]{:S(2)}, u32[]{:S(2)}) collective-permute-start(bf16[80,256]{1,0:T(8,128)(2,1)S(1)} %get-tuple-element.36), channel_id=1, source_target_pairs={{0,24},{4,28},{8,0},{12,4},{16,8},{20,12},{24,16},{28,20},{32,56},... | collective-permute-start | bytes 122888 | tf_op jit(solution)/shard_map/ppermute | solution.py:249
  54.7 4.4 %collective-permute-start.12 = (bf16[80,256]{1,0:T(8,128)(2,1)S(1)}, bf16[80,256]{1,0:T(8,128)(2,1)S(1)}, u32[]{:S(2)}, u32[]{:S(2)}) collective-permute-start(bf16[80,256]{1,0:T(8,128)(2,1)S(1)} %get-tuple-element.37), channel_id=1, source_target_pairs={{0,16},{4,20},{8,24},{12,28},{16,0},{20,4},{24,8},{28,12},{32,48},... | collective-permute-start | bytes 122888 | tf_op jit(solution)/shard_map/ppermute | solution.py:249
  59.2 6.5 %collective-permute-start.13 = (bf16[272,256]{1,0:T(8,128)(2,1)S(1)}, bf16[272,256]{1,0:T(8,128)(2,1)S(1)}, u32[]{:S(2)}, u32[]{:S(2)}) collective-permute-start(bf16[272,256]{1,0:T(8,128)(2,1)S(1)} %get-tuple-element.39), channel_id=1, source_target_pairs={{0,4},{4,0},{8,12},{12,8},{16,20},{20,16},{24,28},{28,24},{32,36},... | collective-permute-start | bytes 417800 | tf_op jit(solution)/shard_map/ppermute | solution.py:249
  64.1 1.6 %copy-start.1 = (bf16[512,2048]{1,0:T(8,128)(2,1)S(1)}, bf16[512,2048]{1,0:T(8,128)(2,1)}, u32[]{:S(2)}) copy-start(bf16[512,2048]{1,0:T(8,128)(2,1)} %w_out.1) | copy-start | bytes 6291460
  66.9 14.8 %collective-permute-start.14 = (bf16[256,512]{1,0:T(8,128)(2,1)S(1)}, bf16[256,512]{1,0:T(8,128)(2,1)S(1)}, u32[]{:S(2)}, u32[]{:S(2)}) collective-permute-start(bf16[256,512]{1,0:T(8,128)(2,1)S(1)} %get-tuple-element.48), channel_id=1, source_target_pairs={{0,1},{1,2},{2,3},{3,0},{4,5},{5,6},{6,7},{7,4},{8,9},{9,10},{10,1... | collective-permute-start | bytes 786440 | tf_op jit(solution)/shard_map/ppermute | solution.py:236
  67.0 14.7 %collective-permute-start.15 = (bf16[256,512]{1,0:T(8,128)(2,1)S(1)}, bf16[256,512]{1,0:T(8,128)(2,1)S(1)}, u32[]{:S(2)}, u32[]{:S(2)}) collective-permute-start(bf16[256,512]{1,0:T(8,128)(2,1)S(1)} %get-tuple-element.49), channel_id=1, source_target_pairs={{0,3},{1,0},{2,1},{3,2},{4,7},{5,4},{6,5},{7,6},{8,11},{9,8},{10,9... | collective-permute-start | bytes 786440 | tf_op jit(solution)/shard_map/ppermute | solution.py:236
  69.6 12.1 %collective-permute-start.16 = (bf16[256,512]{1,0:T(8,128)(2,1)S(1)}, bf16[256,512]{1,0:T(8,128)(2,1)S(1)}, u32[]{:S(2)}, u32[]{:S(2)}) collective-permute-start(bf16[256,512]{1,0:T(8,128)(2,1)S(1)} %get-tuple-element.50), channel_id=1, source_target_pairs={{0,2},{1,3},{2,0},{3,1},{4,6},{5,7},{6,4},{7,5},{8,10},{9,11},{10,... | collective-permute-start | bytes 786440 | tf_op jit(solution)/shard_map/ppermute | solution.py:236
  (5 other events, 3.6 us)

commit v2 on v1

--- a/solution.py
+++ b/solution.py
@@ -15,7 +15,7 @@
 F32 = jnp.float32
 BF = jnp.bfloat16
 VM = pl.BlockSpec(memory_space=pltpu.VMEM)
-SM = pl.BlockSpec(memory_space=pltpu.SMEM)
+HBM = pl.BlockSpec(memory_space=pltpu.HBM)
 
 
 def dot(a, b, dims=((1,), (0,))):
@@ -31,8 +31,11 @@
     return pl.ds(pl.multiple_of(index * size, size), size)
 
 
-def turn(index, distance):
-    return lax.rem(index + distance, 4)
+FLIPS = (0, 2, 1, 3)
+
+
+def flip(index, bits):
+    return lax.bitwise_xor(index, bits)
 
 
 def load(ref):
@@ -77,11 +80,21 @@
     return dot(mask, three) + dot(mask, two) + dot(mask, one)
 
 
-def front_kernel(t0, t1, t2, t3, gain, wk, wv, gd, gu, bias, idc, ids,
+def stage_kernel(*refs):
+    count = len(refs) // 2
+    done = refs[-1]
+    copies = [pltpu.make_async_copy(refs[i], refs[count + i], done.at[i]) for i in range(count)]
+    for copy in copies:
+        copy.start()
+    for copy in copies:
+        copy.wait()
+
+
+def front_kernel(t0, t1, t2, t3, gain, wk, wv, gd, gu, bias, idc,
                  normed, key_o, value_o, cum_o, keep_o, send_o):
     x = lax.axis_index("tp")
     _, _, c = place()
-    parts = [(t0, x), (t1, turn(x, 3)), (t2, turn(x, 1)), (t3, turn(x, 2))]
+    parts = [(ref, flip(x, d)) for d, ref in zip(FLIPS, (t0, t1, t2, t3))]
     squares = 0.0
     for ref, _ in parts:
         wide = ref[...].astype(F32)
@@ -103,8 +116,9 @@
     cum_o[...] = cum
     ends = [cum[C * b + C - 1:C * b + C] for b in range(4)]
     after = [ends[1] + ends[2] + ends[3], ends[2] + ends[3], ends[3], jnp.zeros_like(ends[3])]
-    first, last = ids[0], ids[4 * C - 1]
-    keep = (idc[...] == last).astype(F32)
+    ids = idc[...].astype(F32)
+    first, last = ids[0:1], ids[4 * C - 1:]
+    keep = (ids == last).astype(F32)
     ending = []
     for b in range(4):
         rows = slice(C * b, C * b + C)
@@ -113,7 +127,7 @@
     ending = jnp.concatenate(ending, axis=0)
     decay = jnp.exp(ends[0] + after[0])
     decay = jnp.where(first == last, decay, 0.0)
-    meta = meta_of(decay, first.astype(F32), last.astype(F32))
+    meta = meta_of(decay, first, last)
     for ref, side in ((keep_o, c), (send_o, 1 - c)):
         ref[0:HALF] = dot(value_o[:, at(side, HALF)], ending, ((0,), (0,))).astype(BF)
         ref[HALF:] = meta
@@ -156,15 +170,15 @@
     total = joined(pick(c == 0, a, b), pick(c == 0, b, a))
     scratch[...] = total[0].astype(BF)
     meta = meta_of(*total[1:])
-    for ref, d in ((own, 0), (s1, 1), (s2, 3), (s3, 2)):
-        ref[0:QUARTER] = scratch[at(turn(y, d), QUARTER), :]
+    for d, ref in zip(FLIPS, (own, s1, s2, s3)):
+        ref[0:QUARTER] = scratch[at(flip(y, d), QUARTER), :]
         ref[QUARTER:] = meta
 
 
 def stack_rows(parts, stack):
     _, y, _ = place()
-    for ref, d in zip(parts, (0, 3, 1, 2)):
-        stack[turn(y, d)] = ref[...]
+    for d, ref in zip(FLIPS, parts):
+        stack[flip(y, d)] = ref[...]
     return [load(stack.at[i]) for i in range(4)]
 
 
@@ -176,25 +190,34 @@
     save(total, run)
 
 
-def two_rows_kernel(row, before, total):
-    save(total, joined(load(before), load(row)))
-
-
-def spread_kernel(own, r1, r2, r3, one, two, far, own_o, s1, s2, s3, stack):
-    _, y, _ = place()
+def two_rows_kernel(row, beside, total):
+    z, _, _ = place()
+    a, b = load(row), load(beside)
+    odd = lax.rem(z, 2) == 1
+    save(total, joined(pick(odd, b, a), pick(odd, a, b)))
+
+
+def four_rows_kernel(pair, beside, total):
+    save(total, joined(load(beside), load(pair)))
+
+
+def spread_kernel(own, r1, r2, r3, z1, z2, z3, own_o, s1, s2, s3, stack):
+    z, y, _ = place()
     chips = stack_rows((own, r1, r2, r3), stack)
-    run = joined(joined(load(far), load(two)), load(one))
+    state, *rest = pick(z == 4, load(z3), load(z2))
+    before = (jnp.where((lax.rem(z, 4) >= 2) | (z == 4), state, 0.0), *rest)
+    run = pick(lax.rem(z, 2) == 1, joined(before, load(z1)), before)
     for i in range(4):
         save(stack.at[i], run)
         run = joined(run, chips[i])
-    for ref, d in ((own_o, 0), (s1, 1), (s2, 3), (s3, 2)):
-        ref[...] = stack[turn(y, d)]
+    for d, ref in zip(FLIPS, (own_o, s1, s2, s3)):
+        ref[...] = stack[flip(y, d)]
 
 
 def unpair_kernel(own, r1, r2, r3, mine, other, keep, send, scratch):
     _, y, c = place()
-    for ref, d in zip((own, r1, r2, r3), (0, 3, 1, 2)):
-        scratch[at(turn(y, d), QUARTER), :] = ref[0:QUARTER]
+    for d, ref in zip(FLIPS, (own, r1, r2, r3)):
+        scratch[at(flip(y, d), QUARTER), :] = ref[0:QUARTER]
     meta = own[QUARTER:].astype(F32)
     into = (scratch[...].astype(F32), meta[0:1] + meta[1:2], meta[2:3], meta[3:4])
     after = joined(into, pick(c == 0, load(mine), load(other)))
@@ -202,7 +225,7 @@
     save(send, pick(c == 0, after, into))
 
 
-def back_kernel(mine, other, query, attn_r, gate, idc, w_out, own, s1, s2, s3, attn):
+def back_kernel(mine, other, query, attn_r, gate, idc, w_out, gated_o, s2, attn):
     x = lax.axis_index("tp")
     _, _, c = place()
     prev = mine[HALF:].astype(F32)[3:4, 0:1]
@@ -212,12 +235,22 @@
         attn[:, at(side, HALF)] = attn_r[:, at(side, HALF)] + jnp.where(seen, inter, 0.0)
     full = attn[...]
     scale = lax.rsqrt(jnp.mean(full * full, axis=1, keepdims=True) + 1e-05)
-    gated = (full * scale * gate[...]).astype(BF)
-    for ref, d in ((s3, 2), (s1, 1), (s2, 3), (own, 0)):
-        ref[...] = dot(gated, w_out[:, at(turn(x, d), F)]).astype(ref.dtype)
-
-
-def call(kernel, outs, args, specs=None, scratch=(), flops=0, name=None):
+    gated_o[...] = (full * scale * gate[...]).astype(BF)
+    s2[...] = dot(gated_o[...], w_out[:, at(flip(x, 2), F)]).astype(BF)
+
+
+def beside_kernel(gated, w_out, s1, s3):
+    x = lax.axis_index("tp")
+    for d, ref in ((3, s3), (1, s1)):
+        ref[...] = dot(gated[...], w_out[:, at(flip(x, d), F)]).astype(BF)
+
+
+def here_kernel(gated, w_out, own):
+    x = lax.axis_index("tp")
+    own[...] = dot(gated[...], w_out[:, at(x, F)])
+
+
+def call(kernel, outs, args, specs=None, scratch=(), flops=0, name=None, vmem=24):
     shapes = [jax.ShapeDtypeStruct(s, d) for s, d in outs]
     bytes_accessed = sum(a.size * a.dtype.itemsize for a in list(args) + shapes)
     return pl.pallas_call(
@@ -226,23 +259,22 @@
         in_specs=specs or [VM] * len(args),
         out_specs=[VM] * len(outs),
         scratch_shapes=list(scratch),
-        compiler_params=pltpu.CompilerParams(vmem_limit_bytes=24 << 20),
+        compiler_params=pltpu.CompilerParams(vmem_limit_bytes=vmem << 20),
         cost_estimate=pl.CostEstimate(flops=flops, bytes_accessed=bytes_accessed, transcendentals=0),
         name=name,
     )(*args)
 
 
-def over_tp(block, distance):
-    return lax.ppermute(block, "tp", [(i, (i + distance) % 4) for i in range(4)])
+def over_tp(block, bits):
+    return lax.ppermute(block, "tp", [(i, i ^ bits) for i in range(4)])
 
 
 def seq_route(move):
-    pairs = []
+    route = []
     for i in range(64):
         z, y, c = move(i // 8, i // 2 % 4, i % 2)
-        if z < 8:
-            pairs.append((i, z * 8 + y * 2 + c))
-    return pairs
+        route.append((i, z * 8 + y * 2 + c))
+    return route
 
 
 def over_seq(block, move):
@@ -251,7 +283,7 @@
 
 def over_y(blocks):
     return [
-        over_seq(b, lambda z, y, c, d=d: (z, (y + d) % 4, c)) for b, d in zip(blocks, (1, 3, 2))
+        over_seq(b, lambda z, y, c, d=d: (z, y ^ d, c)) for d, b in zip(FLIPS[1:], blocks)
     ]
 
 
@@ -262,18 +294,20 @@
 def per_device(tokens, norm_gain, w_query, w_key, w_value, w_gate_out, gate_down, gate_up,
                gate_bias, head_gain, w_out, request_ids):
     rows = tokens.shape[0]
-    t3 = over_tp(tokens, 2)
-    t1 = over_tp(tokens, 1)
-    t2 = over_tp(tokens, 3)
+    t1, t2, t3 = (over_tp(tokens, d) for d in FLIPS[1:])
     idc, idr = request_ids.reshape(rows, 1), request_ids.reshape(1, rows)
     piece = (QUARTER + META, K)
     half = (HALF + META, K)
+    held = (tokens, norm_gain.reshape(4, 1, F), w_key, w_value, gate_down.T, gate_up,
+            gate_bias.reshape(1, K))
+    tokens, gain, w_key, w_value, down, up, bias = call(
+        stage_kernel, [(a.shape, a.dtype) for a in held], held, specs=[HBM] * len(held),
+        scratch=[pltpu.SemaphoreType.DMA((len(held),))], name="stage")
     normed, key, value, cum, mine, send = call(
         front_kernel,
         [((4, rows, F), BF), ((rows, K), BF), ((rows, V), BF), ((rows, K), F32), (half, BF), (half, BF)],
-        (tokens, t1, t2, t3, norm_gain.reshape(4, 1, F), w_key, w_value, gate_down.T, gate_up,
-         gate_bias.reshape(1, K), idc, request_ids),
-        specs=[VM] * 11 + [SM], flops=2 * rows * 2048 * 784, name="front")
+        (tokens, t1, t2, t3, gain, w_key, w_value, down, up, bias, idc),
+        flops=2 * rows * 2048 * 784, name="front")
     other = swap(send)
     query, attn, gate = call(
         inner_kernel,
@@ -282,23 +316,28 @@
         flops=2 * rows * 2048 * 1024, name="inner")
     own, s1, s2, s3 = call(pair_kernel, [(piece, BF)] * 4, (mine, other),
                            scratch=[pltpu.VMEM((HALF, K), BF)], name="pair")
-    chips = [own] + over_y((s1, s2, s3))
+    r1, r2, r3 = over_y((s1, s2, s3))
+    r1, query = lax.optimization_barrier((r1, query))
+    chips = [own, r1, r2, r3]
     row, = call(row_kernel, [(piece, BF)], chips, scratch=[pltpu.VMEM((4,) + piece, BF)], name="row")
-    one = over_seq(row, lambda z, y, c: (z + 1, y, c))
-    far = over_seq(row, lambda z, y, c: (4 if z == 0 else 8, y, c))
-    pair, = call(two_rows_kernel, [(piece, BF)], (row, one), name="two_rows")
-    two = over_seq(pair, lambda z, y, c: (z + 2, y, c))
-    own, s1, s2, s3 = call(spread_kernel, [(piece, BF)] * 4, (*chips, one, two, far),
+    z1 = over_seq(row, lambda z, y, c: (z ^ 1, y, c))
+    pair, = call(two_rows_kernel, [(piece, BF)], (row, z1), name="two_rows")
+    z2 = over_seq(pair, lambda z, y, c: (z ^ 2, y, c))
+    four, = call(four_rows_kernel, [(piece, BF)], (pair, z2), name="four_rows")
+    z3 = over_seq(four, lambda z, y, c: ({3: 4, 4: 3}.get(z, z), y, c))
+    own, s1, s2, s3 = call(spread_kernel, [(piece, BF)] * 4, (*chips, z1, z2, z3),
                            scratch=[pltpu.VMEM((4,) + piece, BF)], name="spread")
     keep, send = call(unpair_kernel, [(half, BF)] * 2, (own, *over_y((s1, s2, s3)), mine, other),
                       scratch=[pltpu.VMEM((HALF, K), BF)], name="unpair")
-    own, s1, s2, s3 = call(
-        back_kernel, [((rows, F), F32)] + [((rows, F), BF)] * 3,
+    gated, s2 = call(
+        back_kernel, [((rows, V), BF), ((rows, F), BF)],
         (keep, swap(send), query, attn, gate, idc, w_out),
-        scratch=[pltpu.VMEM((rows, V), F32)], flops=2 * rows * V * 2304, name="back")
-    p3 = over_tp(s3, 2)
-    p1 = over_tp(s1, 1)
-    p2 = over_tp(s2, 3)
+        scratch=[pltpu.VMEM((rows, V), F32)], flops=2 * rows * V * 768, name="back")
+    p2 = over_tp(s2, 2)
+    s1, s3 = call(beside_kernel, [((rows, F), BF)] * 2, (gated, w_out),
+                  flops=4 * rows * V * F, name="beside")
+    p1, p3 = over_tp(s1, 1), over_tp(s3, 3)
+    own, = call(here_kernel, [((rows, F), F32)], (gated, w_out), flops=2 * rows * V * F, name="here")
     return (own + p1.astype(F32) + p2.astype(F32) + p3.astype(F32)).astype(BF)
 
 

time: 83 us -> 71 us (0.86)
  the two profiles are of different devices: /device:TPU:1 before, /device:TPU:97 now
where the time goes in v2:
time: 71 us; the launch traced here: 70.7 us
  waiting for transfers between devices  29.5 us (42%)
  starting transfers between devices  26.2 us (37%)
  local copies, waits for them, and re-layouts  7.5 us (11%)
  Pallas kernels  6.45 us (9%)
  other arithmetic  0.84 us (1%)
    ppermute x11, starting transfers between devices, over_seq(): return lax.ppermute(block, 'seq', seq_route(move))  18.8 us
    ppermute x6, waiting for transfers between devices, over_tp(): return lax.ppermute(block, 'tp', [(i, i ^ bits) for i in range(4)])  14.9 us
    ppermute x11, waiting for transfers between devices, over_seq(): return lax.ppermute(block, 'seq', seq_route(move))  14.6 us
    ppermute x6, starting transfers between devices, over_tp(): return lax.ppermute(block, 'tp', [(i, i ^ bits) for i in range(4)])  7.41 us
    unnamed x24, local copies, waits for them, and re-layouts  6.7 us
    pallas_call x12, Pallas kernels, call(): pl.pallas_call(kernel, out_shape=shapes, in_specs=specs or [VM] * len(arg...  6.45 us
  transfers between devices with their start and end apart: 17, of which 13 were waited for; matrix products, arithmetic and copies ran while one was open for 1% of the time, Pallas kernels for 4%

profile of v2, /device:TPU:97, one launch (start us, length us, event | category | flops | bytes accessed | tf_op | source)
XLA Modules:
  0.0 70.7 jit_solution(1023574291559698179)
XLA Ops:
  0.0 2.7 %collective-permute-start = (bf16[256,512]{1,0:T(8,128)(2,1)}, bf16[256,512]{1,0:T(8,128)(2,1)S(1)}, u32[]{:S(2)}, u32[]{:S(2)}) collective-permute-start(bf16[256,512]{1,0:T(8,128)(2,1)} %refs_0_.1), channel_id=1, source_target_pairs={{0,2},{1,3},{2,0},{3,1},{4,6},{5,7},{6,4},{7,5},{8,10},{9,11},{10,... | collective-permute-start | bytes 786440 | tf_op jit(solution)/shard_map/ppermute | solution.py:269
  4.4 1.6 %copy-done.2 = bf16[2048,512]{1,0:T(8,128)(2,1)S(1)} copy-done((bf16[2048,512]{1,0:T(8,128)(2,1)S(1)}, bf16[2048,512]{1,0:T(8,128)(2,1)}, u32[]{:S(2)}) %copy-start.2) | copy-done | bytes 2097176
  6.0 1.2 %copy-done.4 = bf16[2048,256]{1,0:T(8,128)(2,1)S(1)} copy-done((bf16[2048,256]{1,0:T(8,128)(2,1)S(1)}, bf16[2048,256]{1,0:T(8,128)(2,1)}, u32[]{:S(2)}) %copy-start.4) | copy-done | bytes 1048600
  7.2 0.9 %copy-done.5 = bf16[256,512]{1,0:T(8,128)(2,1)S(1)} copy-done((bf16[256,512]{1,0:T(8,128)(2,1)S(1)}, bf16[256,512]{1,0:T(8,128)(2,1)}, u32[]{:S(2)}) %copy-start.5) | copy-done | bytes 262168
  11.5 4.0 %collective-permute-done.2.t3 = bf16[256,512]{1,0:T(8,128)(2,1)S(1)} collective-permute-done((bf16[256,512]{1,0:T(8,128)(2,1)}, bf16[256,512]{1,0:T(8,128)(2,1)S(1)}, u32[]{:S(2)}, u32[]{:S(2)}) %collective-permute-start.2) | collective-permute-done | bytes 262176 | tf_op jit(solution)/shard_map/ppermute | solution.py:269
  15.6 2.5 %front.1 = (bf16[4,256,512]{2,1,0:T(8,128)(2,1)S(1)}, bf16[256,256]{1,0:T(8,128)(2,1)S(1)}, bf16[256,512]{1,0:T(8,128)(2,1)S(1)}, f32[256,256]{1,0:T(8,128)S(1)}...) custom-call(bf16[256,512]{1,0:T(8,128)(2,1)S(1)} %get-tuple-element.37.t0, ...), custom_call_target="tpu_custom_call" | custom-call | flops 822083584 | bytes 6260736 | tf_op jit(solution)/shard_map/front/pallas_call | solution.py:256
  18.7 1.0 %collective-permute-done.3.other = bf16[272,256]{1,0:T(8,128)(2,1)S(1)} collective-permute-done((bf16[272,256]{1,0:T(8,128)(2,1)S(1)}, bf16[272,256]{1,0:T(8,128)(2,1)S(1)}, u32[]{:S(2)}, u32[]{:S(2)}) %collective-permute-start.3) | collective-permute-done | bytes 139296 | tf_op jit(solution)/shard_map/ppermute | solution.py:281
  19.9 3.0 %collective-permute-start.4 = (bf16[80,256]{1,0:T(8,128)(2,1)S(1)}, bf16[80,256]{1,0:T(8,128)(2,1)S(1)}, u32[]{:S(2)}, u32[]{:S(2)}) collective-permute-start(bf16[80,256]{1,0:T(8,128)(2,1)S(1)} %get-tuple-element.47), channel_id=1, source_target_pairs={{0,16},{4,20},{8,24},{12,28},{16,0},{20,4},{24,8},{28,12},{32,48},... | collective-permute-start | bytes 122888 | tf_op jit(solution)/shard_map/ppermute | solution.py:281
  23.7 1.6 %inner.1 = (bf16[256,256]{1,0:T(8,128)(2,1)S(1)}, f32[256,512]{1,0:T(8,128)S(1)}, f32[256,512]{1,0:T(8,128)S(1)}) custom-call(bf16[4,256,512]{2,1,0:T(8,128)(2,1)S(1)} %get-tuple-element.48.normed, bf16[2048,256]{1,0:T(8,128)(2,1)S(1)} %copy-done.3, bf16[2048,512]{1,0:T(8,128)(2,1)S(1)} %copy-done.1, bf16[256,256]{1,0:T(8,128)(2,1)S(1)} %get-tuple-element.49.key_r, ...), custom_call_target="tpu_custom_call" | custom-call | flops 1073741824 | bytes 6033408 | tf_op jit(solution)/shard_map/inner/pallas_call | solution.py:256
  25.9 1.4 %collective-permute-done.6.r3 = bf16[80,256]{1,0:T(8,128)(2,1)S(1)} collective-permute-done((bf16[80,256]{1,0:T(8,128)(2,1)S(1)}, bf16[80,256]{1,0:T(8,128)(2,1)S(1)}, u32[]{:S(2)}, u32[]{:S(2)}) %collective-permute-start.6) | collective-permute-done | bytes 40992 | tf_op jit(solution)/shard_map/ppermute | solution.py:281
  27.5 2.8 %collective-permute-done.7.beside.z1 = bf16[80,256]{1,0:T(8,128)(2,1)S(1)} collective-permute-done((bf16[80,256]{1,0:T(8,128)(2,1)S(1)}, bf16[80,256]{1,0:T(8,128)(2,1)S(1)}, u32[]{:S(2)}, u32[]{:S(2)}) %collective-permute-start.7) | collective-permute-done | bytes 40992 | tf_op jit(solution)/shard_map/ppermute | solution.py:281
  30.5 3.9 %collective-permute-done.8.beside.z2 = bf16[80,256]{1,0:T(8,128)(2,1)S(1)} collective-permute-done((bf16[80,256]{1,0:T(8,128)(2,1)S(1)}, bf16[80,256]{1,0:T(8,128)(2,1)S(1)}, u32[]{:S(2)}, u32[]{:S(2)}) %collective-permute-start.8) | collective-permute-done | bytes 40992 | tf_op jit(solution)/shard_map/ppermute | solution.py:281
  34.4 4.6 %collective-permute-start.9 = (bf16[80,256]{1,0:T(8,128)(2,1)S(1)}, bf16[80,256]{1,0:T(8,128)(2,1)S(1)}, u32[]{:S(2)}, u32[]{:S(2)}) collective-permute-start(bf16[80,256]{1,0:T(8,128)(2,1)S(1)} %four_rows.1), channel_id=1, source_target_pairs={{0,0},{4,4},{8,8},{12,12},{16,16},{20,20},{24,24},{28,28},{32,32},... | collective-permute-start | bytes 122888 | tf_op jit(solution)/shard_map/ppermute | solution.py:281
  39.0 1.4 %collective-permute-done.9.z3 = bf16[80,256]{1,0:T(8,128)(2,1)S(1)} collective-permute-done((bf16[80,256]{1,0:T(8,128)(2,1)S(1)}, bf16[80,256]{1,0:T(8,128)(2,1)S(1)}, u32[]{:S(2)}, u32[]{:S(2)}) %collective-permute-start.9) | collective-permute-done | bytes 40992 | tf_op jit(solution)/shard_map/ppermute | solution.py:281
  41.2 0.9 %collective-permute-start.11 = (bf16[80,256]{1,0:T(8,128)(2,1)S(1)}, bf16[80,256]{1,0:T(8,128)(2,1)S(1)}, u32[]{:S(2)}, u32[]{:S(2)}) collective-permute-start(bf16[80,256]{1,0:T(8,128)(2,1)S(1)} %get-tuple-element.58), channel_id=1, source_target_pairs={{0,8},{4,12},{8,0},{12,4},{16,24},{20,28},{24,16},{28,20},{32,40},... | collective-permute-start | bytes 122888 | tf_op jit(solution)/shard_map/ppermute | solution.py:281
  42.2 1.7 %collective-permute-start.12 = (bf16[80,256]{1,0:T(8,128)(2,1)S(1)}, bf16[80,256]{1,0:T(8,128)(2,1)S(1)}, u32[]{:S(2)}, u32[]{:S(2)}) collective-permute-start(bf16[80,256]{1,0:T(8,128)(2,1)S(1)} %get-tuple-element.59), channel_id=1, source_target_pairs={{0,24},{4,28},{8,16},{12,20},{16,8},{20,12},{24,0},{28,4},{32,56},... | collective-permute-start | bytes 122888 | tf_op jit(solution)/shard_map/ppermute | solution.py:281
  43.8 1.1 %collective-permute-done.10.r1 = bf16[80,256]{1,0:T(8,128)(2,1)S(1)} collective-permute-done((bf16[80,256]{1,0:T(8,128)(2,1)S(1)}, bf16[80,256]{1,0:T(8,128)(2,1)S(1)}, u32[]{:S(2)}, u32[]{:S(2)}) %collective-permute-start.10) | collective-permute-done | bytes 40992 | tf_op jit(solution)/shard_map/ppermute | solution.py:281
  44.9 1.3 %collective-permute-done.12.r3 = bf16[80,256]{1,0:T(8,128)(2,1)S(1)} collective-permute-done((bf16[80,256]{1,0:T(8,128)(2,1)S(1)}, bf16[80,256]{1,0:T(8,128)(2,1)S(1)}, u32[]{:S(2)}, u32[]{:S(2)}) %collective-permute-start.12) | collective-permute-done | bytes 40992 | tf_op jit(solution)/shard_map/ppermute | solution.py:281
  46.4 6.2 %collective-permute-start.13 = (bf16[272,256]{1,0:T(8,128)(2,1)S(1)}, bf16[272,256]{1,0:T(8,128)(2,1)S(1)}, u32[]{:S(2)}, u32[]{:S(2)}) collective-permute-start(bf16[272,256]{1,0:T(8,128)(2,1)S(1)} %get-tuple-element.61), channel_id=1, source_target_pairs={{0,4},{4,0},{8,12},{12,8},{16,20},{20,16},{24,28},{28,24},{32,36},... | collective-permute-start | bytes 417800 | tf_op jit(solution)/shard_map/ppermute | solution.py:281
  52.6 1.0 %collective-permute-done.13.other = bf16[272,256]{1,0:T(8,128)(2,1)S(1)} collective-permute-done((bf16[272,256]{1,0:T(8,128)(2,1)S(1)}, bf16[272,256]{1,0:T(8,128)(2,1)S(1)}, u32[]{:S(2)}, u32[]{:S(2)}) %collective-permute-start.13) | collective-permute-done | bytes 139296 | tf_op jit(solution)/shard_map/ppermute | solution.py:281
  54.4 1.9 %collective-permute-start.15 = (bf16[256,512]{1,0:T(8,128)(2,1)S(1)}, bf16[256,512]{1,0:T(8,128)(2,1)S(1)}, u32[]{:S(2)}, u32[]{:S(2)}) collective-permute-start(bf16[256,512]{1,0:T(8,128)(2,1)S(1)} %get-tuple-element.67), channel_id=1, source_target_pairs={{0,2},{1,3},{2,0},{3,1},{4,6},{5,7},{6,4},{7,5},{8,10},{9,11},{10,... | collective-permute-start | bytes 786440 | tf_op jit(solution)/shard_map/ppermute | solution.py:269
  56.7 1.2 %collective-permute-start.14 = (bf16[256,512]{1,0:T(8,128)(2,1)S(1)}, bf16[256,512]{1,0:T(8,128)(2,1)S(1)}, u32[]{:S(2)}, u32[]{:S(2)}) collective-permute-start(bf16[256,512]{1,0:T(8,128)(2,1)S(1)} %get-tuple-element.66), channel_id=1, source_target_pairs={{0,1},{1,0},{2,3},{3,2},{4,5},{5,4},{6,7},{7,6},{8,9},{9,8},{10,11... | collective-permute-start | bytes 786440 | tf_op jit(solution)/shard_map/ppermute | solution.py:269
  58.9 4.6 %collective-permute-done.15 = bf16[256,512]{1,0:T(8,128)(2,1)S(1)} collective-permute-done((bf16[256,512]{1,0:T(8,128)(2,1)S(1)}, bf16[256,512]{1,0:T(8,128)(2,1)S(1)}, u32[]{:S(2)}, u32[]{:S(2)}) %collective-permute-start.15) | collective-permute-done | bytes 262176 | tf_op jit(solution)/shard_map/ppermute | solution.py:269
  63.5 5.6 %collective-permute-done.14 = bf16[256,512]{1,0:T(8,128)(2,1)S(1)} collective-permute-done((bf16[256,512]{1,0:T(8,128)(2,1)S(1)}, bf16[256,512]{1,0:T(8,128)(2,1)S(1)}, u32[]{:S(2)}, u32[]{:S(2)}) %collective-permute-start.14) | collective-permute-done | bytes 262176 | tf_op jit(solution)/shard_map/ppermute | solution.py:269
  (48 shorter events, 12.3 us)
Async XLA Ops:
  0.0 11.5 %collective-permute-start = (bf16[256,512]{1,0:T(8,128)(2,1)}, bf16[256,512]{1,0:T(8,128)(2,1)S(1)}, u32[]{:S(2)}, u32[]{:S(2)}) collective-permute-start(bf16[256,512]{1,0:T(8,128)(2,1)} %refs_0_.1), channel_id=1, source_target_pairs={{0,2},{1,3},{2,0},{3,1},{4,6},{5,7},{6,4},{7,5},{8,10},{9,11},{10,... | collective-permute-start | bytes 786440 | tf_op jit(solution)/shard_map/ppermute | solution.py:269
  2.7 12.8 %collective-permute-start.2 = (bf16[256,512]{1,0:T(8,128)(2,1)}, bf16[256,512]{1,0:T(8,128)(2,1)S(1)}, u32[]{:S(2)}, u32[]{:S(2)}) collective-permute-start(bf16[256,512]{1,0:T(8,128)(2,1)} %refs_0_.1), channel_id=1, source_target_pairs={{0,3},{1,2},{2,1},{3,0},{4,7},{5,6},{6,5},{7,4},{8,11},{9,10},{10,... | collective-permute-start | bytes 786440 | tf_op jit(solution)/shard_map/ppermute | solution.py:269
  3.6 12.0 %collective-permute-start.1 = (bf16[256,512]{1,0:T(8,128)(2,1)}, bf16[256,512]{1,0:T(8,128)(2,1)S(1)}, u32[]{:S(2)}, u32[]{:S(2)}) collective-permute-start(bf16[256,512]{1,0:T(8,128)(2,1)} %refs_0_.1), channel_id=1, source_target_pairs={{0,1},{1,0},{2,3},{3,2},{4,5},{5,4},{6,7},{7,6},{8,9},{9,8},{10,11... | collective-permute-start | bytes 786440 | tf_op jit(solution)/shard_map/ppermute | solution.py:269
  4.4 1.6 %copy-start.2 = (bf16[2048,512]{1,0:T(8,128)(2,1)S(1)}, bf16[2048,512]{1,0:T(8,128)(2,1)}, u32[]{:S(2)}) copy-start(bf16[2048,512]{1,0:T(8,128)(2,1)} %refs_3_.1) | copy-start | bytes 6291460
  6.0 1.2 %copy-start.4 = (bf16[2048,256]{1,0:T(8,128)(2,1)S(1)}, bf16[2048,256]{1,0:T(8,128)(2,1)}, u32[]{:S(2)}) copy-start(bf16[2048,256]{1,0:T(8,128)(2,1)} %refs_2_.1) | copy-start | bytes 3145732
  15.6 8.1 %copy-start.1 = (bf16[2048,512]{1,0:T(8,128)(2,1)S(1)}, bf16[2048,512]{1,0:T(8,128)(2,1)}, u32[]{:S(2)}) copy-start(bf16[2048,512]{1,0:T(8,128)(2,1)} %wg.1) | copy-start | bytes 6291460
  15.6 8.1 %copy-start.3 = (bf16[2048,256]{1,0:T(8,128)(2,1)S(1)}, bf16[2048,256]{1,0:T(8,128)(2,1)}, u32[]{:S(2)}) copy-start(bf16[2048,256]{1,0:T(8,128)(2,1)} %wq.1) | copy-start | bytes 3145732
  15.6 8.1 %copy-start.9 = (s32[256]{0:T(256)S(1)}, s32[256]{0:T(256)}, u32[]{:S(2)}) copy-start(s32[256]{0:T(256)} %param.23) | copy-start | bytes 3076
  15.6 8.1 %copy-start.10 = (f32[512]{0:T(512)S(1)}, f32[512]{0:T(512)}, u32[]{:S(2)}) copy-start(f32[512]{0:T(512)} %param.21) | copy-start | bytes 6148
  18.1 1.7 %collective-permute-start.3 = (bf16[272,256]{1,0:T(8,128)(2,1)S(1)}, bf16[272,256]{1,0:T(8,128)(2,1)S(1)}, u32[]{:S(2)}, u32[]{:S(2)}) collective-permute-start(bf16[272,256]{1,0:T(8,128)(2,1)S(1)} %get-tuple-element.45), channel_id=1, source_target_pairs={{0,4},{4,0},{8,12},{12,8},{16,20},{20,16},{24,28},{28,24},{32,36},... | collective-permute-start | bytes 417800 | tf_op jit(solution)/shard_map/ppermute | solution.py:281
  19.9 5.4 %collective-permute-start.4 = (bf16[80,256]{1,0:T(8,128)(2,1)S(1)}, bf16[80,256]{1,0:T(8,128)(2,1)S(1)}, u32[]{:S(2)}, u32[]{:S(2)}) collective-permute-start(bf16[80,256]{1,0:T(8,128)(2,1)S(1)} %get-tuple-element.47), channel_id=1, source_target_pairs={{0,16},{4,20},{8,24},{12,28},{16,0},{20,4},{24,8},{28,12},{32,48},... | collective-permute-start | bytes 122888 | tf_op jit(solution)/shard_map/ppermute | solution.py:281
  22.9 3.0 %collective-permute-start.5 = (bf16[80,256]{1,0:T(8,128)(2,1)S(1)}, bf16[80,256]{1,0:T(8,128)(2,1)S(1)}, u32[]{:S(2)}, u32[]{:S(2)}) collective-permute-start(bf16[80,256]{1,0:T(8,128)(2,1)S(1)} %get-tuple-element.54), channel_id=1, source_target_pairs={{0,8},{4,12},{8,0},{12,4},{16,24},{20,28},{24,16},{28,20},{32,40},... | collective-permute-start | bytes 122888 | tf_op jit(solution)/shard_map/ppermute | solution.py:281
  23.3 4.1 %collective-permute-start.6 = (bf16[80,256]{1,0:T(8,128)(2,1)S(1)}, bf16[80,256]{1,0:T(8,128)(2,1)S(1)}, u32[]{:S(2)}, u32[]{:S(2)}) collective-permute-start(bf16[80,256]{1,0:T(8,128)(2,1)S(1)} %get-tuple-element.55), channel_id=1, source_target_pairs={{0,24},{4,28},{8,16},{12,20},{16,8},{20,12},{24,0},{28,4},{32,56},... | collective-permute-start | bytes 122888 | tf_op jit(solution)/shard_map/ppermute | solution.py:281
  23.7 30.0 %copy-start = (bf16[512,2048]{1,0:T(8,128)(2,1)S(1)}, bf16[512,2048]{1,0:T(8,128)(2,1)}, u32[]{:S(2)}) copy-start(bf16[512,2048]{1,0:T(8,128)(2,1)} %w_out.5) | copy-start | bytes 6291460
  27.4 2.9 %collective-permute-start.7 = (bf16[80,256]{1,0:T(8,128)(2,1)S(1)}, bf16[80,256]{1,0:T(8,128)(2,1)S(1)}, u32[]{:S(2)}, u32[]{:S(2)}) collective-permute-start(bf16[80,256]{1,0:T(8,128)(2,1)S(1)} %row.1), channel_id=1, source_target_pairs={{0,32},{4,36},{8,40},{12,44},{16,48},{20,52},{24,56},{28,60},{32,0... | collective-permute-start | bytes 122888 | tf_op jit(solution)/shard_map/ppermute | solution.py:281
  30.4 4.0 %collective-permute-start.8 = (bf16[80,256]{1,0:T(8,128)(2,1)S(1)}, bf16[80,256]{1,0:T(8,128)(2,1)S(1)}, u32[]{:S(2)}, u32[]{:S(2)}) collective-permute-start(bf16[80,256]{1,0:T(8,128)(2,1)S(1)} %two_rows.1.pair), channel_id=1, source_target_pairs={{0,64},{4,68},{8,72},{12,76},{16,80},{20,84},{24,88},{28,92},{32,9... | collective-permute-start | bytes 122888 | tf_op jit(solution)/shard_map/ppermute | solution.py:281
  34.4 6.0 %collective-permute-start.9 = (bf16[80,256]{1,0:T(8,128)(2,1)S(1)}, bf16[80,256]{1,0:T(8,128)(2,1)S(1)}, u32[]{:S(2)}, u32[]{:S(2)}) collective-permute-start(bf16[80,256]{1,0:T(8,128)(2,1)S(1)} %four_rows.1), channel_id=1, source_target_pairs={{0,0},{4,4},{8,8},{12,12},{16,16},{20,20},{24,24},{28,28},{32,32},... | collective-permute-start | bytes 122888 | tf_op jit(solution)/shard_map/ppermute | solution.py:281
  40.5 4.4 %collective-permute-start.10 = (bf16[80,256]{1,0:T(8,128)(2,1)S(1)}, bf16[80,256]{1,0:T(8,128)(2,1)S(1)}, u32[]{:S(2)}, u32[]{:S(2)}) collective-permute-start(bf16[80,256]{1,0:T(8,128)(2,1)S(1)} %get-tuple-element.57), channel_id=1, source_target_pairs={{0,16},{4,20},{8,24},{12,28},{16,0},{20,4},{24,8},{28,12},{32,48},... | collective-permute-start | bytes 122888 | tf_op jit(solution)/shard_map/ppermute | solution.py:281
  41.2 3.7 %collective-permute-start.11 = (bf16[80,256]{1,0:T(8,128)(2,1)S(1)}, bf16[80,256]{1,0:T(8,128)(2,1)S(1)}, u32[]{:S(2)}, u32[]{:S(2)}) collective-permute-start(bf16[80,256]{1,0:T(8,128)(2,1)S(1)} %get-tuple-element.58), channel_id=1, source_target_pairs={{0,8},{4,12},{8,0},{12,4},{16,24},{20,28},{24,16},{28,20},{32,40},... | collective-permute-start | bytes 122888 | tf_op jit(solution)/shard_map/ppermute | solution.py:281
  42.2 4.1 %collective-permute-start.12 = (bf16[80,256]{1,0:T(8,128)(2,1)S(1)}, bf16[80,256]{1,0:T(8,128)(2,1)S(1)}, u32[]{:S(2)}, u32[]{:S(2)}) collective-permute-start(bf16[80,256]{1,0:T(8,128)(2,1)S(1)} %get-tuple-element.59), channel_id=1, source_target_pairs={{0,24},{4,28},{8,16},{12,20},{16,8},{20,12},{24,0},{28,4},{32,56},... | collective-permute-start | bytes 122888 | tf_op jit(solution)/shard_map/ppermute | solution.py:281
  46.4 7.2 %collective-permute-start.13 = (bf16[272,256]{1,0:T(8,128)(2,1)S(1)}, bf16[272,256]{1,0:T(8,128)(2,1)S(1)}, u32[]{:S(2)}, u32[]{:S(2)}) collective-permute-start(bf16[272,256]{1,0:T(8,128)(2,1)S(1)} %get-tuple-element.61), channel_id=1, source_target_pairs={{0,4},{4,0},{8,12},{12,8},{16,20},{20,16},{24,28},{28,24},{32,36},... | collective-permute-start | bytes 417800 | tf_op jit(solution)/shard_map/ppermute | solution.py:281
  54.4 9.2 %collective-permute-start.15 = (bf16[256,512]{1,0:T(8,128)(2,1)S(1)}, bf16[256,512]{1,0:T(8,128)(2,1)S(1)}, u32[]{:S(2)}, u32[]{:S(2)}) collective-permute-start(bf16[256,512]{1,0:T(8,128)(2,1)S(1)} %get-tuple-element.67), channel_id=1, source_target_pairs={{0,2},{1,3},{2,0},{3,1},{4,6},{5,7},{6,4},{7,5},{8,10},{9,11},{10,... | collective-permute-start | bytes 786440 | tf_op jit(solution)/shard_map/ppermute | solution.py:269
  56.7 12.4 %collective-permute-start.14 = (bf16[256,512]{1,0:T(8,128)(2,1)S(1)}, bf16[256,512]{1,0:T(8,128)(2,1)S(1)}, u32[]{:S(2)}, u32[]{:S(2)}) collective-permute-start(bf16[256,512]{1,0:T(8,128)(2,1)S(1)} %get-tuple-element.66), channel_id=1, source_target_pairs={{0,1},{1,0},{2,3},{3,2},{4,5},{5,4},{6,7},{7,6},{8,9},{9,8},{10,11... | collective-permute-start | bytes 786440 | tf_op jit(solution)/shard_map/ppermute | solution.py:269
  57.9 11.9 %collective-permute-start.16 = (bf16[256,512]{1,0:T(8,128)(2,1)S(1)}, bf16[256,512]{1,0:T(8,128)(2,1)S(1)}, u32[]{:S(2)}, u32[]{:S(2)}) collective-permute-start(bf16[256,512]{1,0:T(8,128)(2,1)S(1)} %get-tuple-element.68), channel_id=1, source_target_pairs={{0,3},{1,2},{2,1},{3,0},{4,7},{5,6},{6,5},{7,4},{8,11},{9,10},{10,... | collective-permute-start | bytes 786440 | tf_op jit(solution)/shard_map/ppermute | solution.py:269
  (5 other events, 3.9 us)

commit v3 on v2

--- a/solution.py
+++ b/solution.py
@@ -9,8 +9,7 @@
 V = 512
 C = 64
 F = 512
-HALF = 256
-QUARTER = 64
+QUARTER = 128
 META = 16
 F32 = jnp.float32
 BF = jnp.bfloat16
@@ -91,9 +90,8 @@
 
 
 def front_kernel(t0, t1, t2, t3, gain, wk, wv, gd, gu, bias, idc,
-                 normed, key_o, value_o, cum_o, keep_o, send_o):
+                 normed, key_o, value_o, cum_o, element):
     x = lax.axis_index("tp")
-    _, _, c = place()
     parts = [(ref, flip(x, d)) for d, ref in zip(FLIPS, (t0, t1, t2, t3))]
     squares = 0.0
     for ref, _ in parts:
@@ -127,10 +125,8 @@
     ending = jnp.concatenate(ending, axis=0)
     decay = jnp.exp(ends[0] + after[0])
     decay = jnp.where(first == last, decay, 0.0)
-    meta = meta_of(decay, first, last)
-    for ref, side in ((keep_o, c), (send_o, 1 - c)):
-        ref[0:HALF] = dot(value_o[:, at(side, HALF)], ending, ((0,), (0,))).astype(BF)
-        ref[HALF:] = meta
+    element[0:V] = dot(value_o[...], ending, ((0,), (0,))).astype(BF)
+    element[V:] = meta_of(decay, first, last)
 
 
 def inner_kernel(normed, wq, wg, key_r, value_r, cum_r, idc, idr, head_gain,
@@ -165,9 +161,8 @@
 
 
 def pair_kernel(mine, other, own, s1, s2, s3, scratch):
-    _, y, c = place()
-    a, b = load(mine), load(other)
-    total = joined(pick(c == 0, a, b), pick(c == 0, b, a))
+    _, y, _ = place()
+    total = joined(load(other), load(mine))
     scratch[...] = total[0].astype(BF)
     meta = meta_of(*total[1:])
     for d, ref in zip(FLIPS, (own, s1, s2, s3)):
@@ -197,14 +192,10 @@
     save(total, joined(pick(odd, b, a), pick(odd, a, b)))
 
 
-def four_rows_kernel(pair, beside, total):
-    save(total, joined(load(beside), load(pair)))
-
-
-def spread_kernel(own, r1, r2, r3, z1, z2, z3, own_o, s1, s2, s3, stack):
+def spread_kernel(own, r1, r2, r3, z1, far3, far1, z2, own_o, s1, s2, s3, stack):
     z, y, _ = place()
     chips = stack_rows((own, r1, r2, r3), stack)
-    state, *rest = pick(z == 4, load(z3), load(z2))
+    state, *rest = pick(z == 4, joined(load(far1), load(far3)), load(z2))
     before = (jnp.where((lax.rem(z, 4) >= 2) | (z == 4), state, 0.0), *rest)
     run = pick(lax.rem(z, 2) == 1, joined(before, load(z1)), before)
     for i in range(4):
@@ -214,26 +205,21 @@
         ref[...] = stack[flip(y, d)]
 
 
-def unpair_kernel(own, r1, r2, r3, mine, other, keep, send, scratch):
-    _, y, c = place()
+def unpair_kernel(own, r1, r2, r3, other, into, after):
+    _, y, _ = place()
     for d, ref in zip(FLIPS, (own, r1, r2, r3)):
-        scratch[at(flip(y, d), QUARTER), :] = ref[0:QUARTER]
-    meta = own[QUARTER:].astype(F32)
-    into = (scratch[...].astype(F32), meta[0:1] + meta[1:2], meta[2:3], meta[3:4])
-    after = joined(into, pick(c == 0, load(mine), load(other)))
-    save(keep, pick(c == 0, into, after))
-    save(send, pick(c == 0, after, into))
-
-
-def back_kernel(mine, other, query, attn_r, gate, idc, w_out, gated_o, s2, attn):
+        into[at(flip(y, d), QUARTER), :] = ref[0:QUARTER]
+    into[V:] = own[QUARTER:]
+    save(after, joined(load(into), load(other)))
+
+
+def back_kernel(after, into, query, attn_r, gate, idc, w_out, gated_o, s2):
     x = lax.axis_index("tp")
     _, _, c = place()
-    prev = mine[HALF:].astype(F32)[3:4, 0:1]
-    seen = idc[...].astype(F32) == prev
-    for ref, side in ((mine, c), (other, 1 - c)):
-        inter = dot(query[...], ref[0:HALF], ((1,), (1,)))
-        attn[:, at(side, HALF)] = attn_r[:, at(side, HALF)] + jnp.where(seen, inter, 0.0)
-    full = attn[...]
+    before = jnp.where(c == 0, into[...].astype(F32), after[...].astype(F32))
+    seen = idc[...].astype(F32) == before[V + 3:V + 4, 0:1]
+    inter = dot(query[...], before[0:V].astype(BF), ((1,), (1,)))
+    full = attn_r[...] + jnp.where(seen, inter, 0.0)
     scale = lax.rsqrt(jnp.mean(full * full, axis=1, keepdims=True) + 1e-05)
     gated_o[...] = (full * scale * gate[...]).astype(BF)
     s2[...] = dot(gated_o[...], w_out[:, at(flip(x, 2), F)]).astype(BF)
@@ -269,21 +255,30 @@
     return lax.ppermute(block, "tp", [(i, i ^ bits) for i in range(4)])
 
 
-def seq_route(move):
+def over_seq(block, move):
     route = []
     for i in range(64):
         z, y, c = move(i // 8, i // 2 % 4, i % 2)
         route.append((i, z * 8 + y * 2 + c))
-    return route
-
-
-def over_seq(block, move):
-    return lax.ppermute(block, "seq", seq_route(move))
+    return lax.ppermute(block, "seq", route)
+
+
+def over_chips(block, move):
+    route = []
+    for i in range(256):
+        z, y, c, x = i // 32, i // 8 % 4, i // 4 % 2, i % 4
+        z, y, x = (*move(z, y), x) if c else (z, y, x ^ 1)
+        route.append((i, ((z * 4 + y) * 2 + c) * 4 + x))
+    return lax.ppermute(block, ("seq", "tp"), route)
+
+
+def to_row_4(block, z):
+    return lax.ppermute(block, "seq", [(z * 8 + i, 32 + i) for i in range(1, 8, 2)])
 
 
 def over_y(blocks):
     return [
-        over_seq(b, lambda z, y, c, d=d: (z, y ^ d, c)) for d, b in zip(FLIPS[1:], blocks)
+        over_chips(b, lambda z, y, d=d: (z, y ^ d)) for d, b in zip(FLIPS[1:], blocks)
     ]
 
 
@@ -297,42 +292,41 @@
     t1, t2, t3 = (over_tp(tokens, d) for d in FLIPS[1:])
     idc, idr = request_ids.reshape(rows, 1), request_ids.reshape(1, rows)
     piece = (QUARTER + META, K)
-    half = (HALF + META, K)
+    whole = (V + META, K)
     held = (tokens, norm_gain.reshape(4, 1, F), w_key, w_value, gate_down.T, gate_up,
             gate_bias.reshape(1, K))
     tokens, gain, w_key, w_value, down, up, bias = call(
         stage_kernel, [(a.shape, a.dtype) for a in held], held, specs=[HBM] * len(held),
         scratch=[pltpu.SemaphoreType.DMA((len(held),))], name="stage")
-    normed, key, value, cum, mine, send = call(
+    normed, key, value, cum, mine = call(
         front_kernel,
-        [((4, rows, F), BF), ((rows, K), BF), ((rows, V), BF), ((rows, K), F32), (half, BF), (half, BF)],
+        [((4, rows, F), BF), ((rows, K), BF), ((rows, V), BF), ((rows, K), F32), (whole, BF)],
         (tokens, t1, t2, t3, gain, w_key, w_value, down, up, bias, idc),
         flops=2 * rows * 2048 * 784, name="front")
-    other = swap(send)
+    other = swap(mine)
     query, attn, gate = call(
         inner_kernel,
         [((rows, K), BF), ((rows, V), F32), ((rows, V), F32)],
         (normed, w_query, w_gate_out, key, value, cum, idc, idr, head_gain.reshape(1, V)),
         flops=2 * rows * 2048 * 1024, name="inner")
     own, s1, s2, s3 = call(pair_kernel, [(piece, BF)] * 4, (mine, other),
-                           scratch=[pltpu.VMEM((HALF, K), BF)], name="pair")
+                           scratch=[pltpu.VMEM((V, K), BF)], name="pair")
     r1, r2, r3 = over_y((s1, s2, s3))
     r1, query = lax.optimization_barrier((r1, query))
     chips = [own, r1, r2, r3]
     row, = call(row_kernel, [(piece, BF)], chips, scratch=[pltpu.VMEM((4,) + piece, BF)], name="row")
-    z1 = over_seq(row, lambda z, y, c: (z ^ 1, y, c))
+    z1 = over_chips(row, lambda z, y: (z ^ 1, y))
     pair, = call(two_rows_kernel, [(piece, BF)], (row, z1), name="two_rows")
-    z2 = over_seq(pair, lambda z, y, c: (z ^ 2, y, c))
-    four, = call(four_rows_kernel, [(piece, BF)], (pair, z2), name="four_rows")
-    z3 = over_seq(four, lambda z, y, c: ({3: 4, 4: 3}.get(z, z), y, c))
-    own, s1, s2, s3 = call(spread_kernel, [(piece, BF)] * 4, (*chips, z1, z2, z3),
+    z2 = over_chips(pair, lambda z, y: (z ^ 2, y))
+    far1, far3 = to_row_4(pair, 1), to_row_4(pair, 3)
+    own, s1, s2, s3 = call(spread_kernel, [(piece, BF)] * 4, (*chips, z1, far3, far1, z2),
                            scratch=[pltpu.VMEM((4,) + piece, BF)], name="spread")
-    keep, send = call(unpair_kernel, [(half, BF)] * 2, (own, *over_y((s1, s2, s3)), mine, other),
-                      scratch=[pltpu.VMEM((HALF, K), BF)], name="unpair")
+    into, after = call(unpair_kernel, [(whole, BF)] * 2, (own, *over_y((s1, s2, s3)), other),
+                       name="unpair")
     gated, s2 = call(
         back_kernel, [((rows, V), BF), ((rows, F), BF)],
-        (keep, swap(send), query, attn, gate, idc, w_out),
-        scratch=[pltpu.VMEM((rows, V), F32)], flops=2 * rows * V * 768, name="back")
+        (after, swap(into), query, attn, gate, idc, w_out),
+        flops=2 * rows * V * 768, name="back")
     p2 = over_tp(s2, 2)
     s1, s3 = call(beside_kernel, [((rows, F), BF)] * 2, (gated, w_out),
                   flops=4 * rows * V * F, name="beside")

time: 71 us -> 66.4 us (0.935)
  the two profiles are of different devices: /device:TPU:97 before, /device:TPU:33 now
where the time goes in v3:
time: 66.4 us; the launch traced here: 66 us
  waiting for transfers between devices  26.2 us (39%)
  starting transfers between devices  24.8 us (37%)
  local copies, waits for them, and re-layouts  7.5 us (11%)
  Pallas kernels  6.49 us (10%)
  other arithmetic  0.84 us (1%)
    ppermute x6, waiting for transfers between devices, over_tp(): return lax.ppermute(block, 'tp', [(i, i ^ bits) for i in range(4)])  14.9 us
    ppermute x8, starting transfers between devices, over_chips(): return lax.ppermute(block, ('seq', 'tp'), route)  10.3 us
    ppermute x8, waiting for transfers between devices, over_chips(): return lax.ppermute(block, ('seq', 'tp'), route)  7.86 us
    ppermute x6, starting transfers between devices, over_tp(): return lax.ppermute(block, 'tp', [(i, i ^ bits) for i in range(4)])  7.43 us
    unnamed x24, local copies, waits for them, and re-layouts  6.7 us
    pallas_call x11, Pallas kernels, call(): pl.pallas_call(kernel, out_shape=shapes, in_specs=specs or [VM] * len(arg...  6.49 us
    ppermute x2, starting transfers between devices, to_row_4(): lax.ppermute(block, 'seq', [(z * 8 + i, 32 + i) for i in range(1, 8, 2)])  6.32 us
    ppermute x2, waiting for transfers between devices, over_seq(): return lax.ppermute(block, 'seq', route)  2.71 us
  transfers between devices with their start and end apart: 18, of which 12 were waited for; matrix products, arithmetic and copies ran while one was open for 1% of the time, Pallas kernels for 4%

profile of v3, /device:TPU:33, one launch (start us, length us, event | category | flops | bytes accessed | tf_op | source)
XLA Modules:
  0.0 66.0 jit_solution(3682827367212249588)
XLA Ops:
  0.0 2.7 %collective-permute-start = (bf16[256,512]{1,0:T(8,128)(2,1)}, bf16[256,512]{1,0:T(8,128)(2,1)S(1)}, u32[]{:S(2)}, u32[]{:S(2)}) collective-permute-start(bf16[256,512]{1,0:T(8,128)(2,1)} %refs_0_.1), channel_id=1, source_target_pairs={{0,2},{1,3},{2,0},{3,1},{4,6},{5,7},{6,4},{7,5},{8,10},{9,11},{10,... | collective-permute-start | bytes 786440 | tf_op jit(solution)/shard_map/ppermute | solution.py:255
  2.7 0.9 %collective-permute-start.2 = (bf16[256,512]{1,0:T(8,128)(2,1)}, bf16[256,512]{1,0:T(8,128)(2,1)S(1)}, u32[]{:S(2)}, u32[]{:S(2)}) collective-permute-start(bf16[256,512]{1,0:T(8,128)(2,1)} %refs_0_.1), channel_id=1, source_target_pairs={{0,3},{1,2},{2,1},{3,0},{4,7},{5,6},{6,5},{7,4},{8,11},{9,10},{10,... | collective-permute-start | bytes 786440 | tf_op jit(solution)/shard_map/ppermute | solution.py:255
  4.4 1.6 %copy-done.2 = bf16[2048,512]{1,0:T(8,128)(2,1)S(1)} copy-done((bf16[2048,512]{1,0:T(8,128)(2,1)S(1)}, bf16[2048,512]{1,0:T(8,128)(2,1)}, u32[]{:S(2)}) %copy-start.2) | copy-done | bytes 2097176
  6.0 1.2 %copy-done.4 = bf16[2048,256]{1,0:T(8,128)(2,1)S(1)} copy-done((bf16[2048,256]{1,0:T(8,128)(2,1)S(1)}, bf16[2048,256]{1,0:T(8,128)(2,1)}, u32[]{:S(2)}) %copy-start.4) | copy-done | bytes 1048600
  7.2 0.9 %copy-done.5 = bf16[256,512]{1,0:T(8,128)(2,1)S(1)} copy-done((bf16[256,512]{1,0:T(8,128)(2,1)S(1)}, bf16[256,512]{1,0:T(8,128)(2,1)}, u32[]{:S(2)}) %copy-start.5) | copy-done | bytes 262168
  11.5 4.0 %collective-permute-done.2.t3 = bf16[256,512]{1,0:T(8,128)(2,1)S(1)} collective-permute-done((bf16[256,512]{1,0:T(8,128)(2,1)}, bf16[256,512]{1,0:T(8,128)(2,1)S(1)}, u32[]{:S(2)}, u32[]{:S(2)}) %collective-permute-start.2) | collective-permute-done | bytes 262176 | tf_op jit(solution)/shard_map/ppermute | solution.py:255
  15.6 2.5 %front.1 = (bf16[4,256,512]{2,1,0:T(8,128)(2,1)S(1)}, bf16[256,256]{1,0:T(8,128)(2,1)S(1)}, bf16[256,512]{1,0:T(8,128)(2,1)S(1)}, f32[256,256]{1,0:T(8,128)S(1)}, bf16[528,256]{1,0:T(8,128)(2,1)S(1)}) custom-call(bf16[256,512]{1,0:T(8,128)(2,1)S(1)} %get-tuple-element.36.t0, bf16[256,512]{1,0:T(8,128)(2,1)S(1)} %collective-permute-done.t1, ...), custom_call_target="tpu_custom_call" | custom-call | flops 822083584 | bytes 6252544 | tf_op jit(solution)/shard_map/front/pallas_call | solution.py:242
  18.7 1.2 %collective-permute-done.3.other = bf16[528,256]{1,0:T(8,128)(2,1)S(1)} collective-permute-done((bf16[528,256]{1,0:T(8,128)(2,1)S(1)}, bf16[528,256]{1,0:T(8,128)(2,1)S(1)}, u32[]{:S(2)}, u32[]{:S(2)}) %collective-permute-start.3) | collective-permute-done | bytes 270368 | tf_op jit(solution)/shard_map/ppermute | solution.py:263
  20.1 3.0 %collective-permute-start.4 = (bf16[144,256]{1,0:T(8,128)(2,1)S(1)}, bf16[144,256]{1,0:T(8,128)(2,1)S(1)}, u32[]{:S(2)}, u32[]{:S(2)}) collective-permute-start(bf16[144,256]{1,0:T(8,128)(2,1)S(1)} %get-tuple-element.45), channel_id=1, source_target_pairs={{0,1},{1,0},{2,3},{3,2},{4,20},{5,21},{6,22},{7,23},{8,9},{9,8},{1... | collective-permute-start | bytes 221192 | tf_op jit(solution)/shard_map/ppermute | solution.py:272
  23.9 1.6 %inner.1 = (bf16[256,256]{1,0:T(8,128)(2,1)S(1)}, f32[256,512]{1,0:T(8,128)S(1)}, f32[256,512]{1,0:T(8,128)S(1)}) custom-call(bf16[4,256,512]{2,1,0:T(8,128)(2,1)S(1)} %get-tuple-element.46.normed, bf16[2048,256]{1,0:T(8,128)(2,1)S(1)} %copy-done.3, bf16[2048,512]{1,0:T(8,128)(2,1)S(1)} %copy-done.1, bf16[256,256]{1,0:T(8,128)(2,1)S(1)} %get-tuple-element.47.key_r, ...), custom_call_target="tpu_custom_call" | custom-call | flops 1073741824 | bytes 6033408 | tf_op jit(solution)/shard_map/inner/pallas_call | solution.py:242
  25.5 1.1 %collective-permute-done.5.r2 = bf16[144,256]{1,0:T(8,128)(2,1)S(1)} collective-permute-done((bf16[144,256]{1,0:T(8,128)(2,1)S(1)}, bf16[144,256]{1,0:T(8,128)(2,1)S(1)}, u32[]{:S(2)}, u32[]{:S(2)}) %collective-permute-start.5) | collective-permute-done | bytes 73760 | tf_op jit(solution)/shard_map/ppermute | solution.py:272
  26.6 1.3 %collective-permute-done.6.r3 = bf16[144,256]{1,0:T(8,128)(2,1)S(1)} collective-permute-done((bf16[144,256]{1,0:T(8,128)(2,1)S(1)}, bf16[144,256]{1,0:T(8,128)(2,1)S(1)}, u32[]{:S(2)}, u32[]{:S(2)}) %collective-permute-start.6) | collective-permute-done | bytes 73760 | tf_op jit(solution)/shard_map/ppermute | solution.py:272
  28.1 3.2 %collective-permute-done.7.beside.z1 = bf16[144,256]{1,0:T(8,128)(2,1)S(1)} collective-permute-done((bf16[144,256]{1,0:T(8,128)(2,1)S(1)}, bf16[144,256]{1,0:T(8,128)(2,1)S(1)}, u32[]{:S(2)}, u32[]{:S(2)}) %collective-permute-start.7) | collective-permute-done | bytes 73760 | tf_op jit(solution)/shard_map/ppermute | solution.py:272
  31.4 3.1 %collective-permute-start.10 = (bf16[144,256]{1,0:T(8,128)(2,1)S(1)}, bf16[144,256]{1,0:T(8,128)(2,1)S(1)}, u32[]{:S(2)}, u32[]{:S(2)}) collective-permute-start(bf16[144,256]{1,0:T(8,128)(2,1)S(1)} %two_rows.1), channel_id=1, source_target_pairs={{0,1},{1,0},{2,3},{3,2},{4,68},{5,69},{6,70},{7,71},{8,9},{9,8},{1... | collective-permute-start | bytes 221192 | tf_op jit(solution)/shard_map/ppermute | solution.py:272
  34.4 5.7 %collective-permute-start.9 = (bf16[144,256]{1,0:T(8,128)(2,1)S(1)}, bf16[144,256]{1,0:T(8,128)(2,1)S(1)}, u32[]{:S(2)}, u32[]{:S(2)}) collective-permute-start(bf16[144,256]{1,0:T(8,128)(2,1)S(1)} %two_rows.1), channel_id=1, source_target_pairs={{36,132},{44,140},{52,148},{60,156},{37,133},{45,141},{53,149},{61... | collective-permute-start | bytes 221192 | tf_op jit(solution)/shard_map/ppermute | solution.py:276
  41.7 1.1 %collective-permute-start.11 = (bf16[144,256]{1,0:T(8,128)(2,1)S(1)}, bf16[144,256]{1,0:T(8,128)(2,1)S(1)}, u32[]{:S(2)}, u32[]{:S(2)}) collective-permute-start(bf16[144,256]{1,0:T(8,128)(2,1)S(1)} %get-tuple-element.55), channel_id=1, source_target_pairs={{0,1},{1,0},{2,3},{3,2},{4,20},{5,21},{6,22},{7,23},{8,9},{9,8},{1... | collective-permute-start | bytes 221192 | tf_op jit(solution)/shard_map/ppermute | solution.py:272
  42.9 2.2 %collective-permute-start.13 = (bf16[144,256]{1,0:T(8,128)(2,1)S(1)}, bf16[144,256]{1,0:T(8,128)(2,1)S(1)}, u32[]{:S(2)}, u32[]{:S(2)}) collective-permute-start(bf16[144,256]{1,0:T(8,128)(2,1)S(1)} %get-tuple-element.57), channel_id=1, source_target_pairs={{0,1},{1,0},{2,3},{3,2},{4,28},{5,29},{6,30},{7,31},{8,9},{9,8},{1... | collective-permute-start | bytes 221192 | tf_op jit(solution)/shard_map/ppermute | solution.py:272
  45.0 1.5 %collective-permute-done.11.r1 = bf16[144,256]{1,0:T(8,128)(2,1)S(1)} collective-permute-done((bf16[144,256]{1,0:T(8,128)(2,1)S(1)}, bf16[144,256]{1,0:T(8,128)(2,1)S(1)}, u32[]{:S(2)}, u32[]{:S(2)}) %collective-permute-start.11) | collective-permute-done | bytes 73760 | tf_op jit(solution)/shard_map/ppermute | solution.py:272
  47.6 1.5 %collective-permute-done.14.into = bf16[528,256]{1,0:T(8,128)(2,1)S(1)} collective-permute-done((bf16[528,256]{1,0:T(8,128)(2,1)S(1)}, bf16[528,256]{1,0:T(8,128)(2,1)S(1)}, u32[]{:S(2)}, u32[]{:S(2)}) %collective-permute-start.14) | collective-permute-done | bytes 270368 | tf_op jit(solution)/shard_map/ppermute | solution.py:263
  49.7 2.1 %collective-permute-start.16 = (bf16[256,512]{1,0:T(8,128)(2,1)S(1)}, bf16[256,512]{1,0:T(8,128)(2,1)S(1)}, u32[]{:S(2)}, u32[]{:S(2)}) collective-permute-start(bf16[256,512]{1,0:T(8,128)(2,1)S(1)} %get-tuple-element.65), channel_id=1, source_target_pairs={{0,2},{1,3},{2,0},{3,1},{4,6},{5,7},{6,4},{7,5},{8,10},{9,11},{10,... | collective-permute-start | bytes 786440 | tf_op jit(solution)/shard_map/ppermute | solution.py:255
  52.3 1.0 %collective-permute-start.15 = (bf16[256,512]{1,0:T(8,128)(2,1)S(1)}, bf16[256,512]{1,0:T(8,128)(2,1)S(1)}, u32[]{:S(2)}, u32[]{:S(2)}) collective-permute-start(bf16[256,512]{1,0:T(8,128)(2,1)S(1)} %get-tuple-element.64), channel_id=1, source_target_pairs={{0,1},{1,0},{2,3},{3,2},{4,5},{5,4},{6,7},{7,6},{8,9},{9,8},{10,11... | collective-permute-start | bytes 786440 | tf_op jit(solution)/shard_map/ppermute | solution.py:255
  54.3 4.8 %collective-permute-done.16 = bf16[256,512]{1,0:T(8,128)(2,1)S(1)} collective-permute-done((bf16[256,512]{1,0:T(8,128)(2,1)S(1)}, bf16[256,512]{1,0:T(8,128)(2,1)S(1)}, u32[]{:S(2)}, u32[]{:S(2)}) %collective-permute-start.16) | collective-permute-done | bytes 262176 | tf_op jit(solution)/shard_map/ppermute | solution.py:255
  59.1 5.6 %collective-permute-done.15 = bf16[256,512]{1,0:T(8,128)(2,1)S(1)} collective-permute-done((bf16[256,512]{1,0:T(8,128)(2,1)S(1)}, bf16[256,512]{1,0:T(8,128)(2,1)S(1)}, u32[]{:S(2)}, u32[]{:S(2)}) %collective-permute-start.15) | collective-permute-done | bytes 262176 | tf_op jit(solution)/shard_map/ppermute | solution.py:255
  65.2 0.8 %add_convert_fusion = bf16[256,512]{1,0:T(8,128)(2,1)} fusion(bf16[256,512]{1,0:T(8,128)(2,1)S(1)} %collective-permute-done.17, bf16[256,512]{1,0:T(8,128)(2,1)S(1)} %collective-permute-done.16, f32[256,512]{1,0:T(8,128)S(1)} %here.1, bf16[256,512]{1,0:T(8,128)(2,1)S(1)} %collective-permute-done.15), kind=kLoop, calls=%fused_computation | loop fusion | flops 917504 | bytes 1572864 | tf_op jit(solution)/shard_map/convert_element_type | solution.py:335
  (49 shorter events, 11.3 us)
Async XLA Ops:
  0.0 11.5 %collective-permute-start = (bf16[256,512]{1,0:T(8,128)(2,1)}, bf16[256,512]{1,0:T(8,128)(2,1)S(1)}, u32[]{:S(2)}, u32[]{:S(2)}) collective-permute-start(bf16[256,512]{1,0:T(8,128)(2,1)} %refs_0_.1), channel_id=1, source_target_pairs={{0,2},{1,3},{2,0},{3,1},{4,6},{5,7},{6,4},{7,5},{8,10},{9,11},{10,... | collective-permute-start | bytes 786440 | tf_op jit(solution)/shard_map/ppermute | solution.py:255
  2.7 12.8 %collective-permute-start.2 = (bf16[256,512]{1,0:T(8,128)(2,1)}, bf16[256,512]{1,0:T(8,128)(2,1)S(1)}, u32[]{:S(2)}, u32[]{:S(2)}) collective-permute-start(bf16[256,512]{1,0:T(8,128)(2,1)} %refs_0_.1), channel_id=1, source_target_pairs={{0,3},{1,2},{2,1},{3,0},{4,7},{5,6},{6,5},{7,4},{8,11},{9,10},{10,... | collective-permute-start | bytes 786440 | tf_op jit(solution)/shard_map/ppermute | solution.py:255
  3.6 12.0 %collective-permute-start.1 = (bf16[256,512]{1,0:T(8,128)(2,1)}, bf16[256,512]{1,0:T(8,128)(2,1)S(1)}, u32[]{:S(2)}, u32[]{:S(2)}) collective-permute-start(bf16[256,512]{1,0:T(8,128)(2,1)} %refs_0_.1), channel_id=1, source_target_pairs={{0,1},{1,0},{2,3},{3,2},{4,5},{5,4},{6,7},{7,6},{8,9},{9,8},{10,11... | collective-permute-start | bytes 786440 | tf_op jit(solution)/shard_map/ppermute | solution.py:255
  4.4 1.6 %copy-start.2 = (bf16[2048,512]{1,0:T(8,128)(2,1)S(1)}, bf16[2048,512]{1,0:T(8,128)(2,1)}, u32[]{:S(2)}) copy-start(bf16[2048,512]{1,0:T(8,128)(2,1)} %refs_3_.1) | copy-start | bytes 6291460
  15.6 8.3 %copy-start.1 = (bf16[2048,512]{1,0:T(8,128)(2,1)S(1)}, bf16[2048,512]{1,0:T(8,128)(2,1)}, u32[]{:S(2)}) copy-start(bf16[2048,512]{1,0:T(8,128)(2,1)} %wg.1) | copy-start | bytes 6291460
  15.6 8.3 %copy-start.3 = (bf16[2048,256]{1,0:T(8,128)(2,1)S(1)}, bf16[2048,256]{1,0:T(8,128)(2,1)}, u32[]{:S(2)}) copy-start(bf16[2048,256]{1,0:T(8,128)(2,1)} %wq.1) | copy-start | bytes 3145732
  15.6 8.3 %copy-start.9 = (s32[256]{0:T(256)S(1)}, s32[256]{0:T(256)}, u32[]{:S(2)}) copy-start(s32[256]{0:T(256)} %param.23) | copy-start | bytes 3076
  15.6 8.3 %copy-start.10 = (f32[512]{0:T(512)S(1)}, f32[512]{0:T(512)}, u32[]{:S(2)}) copy-start(f32[512]{0:T(512)} %param.21) | copy-start | bytes 6148
  18.1 1.9 %collective-permute-start.3 = (bf16[528,256]{1,0:T(8,128)(2,1)S(1)}, bf16[528,256]{1,0:T(8,128)(2,1)S(1)}, u32[]{:S(2)}, u32[]{:S(2)}) collective-permute-start(bf16[528,256]{1,0:T(8,128)(2,1)S(1)} %get-tuple-element.43.mine), channel_id=1, source_target_pairs={{0,4},{4,0},{8,12},{12,8},{16,20},{20,16},{24,28},{28,24},{32,36},... | collective-permute-start | bytes 811016 | tf_op jit(solution)/shard_map/ppermute | solution.py:263
  20.1 5.4 %collective-permute-start.4 = (bf16[144,256]{1,0:T(8,128)(2,1)S(1)}, bf16[144,256]{1,0:T(8,128)(2,1)S(1)}, u32[]{:S(2)}, u32[]{:S(2)}) collective-permute-start(bf16[144,256]{1,0:T(8,128)(2,1)S(1)} %get-tuple-element.45), channel_id=1, source_target_pairs={{0,1},{1,0},{2,3},{3,2},{4,20},{5,21},{6,22},{7,23},{8,9},{9,8},{1... | collective-permute-start | bytes 221192 | tf_op jit(solution)/shard_map/ppermute | solution.py:272
  23.1 3.5 %collective-permute-start.5 = (bf16[144,256]{1,0:T(8,128)(2,1)S(1)}, bf16[144,256]{1,0:T(8,128)(2,1)S(1)}, u32[]{:S(2)}, u32[]{:S(2)}) collective-permute-start(bf16[144,256]{1,0:T(8,128)(2,1)S(1)} %get-tuple-element.52), channel_id=1, source_target_pairs={{0,1},{1,0},{2,3},{3,2},{4,12},{5,13},{6,14},{7,15},{8,9},{9,8},{1... | collective-permute-start | bytes 221192 | tf_op jit(solution)/shard_map/ppermute | solution.py:272
  23.5 4.4 %collective-permute-start.6 = (bf16[144,256]{1,0:T(8,128)(2,1)S(1)}, bf16[144,256]{1,0:T(8,128)(2,1)S(1)}, u32[]{:S(2)}, u32[]{:S(2)}) collective-permute-start(bf16[144,256]{1,0:T(8,128)(2,1)S(1)} %get-tuple-element.53), channel_id=1, source_target_pairs={{0,1},{1,0},{2,3},{3,2},{4,28},{5,29},{6,30},{7,31},{8,9},{9,8},{1... | collective-permute-start | bytes 221192 | tf_op jit(solution)/shard_map/ppermute | solution.py:272
  23.9 25.2 %copy-start = (bf16[512,2048]{1,0:T(8,128)(2,1)S(1)}, bf16[512,2048]{1,0:T(8,128)(2,1)}, u32[]{:S(2)}) copy-start(bf16[512,2048]{1,0:T(8,128)(2,1)} %w_out.5) | copy-start | bytes 6291460
  28.0 3.3 %collective-permute-start.7 = (bf16[144,256]{1,0:T(8,128)(2,1)S(1)}, bf16[144,256]{1,0:T(8,128)(2,1)S(1)}, u32[]{:S(2)}, u32[]{:S(2)}) collective-permute-start(bf16[144,256]{1,0:T(8,128)(2,1)S(1)} %row.1), channel_id=1, source_target_pairs={{0,1},{1,0},{2,3},{3,2},{4,36},{5,37},{6,38},{7,39},{8,9},{9,8},{1... | collective-permute-start | bytes 221192 | tf_op jit(solution)/shard_map/ppermute | solution.py:272
  31.4 9.4 %collective-permute-start.10 = (bf16[144,256]{1,0:T(8,128)(2,1)S(1)}, bf16[144,256]{1,0:T(8,128)(2,1)S(1)}, u32[]{:S(2)}, u32[]{:S(2)}) collective-permute-start(bf16[144,256]{1,0:T(8,128)(2,1)S(1)} %two_rows.1), channel_id=1, source_target_pairs={{0,1},{1,0},{2,3},{3,2},{4,68},{5,69},{6,70},{7,71},{8,9},{9,8},{1... | collective-permute-start | bytes 221192 | tf_op jit(solution)/shard_map/ppermute | solution.py:272
  34.4 7.1 %collective-permute-start.9 = (bf16[144,256]{1,0:T(8,128)(2,1)S(1)}, bf16[144,256]{1,0:T(8,128)(2,1)S(1)}, u32[]{:S(2)}, u32[]{:S(2)}) collective-permute-start(bf16[144,256]{1,0:T(8,128)(2,1)S(1)} %two_rows.1), channel_id=1, source_target_pairs={{36,132},{44,140},{52,148},{60,156},{37,133},{45,141},{53,149},{61... | collective-permute-start | bytes 221192 | tf_op jit(solution)/shard_map/ppermute | solution.py:276
  40.1 1.4 %collective-permute-start.8 = (bf16[144,256]{1,0:T(8,128)(2,1)S(1)}, bf16[144,256]{1,0:T(8,128)(2,1)S(1)}, u32[]{:S(2)}, u32[]{:S(2)}) collective-permute-start(bf16[144,256]{1,0:T(8,128)(2,1)S(1)} %two_rows.1), channel_id=1, source_target_pairs={{100,132},{108,140},{116,148},{124,156},{101,133},{109,141},{117,1... | collective-permute-start | bytes 221192 | tf_op jit(solution)/shard_map/ppermute | solution.py:276
  41.7 4.8 %collective-permute-start.11 = (bf16[144,256]{1,0:T(8,128)(2,1)S(1)}, bf16[144,256]{1,0:T(8,128)(2,1)S(1)}, u32[]{:S(2)}, u32[]{:S(2)}) collective-permute-start(bf16[144,256]{1,0:T(8,128)(2,1)S(1)} %get-tuple-element.55), channel_id=1, source_target_pairs={{0,1},{1,0},{2,3},{3,2},{4,20},{5,21},{6,22},{7,23},{8,9},{9,8},{1... | collective-permute-start | bytes 221192 | tf_op jit(solution)/shard_map/ppermute | solution.py:272
  42.8 3.7 %collective-permute-start.12 = (bf16[144,256]{1,0:T(8,128)(2,1)S(1)}, bf16[144,256]{1,0:T(8,128)(2,1)S(1)}, u32[]{:S(2)}, u32[]{:S(2)}) collective-permute-start(bf16[144,256]{1,0:T(8,128)(2,1)S(1)} %get-tuple-element.56), channel_id=1, source_target_pairs={{0,1},{1,0},{2,3},{3,2},{4,12},{5,13},{6,14},{7,15},{8,9},{9,8},{1... | collective-permute-start | bytes 221192 | tf_op jit(solution)/shard_map/ppermute | solution.py:272
  42.9 4.4 %collective-permute-start.13 = (bf16[144,256]{1,0:T(8,128)(2,1)S(1)}, bf16[144,256]{1,0:T(8,128)(2,1)S(1)}, u32[]{:S(2)}, u32[]{:S(2)}) collective-permute-start(bf16[144,256]{1,0:T(8,128)(2,1)S(1)} %get-tuple-element.57), channel_id=1, source_target_pairs={{0,1},{1,0},{2,3},{3,2},{4,28},{5,29},{6,30},{7,31},{8,9},{9,8},{1... | collective-permute-start | bytes 221192 | tf_op jit(solution)/shard_map/ppermute | solution.py:272
  47.5 1.6 %collective-permute-start.14 = (bf16[528,256]{1,0:T(8,128)(2,1)S(1)}, bf16[528,256]{1,0:T(8,128)(2,1)S(1)}, u32[]{:S(2)}, u32[]{:S(2)}) collective-permute-start(bf16[528,256]{1,0:T(8,128)(2,1)S(1)} %get-tuple-element.59), channel_id=1, source_target_pairs={{0,4},{4,0},{8,12},{12,8},{16,20},{20,16},{24,28},{28,24},{32,36},... | collective-permute-start | bytes 811016 | tf_op jit(solution)/shard_map/ppermute | solution.py:263
  49.7 9.4 %collective-permute-start.16 = (bf16[256,512]{1,0:T(8,128)(2,1)S(1)}, bf16[256,512]{1,0:T(8,128)(2,1)S(1)}, u32[]{:S(2)}, u32[]{:S(2)}) collective-permute-start(bf16[256,512]{1,0:T(8,128)(2,1)S(1)} %get-tuple-element.65), channel_id=1, source_target_pairs={{0,2},{1,3},{2,0},{3,1},{4,6},{5,7},{6,4},{7,5},{8,10},{9,11},{10,... | collective-permute-start | bytes 786440 | tf_op jit(solution)/shard_map/ppermute | solution.py:255
  52.3 12.4 %collective-permute-start.15 = (bf16[256,512]{1,0:T(8,128)(2,1)S(1)}, bf16[256,512]{1,0:T(8,128)(2,1)S(1)}, u32[]{:S(2)}, u32[]{:S(2)}) collective-permute-start(bf16[256,512]{1,0:T(8,128)(2,1)S(1)} %get-tuple-element.64), channel_id=1, source_target_pairs={{0,1},{1,0},{2,3},{3,2},{4,5},{5,4},{6,7},{7,6},{8,9},{9,8},{10,11... | collective-permute-start | bytes 786440 | tf_op jit(solution)/shard_map/ppermute | solution.py:255
  53.3 11.9 %collective-permute-start.17 = (bf16[256,512]{1,0:T(8,128)(2,1)S(1)}, bf16[256,512]{1,0:T(8,128)(2,1)S(1)}, u32[]{:S(2)}, u32[]{:S(2)}) collective-permute-start(bf16[256,512]{1,0:T(8,128)(2,1)S(1)} %get-tuple-element.66), channel_id=1, source_target_pairs={{0,3},{1,2},{2,1},{3,0},{4,7},{5,6},{6,5},{7,4},{8,11},{9,10},{10,... | collective-permute-start | bytes 786440 | tf_op jit(solution)/shard_map/ppermute | solution.py:255
  (6 other events, 5.1 us)

commit v4 on v3

--- a/solution.py
+++ b/solution.py
@@ -160,6 +160,16 @@
         attn_o[rows] = dot(weights, value_r[0:C * b + C])
 
 
+def hold_kernel(a, b, c, d):
+    c[...] = a[...]
+    d[...] = b[...]
+
+
+def at_middle():
+    z, y, _ = place()
+    return (z == 4) & (y == 0)
+
+
 def pair_kernel(mine, other, own, s1, s2, s3, scratch):
     _, y, _ = place()
     total = joined(load(other), load(mine))
@@ -192,11 +202,12 @@
     save(total, joined(pick(odd, b, a), pick(odd, a, b)))
 
 
-def spread_kernel(own, r1, r2, r3, z1, far3, far1, z2, own_o, s1, s2, s3, stack):
+def spread_kernel(own, r1, r2, r3, z1, z2, pair, own_o, s1, s2, s3, half, stack):
     z, y, _ = place()
     chips = stack_rows((own, r1, r2, r3), stack)
-    state, *rest = pick(z == 4, joined(load(far1), load(far3)), load(z2))
-    before = (jnp.where((lax.rem(z, 4) >= 2) | (z == 4), state, 0.0), *rest)
+    other = load(z2)
+    save(half, joined(other, load(pair)))
+    before = (jnp.where(lax.rem(z, 4) >= 2, other[0], 0.0), *other[1:])
     run = pick(lax.rem(z, 2) == 1, joined(before, load(z1)), before)
     for i in range(4):
         save(stack.at[i], run)
@@ -205,20 +216,32 @@
         ref[...] = stack[flip(y, d)]
 
 
-def unpair_kernel(own, r1, r2, r3, other, into, after):
+def unpair_kernel(own, far0, far2, r1, r2, r3, other, into, after):
     _, y, _ = place()
     for d, ref in zip(FLIPS, (own, r1, r2, r3)):
         into[at(flip(y, d), QUARTER), :] = ref[0:QUARTER]
     into[V:] = own[QUARTER:]
     save(after, joined(load(into), load(other)))
 
-
-def back_kernel(after, into, query, attn_r, gate, idc, w_out, gated_o, s2):
+    @pl.when(at_middle())
+    def _():
+        into[QUARTER:2 * QUARTER] = far0[0:QUARTER]
+        into[3 * QUARTER:V] = far2[0:QUARTER]
+
+
+def back_kernel(after, into, far0, far2, query, attn_r, gate, idc, w_out, gated_o, s2, before):
     x = lax.axis_index("tp")
     _, _, c = place()
-    before = jnp.where(c == 0, into[...].astype(F32), after[...].astype(F32))
-    seen = idc[...].astype(F32) == before[V + 3:V + 4, 0:1]
-    inter = dot(query[...], before[0:V].astype(BF), ((1,), (1,)))
+    before[...] = jnp.where(c == 0, into[...].astype(F32), after[...].astype(F32)).astype(BF)
+
+    @pl.when(at_middle() & (c == 0))
+    def _():
+        before[0:QUARTER] = far0[0:QUARTER]
+        before[2 * QUARTER:3 * QUARTER] = far2[0:QUARTER]
+        before[V:] = far0[QUARTER:]
+
+    seen = idc[...].astype(F32) == before[V:].astype(F32)[3:4, 0:1]
+    inter = dot(query[...], before[0:V], ((1,), (1,)))
     full = attn_r[...] + jnp.where(seen, inter, 0.0)
     scale = lax.rsqrt(jnp.mean(full * full, axis=1, keepdims=True) + 1e-05)
     gated_o[...] = (full * scale * gate[...]).astype(BF)
@@ -272,8 +295,18 @@
     return lax.ppermute(block, ("seq", "tp"), route)
 
 
-def to_row_4(block, z):
-    return lax.ppermute(block, "seq", [(z * 8 + i, 32 + i) for i in range(1, 8, 2)])
+def to_middle(block, y):
+    pairs = {25 + 2 * (y + i): 32 + i for i in range(2)}
+    pairs |= {b: a for a, b in pairs.items()}
+    route = []
+    for i in range(256):
+        seq, x = i // 4, i % 4
+        if seq not in pairs:
+            seq, x = (seq, x ^ 1) if seq ^ 1 in pairs else (seq ^ 1, x)
+        else:
+            seq = pairs[seq]
+        route.append((i, seq * 4 + x))
+    return lax.ppermute(block, ("seq", "tp"), route)
 
 
 def over_y(blocks):
@@ -312,21 +345,22 @@
     own, s1, s2, s3 = call(pair_kernel, [(piece, BF)] * 4, (mine, other),
                            scratch=[pltpu.VMEM((V, K), BF)], name="pair")
     r1, r2, r3 = over_y((s1, s2, s3))
-    r1, query = lax.optimization_barrier((r1, query))
     chips = [own, r1, r2, r3]
     row, = call(row_kernel, [(piece, BF)], chips, scratch=[pltpu.VMEM((4,) + piece, BF)], name="row")
     z1 = over_chips(row, lambda z, y: (z ^ 1, y))
+    z1, query = lax.optimization_barrier((z1, query))
     pair, = call(two_rows_kernel, [(piece, BF)], (row, z1), name="two_rows")
     z2 = over_chips(pair, lambda z, y: (z ^ 2, y))
-    far1, far3 = to_row_4(pair, 1), to_row_4(pair, 3)
-    own, s1, s2, s3 = call(spread_kernel, [(piece, BF)] * 4, (*chips, z1, far3, far1, z2),
-                           scratch=[pltpu.VMEM((4,) + piece, BF)], name="spread")
-    into, after = call(unpair_kernel, [(whole, BF)] * 2, (own, *over_y((s1, s2, s3)), other),
+    own, s1, s2, s3, half = call(spread_kernel, [(piece, BF)] * 5, (*chips, z1, z2, pair),
+                                 scratch=[pltpu.VMEM((4,) + piece, BF)], name="spread")
+    far0, far2 = call(hold_kernel, [(piece, BF)] * 2, (to_middle(half, 0), to_middle(half, 2)),
+                      flops=2 * rows * V * 4096, name="hold")
+    into, after = call(unpair_kernel, [(whole, BF)] * 2, (own, far0, far2, *over_y((s1, s2, s3)), other),
                        name="unpair")
     gated, s2 = call(
         back_kernel, [((rows, V), BF), ((rows, F), BF)],
-        (after, swap(into), query, attn, gate, idc, w_out),
-        flops=2 * rows * V * 768, name="back")
+        (after, swap(into), far0, far2, query, attn, gate, idc, w_out),
+        scratch=[pltpu.VMEM(whole, BF)], flops=2 * rows * V * 768, name="back")
     p2 = over_tp(s2, 2)
     s1, s3 = call(beside_kernel, [((rows, F), BF)] * 2, (gated, w_out),
                   flops=4 * rows * V * F, name="beside")

time: 66.4 us -> 66.2 us (level)
  the two profiles are of different devices: /device:TPU:33 before, /device:TPU:97 now
where the time goes in v4:
time: 66.2 us; the launch traced here: 65.8 us
  waiting for transfers between devices  31.4 us (47%)
  starting transfers between devices  19.4 us (29%)
  local copies, waits for them, and re-layouts  7.5 us (11%)
  Pallas kernels  6.61 us (10%)
  other arithmetic  0.84 us (1%)
    ppermute x6, waiting for transfers between devices, over_tp(): return lax.ppermute(block, 'tp', [(i, i ^ bits) for i in range(4)])  14.9 us
    ppermute x8, waiting for transfers between devices, over_chips(): return lax.ppermute(block, ('seq', 'tp'), route)  13.4 us
    ppermute x6, starting transfers between devices, over_tp(): return lax.ppermute(block, 'tp', [(i, i ^ bits) for i in range(4)])  7.43 us
    ppermute x8, starting transfers between devices, over_chips(): return lax.ppermute(block, ('seq', 'tp'), route)  7.22 us
    unnamed x24, local copies, waits for them, and re-layouts  6.69 us
    pallas_call x12, Pallas kernels, call(): pl.pallas_call(kernel, out_shape=shapes, in_specs=specs or [VM] * len(arg...  6.61 us
    ppermute x2, starting transfers between devices, to_middle(): return lax.ppermute(block, ('seq', 'tp'), route)  3.74 us
    ppermute x2, waiting for transfers between devices, over_seq(): return lax.ppermute(block, 'seq', route)  2.71 us
  transfers between devices with their start and end apart: 18, of which 15 were waited for; matrix products, arithmetic and copies ran while one was open for 1% of the time, Pallas kernels for 4%

profile of v4, /device:TPU:97, one launch (start us, length us, event | category | flops | bytes accessed | tf_op | source)
XLA Modules:
  0.0 65.8 jit_solution(17941096921302725606)
XLA Ops:
  0.0 2.7 %collective-permute-start = (bf16[256,512]{1,0:T(8,128)(2,1)}, bf16[256,512]{1,0:T(8,128)(2,1)S(1)}, u32[]{:S(2)}, u32[]{:S(2)}) collective-permute-start(bf16[256,512]{1,0:T(8,128)(2,1)} %refs_0_.1), channel_id=1, source_target_pairs={{0,2},{1,3},{2,0},{3,1},{4,6},{5,7},{6,4},{7,5},{8,10},{9,11},{10,... | collective-permute-start | bytes 786440 | tf_op jit(solution)/shard_map/ppermute | solution.py:278
  2.7 0.9 %collective-permute-start.2 = (bf16[256,512]{1,0:T(8,128)(2,1)}, bf16[256,512]{1,0:T(8,128)(2,1)S(1)}, u32[]{:S(2)}, u32[]{:S(2)}) collective-permute-start(bf16[256,512]{1,0:T(8,128)(2,1)} %refs_0_.1), channel_id=1, source_target_pairs={{0,3},{1,2},{2,1},{3,0},{4,7},{5,6},{6,5},{7,4},{8,11},{9,10},{10,... | collective-permute-start | bytes 786440 | tf_op jit(solution)/shard_map/ppermute | solution.py:278
  4.4 1.6 %copy-done.2 = bf16[2048,512]{1,0:T(8,128)(2,1)S(1)} copy-done((bf16[2048,512]{1,0:T(8,128)(2,1)S(1)}, bf16[2048,512]{1,0:T(8,128)(2,1)}, u32[]{:S(2)}) %copy-start.2) | copy-done | bytes 2097176
  6.0 1.2 %copy-done.4 = bf16[2048,256]{1,0:T(8,128)(2,1)S(1)} copy-done((bf16[2048,256]{1,0:T(8,128)(2,1)S(1)}, bf16[2048,256]{1,0:T(8,128)(2,1)}, u32[]{:S(2)}) %copy-start.4) | copy-done | bytes 1048600
  7.2 0.9 %copy-done.5 = bf16[256,512]{1,0:T(8,128)(2,1)S(1)} copy-done((bf16[256,512]{1,0:T(8,128)(2,1)S(1)}, bf16[256,512]{1,0:T(8,128)(2,1)}, u32[]{:S(2)}) %copy-start.5) | copy-done | bytes 262168
  11.5 4.0 %collective-permute-done.2.t3 = bf16[256,512]{1,0:T(8,128)(2,1)S(1)} collective-permute-done((bf16[256,512]{1,0:T(8,128)(2,1)}, bf16[256,512]{1,0:T(8,128)(2,1)S(1)}, u32[]{:S(2)}, u32[]{:S(2)}) %collective-permute-start.2) | collective-permute-done | bytes 262176 | tf_op jit(solution)/shard_map/ppermute | solution.py:278
  15.6 2.5 %front.1 = (bf16[4,256,512]{2,1,0:T(8,128)(2,1)S(1)}, bf16[256,256]{1,0:T(8,128)(2,1)S(1)}, bf16[256,512]{1,0:T(8,128)(2,1)S(1)}, f32[256,256]{1,0:T(8,128)S(1)}, bf16[528,256]{1,0:T(8,128)(2,1)S(1)}) custom-call(bf16[256,512]{1,0:T(8,128)(2,1)S(1)} %get-tuple-element.39.t0, bf16[256,512]{1,0:T(8,128)(2,1)S(1)} %collective-permute-done.t1, ...), custom_call_target="tpu_custom_call" | custom-call | flops 822083584 | bytes 6252544 | tf_op jit(solution)/shard_map/front/pallas_call | solution.py:265
  18.8 1.2 %collective-permute-done.3.other = bf16[528,256]{1,0:T(8,128)(2,1)S(1)} collective-permute-done((bf16[528,256]{1,0:T(8,128)(2,1)S(1)}, bf16[528,256]{1,0:T(8,128)(2,1)S(1)}, u32[]{:S(2)}, u32[]{:S(2)}) %collective-permute-start.3) | collective-permute-done | bytes 270368 | tf_op jit(solution)/shard_map/ppermute | solution.py:286
  20.1 3.0 %collective-permute-start.4 = (bf16[144,256]{1,0:T(8,128)(2,1)S(1)}, bf16[144,256]{1,0:T(8,128)(2,1)S(1)}, u32[]{:S(2)}, u32[]{:S(2)}) collective-permute-start(bf16[144,256]{1,0:T(8,128)(2,1)S(1)} %get-tuple-element.48), channel_id=1, source_target_pairs={{0,1},{1,0},{2,3},{3,2},{4,20},{5,21},{6,22},{7,23},{8,9},{9,8},{1... | collective-permute-start | bytes 221192 | tf_op jit(solution)/shard_map/ppermute | solution.py:295
  23.9 1.0 %collective-permute-done.4.r1 = bf16[144,256]{1,0:T(8,128)(2,1)S(1)} collective-permute-done((bf16[144,256]{1,0:T(8,128)(2,1)S(1)}, bf16[144,256]{1,0:T(8,128)(2,1)S(1)}, u32[]{:S(2)}, u32[]{:S(2)}) %collective-permute-start.4) | collective-permute-done | bytes 73760 | tf_op jit(solution)/shard_map/ppermute | solution.py:295
  24.9 1.7 %collective-permute-done.5.r2 = bf16[144,256]{1,0:T(8,128)(2,1)S(1)} collective-permute-done((bf16[144,256]{1,0:T(8,128)(2,1)S(1)}, bf16[144,256]{1,0:T(8,128)(2,1)S(1)}, u32[]{:S(2)}, u32[]{:S(2)}) %collective-permute-start.5) | collective-permute-done | bytes 73760 | tf_op jit(solution)/shard_map/ppermute | solution.py:295
  26.6 1.3 %collective-permute-done.6.r3 = bf16[144,256]{1,0:T(8,128)(2,1)S(1)} collective-permute-done((bf16[144,256]{1,0:T(8,128)(2,1)S(1)}, bf16[144,256]{1,0:T(8,128)(2,1)S(1)}, u32[]{:S(2)}, u32[]{:S(2)}) %collective-permute-start.6) | collective-permute-done | bytes 73760 | tf_op jit(solution)/shard_map/ppermute | solution.py:295
  28.2 1.6 %inner.1 = (bf16[256,256]{1,0:T(8,128)(2,1)S(1)}, f32[256,512]{1,0:T(8,128)S(1)}, f32[256,512]{1,0:T(8,128)S(1)}) custom-call(bf16[4,256,512]{2,1,0:T(8,128)(2,1)S(1)} %get-tuple-element.51.normed, bf16[2048,256]{1,0:T(8,128)(2,1)S(1)} %copy-done.3, bf16[2048,512]{1,0:T(8,128)(2,1)S(1)} %copy-done.1, bf16[256,256]{1,0:T(8,128)(2,1)S(1)} %get-tuple-element.52.key_r, ...), custom_call_target="tpu_custom_call" | custom-call | flops 1073741824 | bytes 6033408 | tf_op jit(solution)/shard_map/inner/pallas_call | solution.py:265
  29.8 1.5 %collective-permute-done.7.beside.z1 = bf16[144,256]{1,0:T(8,128)(2,1)S(1)} collective-permute-done((bf16[144,256]{1,0:T(8,128)(2,1)S(1)}, bf16[144,256]{1,0:T(8,128)(2,1)S(1)}, u32[]{:S(2)}, u32[]{:S(2)}) %collective-permute-start.7) | collective-permute-done | bytes 73760 | tf_op jit(solution)/shard_map/ppermute | solution.py:295
  31.5 4.6 %collective-permute-done.8.z2 = bf16[144,256]{1,0:T(8,128)(2,1)S(1)} collective-permute-done((bf16[144,256]{1,0:T(8,128)(2,1)S(1)}, bf16[144,256]{1,0:T(8,128)(2,1)S(1)}, u32[]{:S(2)}, u32[]{:S(2)}) %collective-permute-start.8) | collective-permute-done | bytes 73760 | tf_op jit(solution)/shard_map/ppermute | solution.py:295
  36.5 3.5 %collective-permute-start.9 = (bf16[144,256]{1,0:T(8,128)(2,1)S(1)}, bf16[144,256]{1,0:T(8,128)(2,1)S(1)}, u32[]{:S(2)}, u32[]{:S(2)}) collective-permute-start(bf16[144,256]{1,0:T(8,128)(2,1)S(1)} %get-tuple-element.58), channel_id=1, source_target_pairs={{0,4},{1,5},{2,6},{3,7},{4,0},{5,1},{6,2},{7,3},{8,12},{9,13},{10,... | collective-permute-start | bytes 221192 | tf_op jit(solution)/shard_map/ppermute | solution.py:309
  40.0 1.9 %collective-permute-start.11 = (bf16[144,256]{1,0:T(8,128)(2,1)S(1)}, bf16[144,256]{1,0:T(8,128)(2,1)S(1)}, u32[]{:S(2)}, u32[]{:S(2)}) collective-permute-start(bf16[144,256]{1,0:T(8,128)(2,1)S(1)} %get-tuple-element.61), channel_id=1, source_target_pairs={{0,1},{1,0},{2,3},{3,2},{4,20},{5,21},{6,22},{7,23},{8,9},{9,8},{1... | collective-permute-start | bytes 221192 | tf_op jit(solution)/shard_map/ppermute | solution.py:295
  43.6 1.1 %collective-permute-done.11.r1 = bf16[144,256]{1,0:T(8,128)(2,1)S(1)} collective-permute-done((bf16[144,256]{1,0:T(8,128)(2,1)S(1)}, bf16[144,256]{1,0:T(8,128)(2,1)S(1)}, u32[]{:S(2)}, u32[]{:S(2)}) %collective-permute-start.11) | collective-permute-done | bytes 73760 | tf_op jit(solution)/shard_map/ppermute | solution.py:295
  45.1 1.8 %collective-permute-done.13.r3 = bf16[144,256]{1,0:T(8,128)(2,1)S(1)} collective-permute-done((bf16[144,256]{1,0:T(8,128)(2,1)S(1)}, bf16[144,256]{1,0:T(8,128)(2,1)S(1)}, u32[]{:S(2)}, u32[]{:S(2)}) %collective-permute-start.13) | collective-permute-done | bytes 73760 | tf_op jit(solution)/shard_map/ppermute | solution.py:295
  47.3 1.5 %collective-permute-done.14.into = bf16[528,256]{1,0:T(8,128)(2,1)S(1)} collective-permute-done((bf16[528,256]{1,0:T(8,128)(2,1)S(1)}, bf16[528,256]{1,0:T(8,128)(2,1)S(1)}, u32[]{:S(2)}, u32[]{:S(2)}) %collective-permute-start.14) | collective-permute-done | bytes 270368 | tf_op jit(solution)/shard_map/ppermute | solution.py:286
  49.6 2.2 %collective-permute-start.16 = (bf16[256,512]{1,0:T(8,128)(2,1)S(1)}, bf16[256,512]{1,0:T(8,128)(2,1)S(1)}, u32[]{:S(2)}, u32[]{:S(2)}) collective-permute-start(bf16[256,512]{1,0:T(8,128)(2,1)S(1)} %get-tuple-element.71), channel_id=1, source_target_pairs={{0,2},{1,3},{2,0},{3,1},{4,6},{5,7},{6,4},{7,5},{8,10},{9,11},{10,... | collective-permute-start | bytes 786440 | tf_op jit(solution)/shard_map/ppermute | solution.py:278
  52.2 0.9 %collective-permute-start.15 = (bf16[256,512]{1,0:T(8,128)(2,1)S(1)}, bf16[256,512]{1,0:T(8,128)(2,1)S(1)}, u32[]{:S(2)}, u32[]{:S(2)}) collective-permute-start(bf16[256,512]{1,0:T(8,128)(2,1)S(1)} %get-tuple-element.70), channel_id=1, source_target_pairs={{0,1},{1,0},{2,3},{3,2},{4,5},{5,4},{6,7},{7,6},{8,9},{9,8},{10,11... | collective-permute-start | bytes 786440 | tf_op jit(solution)/shard_map/ppermute | solution.py:278
  54.1 4.8 %collective-permute-done.16 = bf16[256,512]{1,0:T(8,128)(2,1)S(1)} collective-permute-done((bf16[256,512]{1,0:T(8,128)(2,1)S(1)}, bf16[256,512]{1,0:T(8,128)(2,1)S(1)}, u32[]{:S(2)}, u32[]{:S(2)}) %collective-permute-start.16) | collective-permute-done | bytes 262176 | tf_op jit(solution)/shard_map/ppermute | solution.py:278
  59.0 5.6 %collective-permute-done.15 = bf16[256,512]{1,0:T(8,128)(2,1)S(1)} collective-permute-done((bf16[256,512]{1,0:T(8,128)(2,1)S(1)}, bf16[256,512]{1,0:T(8,128)(2,1)S(1)}, u32[]{:S(2)}, u32[]{:S(2)}) %collective-permute-start.15) | collective-permute-done | bytes 262176 | tf_op jit(solution)/shard_map/ppermute | solution.py:278
  (50 shorter events, 12.5 us)
Async XLA Ops:
  0.0 11.5 %collective-permute-start = (bf16[256,512]{1,0:T(8,128)(2,1)}, bf16[256,512]{1,0:T(8,128)(2,1)S(1)}, u32[]{:S(2)}, u32[]{:S(2)}) collective-permute-start(bf16[256,512]{1,0:T(8,128)(2,1)} %refs_0_.1), channel_id=1, source_target_pairs={{0,2},{1,3},{2,0},{3,1},{4,6},{5,7},{6,4},{7,5},{8,10},{9,11},{10,... | collective-permute-start | bytes 786440 | tf_op jit(solution)/shard_map/ppermute | solution.py:278
  2.7 12.8 %collective-permute-start.2 = (bf16[256,512]{1,0:T(8,128)(2,1)}, bf16[256,512]{1,0:T(8,128)(2,1)S(1)}, u32[]{:S(2)}, u32[]{:S(2)}) collective-permute-start(bf16[256,512]{1,0:T(8,128)(2,1)} %refs_0_.1), channel_id=1, source_target_pairs={{0,3},{1,2},{2,1},{3,0},{4,7},{5,6},{6,5},{7,4},{8,11},{9,10},{10,... | collective-permute-start | bytes 786440 | tf_op jit(solution)/shard_map/ppermute | solution.py:278
  3.6 12.0 %collective-permute-start.1 = (bf16[256,512]{1,0:T(8,128)(2,1)}, bf16[256,512]{1,0:T(8,128)(2,1)S(1)}, u32[]{:S(2)}, u32[]{:S(2)}) collective-permute-start(bf16[256,512]{1,0:T(8,128)(2,1)} %refs_0_.1), channel_id=1, source_target_pairs={{0,1},{1,0},{2,3},{3,2},{4,5},{5,4},{6,7},{7,6},{8,9},{9,8},{10,11... | collective-permute-start | bytes 786440 | tf_op jit(solution)/shard_map/ppermute | solution.py:278
  4.4 1.6 %copy-start.2 = (bf16[2048,512]{1,0:T(8,128)(2,1)S(1)}, bf16[2048,512]{1,0:T(8,128)(2,1)}, u32[]{:S(2)}) copy-start(bf16[2048,512]{1,0:T(8,128)(2,1)} %refs_3_.1) | copy-start | bytes 6291460
  15.6 12.6 %copy-start.1 = (bf16[2048,512]{1,0:T(8,128)(2,1)S(1)}, bf16[2048,512]{1,0:T(8,128)(2,1)}, u32[]{:S(2)}) copy-start(bf16[2048,512]{1,0:T(8,128)(2,1)} %wg.1) | copy-start | bytes 6291460
  15.6 12.6 %copy-start.3 = (bf16[2048,256]{1,0:T(8,128)(2,1)S(1)}, bf16[2048,256]{1,0:T(8,128)(2,1)}, u32[]{:S(2)}) copy-start(bf16[2048,256]{1,0:T(8,128)(2,1)} %wq.1) | copy-start | bytes 3145732
  15.6 12.6 %copy-start.9 = (s32[256]{0:T(256)S(1)}, s32[256]{0:T(256)}, u32[]{:S(2)}) copy-start(s32[256]{0:T(256)} %param.23) | copy-start | bytes 3076
  15.6 12.6 %copy-start.10 = (f32[512]{0:T(512)S(1)}, f32[512]{0:T(512)}, u32[]{:S(2)}) copy-start(f32[512]{0:T(512)} %param.21) | copy-start | bytes 6148
  18.1 1.9 %collective-permute-start.3 = (bf16[528,256]{1,0:T(8,128)(2,1)S(1)}, bf16[528,256]{1,0:T(8,128)(2,1)S(1)}, u32[]{:S(2)}, u32[]{:S(2)}) collective-permute-start(bf16[528,256]{1,0:T(8,128)(2,1)S(1)} %get-tuple-element.46.mine), channel_id=1, source_target_pairs={{0,4},{4,0},{8,12},{12,8},{16,20},{20,16},{24,28},{28,24},{32,36},... | collective-permute-start | bytes 811016 | tf_op jit(solution)/shard_map/ppermute | solution.py:286
  20.1 4.8 %collective-permute-start.4 = (bf16[144,256]{1,0:T(8,128)(2,1)S(1)}, bf16[144,256]{1,0:T(8,128)(2,1)S(1)}, u32[]{:S(2)}, u32[]{:S(2)}) collective-permute-start(bf16[144,256]{1,0:T(8,128)(2,1)S(1)} %get-tuple-element.48), channel_id=1, source_target_pairs={{0,1},{1,0},{2,3},{3,2},{4,20},{5,21},{6,22},{7,23},{8,9},{9,8},{1... | collective-permute-start | bytes 221192 | tf_op jit(solution)/shard_map/ppermute | solution.py:295
  23.1 3.5 %collective-permute-start.5 = (bf16[144,256]{1,0:T(8,128)(2,1)S(1)}, bf16[144,256]{1,0:T(8,128)(2,1)S(1)}, u32[]{:S(2)}, u32[]{:S(2)}) collective-permute-start(bf16[144,256]{1,0:T(8,128)(2,1)S(1)} %get-tuple-element.49), channel_id=1, source_target_pairs={{0,1},{1,0},{2,3},{3,2},{4,12},{5,13},{6,14},{7,15},{8,9},{9,8},{1... | collective-permute-start | bytes 221192 | tf_op jit(solution)/shard_map/ppermute | solution.py:295
  23.5 4.4 %collective-permute-start.6 = (bf16[144,256]{1,0:T(8,128)(2,1)S(1)}, bf16[144,256]{1,0:T(8,128)(2,1)S(1)}, u32[]{:S(2)}, u32[]{:S(2)}) collective-permute-start(bf16[144,256]{1,0:T(8,128)(2,1)S(1)} %get-tuple-element.50), channel_id=1, source_target_pairs={{0,1},{1,0},{2,3},{3,2},{4,28},{5,29},{6,30},{7,31},{8,9},{9,8},{1... | collective-permute-start | bytes 221192 | tf_op jit(solution)/shard_map/ppermute | solution.py:295
  28.0 3.3 %collective-permute-start.7 = (bf16[144,256]{1,0:T(8,128)(2,1)S(1)}, bf16[144,256]{1,0:T(8,128)(2,1)S(1)}, u32[]{:S(2)}, u32[]{:S(2)}) collective-permute-start(bf16[144,256]{1,0:T(8,128)(2,1)S(1)} %row.1), channel_id=1, source_target_pairs={{0,1},{1,0},{2,3},{3,2},{4,36},{5,37},{6,38},{7,39},{8,9},{9,8},{1... | collective-permute-start | bytes 221192 | tf_op jit(solution)/shard_map/ppermute | solution.py:295
  31.4 4.7 %collective-permute-start.8 = (bf16[144,256]{1,0:T(8,128)(2,1)S(1)}, bf16[144,256]{1,0:T(8,128)(2,1)S(1)}, u32[]{:S(2)}, u32[]{:S(2)}) collective-permute-start(bf16[144,256]{1,0:T(8,128)(2,1)S(1)} %two_rows.1.pair), channel_id=1, source_target_pairs={{0,1},{1,0},{2,3},{3,2},{4,68},{5,69},{6,70},{7,71},{8,9},{9,8},{1... | collective-permute-start | bytes 221192 | tf_op jit(solution)/shard_map/ppermute | solution.py:295
  36.3 7.0 %collective-permute-start.10 = (bf16[144,256]{1,0:T(8,128)(2,1)S(1)}, bf16[144,256]{1,0:T(8,128)(2,1)S(1)}, u32[]{:S(2)}, u32[]{:S(2)}) collective-permute-start(bf16[144,256]{1,0:T(8,128)(2,1)S(1)} %get-tuple-element.58), channel_id=1, source_target_pairs={{0,4},{1,5},{2,6},{3,7},{4,0},{5,1},{6,2},{7,3},{8,12},{9,13},{10,... | collective-permute-start | bytes 221192 | tf_op jit(solution)/shard_map/ppermute | solution.py:309
  36.5 7.1 %collective-permute-start.9 = (bf16[144,256]{1,0:T(8,128)(2,1)S(1)}, bf16[144,256]{1,0:T(8,128)(2,1)S(1)}, u32[]{:S(2)}, u32[]{:S(2)}) collective-permute-start(bf16[144,256]{1,0:T(8,128)(2,1)S(1)} %get-tuple-element.58), channel_id=1, source_target_pairs={{0,4},{1,5},{2,6},{3,7},{4,0},{5,1},{6,2},{7,3},{8,12},{9,13},{10,... | collective-permute-start | bytes 221192 | tf_op jit(solution)/shard_map/ppermute | solution.py:309
  40.0 4.7 %collective-permute-start.11 = (bf16[144,256]{1,0:T(8,128)(2,1)S(1)}, bf16[144,256]{1,0:T(8,128)(2,1)S(1)}, u32[]{:S(2)}, u32[]{:S(2)}) collective-permute-start(bf16[144,256]{1,0:T(8,128)(2,1)S(1)} %get-tuple-element.61), channel_id=1, source_target_pairs={{0,1},{1,0},{2,3},{3,2},{4,20},{5,21},{6,22},{7,23},{8,9},{9,8},{1... | collective-permute-start | bytes 221192 | tf_op jit(solution)/shard_map/ppermute | solution.py:295
  41.9 3.2 %collective-permute-start.12 = (bf16[144,256]{1,0:T(8,128)(2,1)S(1)}, bf16[144,256]{1,0:T(8,128)(2,1)S(1)}, u32[]{:S(2)}, u32[]{:S(2)}) collective-permute-start(bf16[144,256]{1,0:T(8,128)(2,1)S(1)} %get-tuple-element.62), channel_id=1, source_target_pairs={{0,1},{1,0},{2,3},{3,2},{4,12},{5,13},{6,14},{7,15},{8,9},{9,8},{1... | collective-permute-start | bytes 221192 | tf_op jit(solution)/shard_map/ppermute | solution.py:295
  42.5 6.4 %copy-start = (bf16[512,2048]{1,0:T(8,128)(2,1)S(1)}, bf16[512,2048]{1,0:T(8,128)(2,1)}, u32[]{:S(2)}) copy-start(bf16[512,2048]{1,0:T(8,128)(2,1)} %w_out.5) | copy-start | bytes 6291460
  42.5 4.4 %collective-permute-start.13 = (bf16[144,256]{1,0:T(8,128)(2,1)S(1)}, bf16[144,256]{1,0:T(8,128)(2,1)S(1)}, u32[]{:S(2)}, u32[]{:S(2)}) collective-permute-start(bf16[144,256]{1,0:T(8,128)(2,1)S(1)} %get-tuple-element.63), channel_id=1, source_target_pairs={{0,1},{1,0},{2,3},{3,2},{4,28},{5,29},{6,30},{7,31},{8,9},{9,8},{1... | collective-permute-start | bytes 221192 | tf_op jit(solution)/shard_map/ppermute | solution.py:295
  47.1 1.8 %collective-permute-start.14 = (bf16[528,256]{1,0:T(8,128)(2,1)S(1)}, bf16[528,256]{1,0:T(8,128)(2,1)S(1)}, u32[]{:S(2)}, u32[]{:S(2)}) collective-permute-start(bf16[528,256]{1,0:T(8,128)(2,1)S(1)} %get-tuple-element.65), channel_id=1, source_target_pairs={{0,4},{4,0},{8,12},{12,8},{16,20},{20,16},{24,28},{28,24},{32,36},... | collective-permute-start | bytes 811016 | tf_op jit(solution)/shard_map/ppermute | solution.py:286
  49.6 9.4 %collective-permute-start.16 = (bf16[256,512]{1,0:T(8,128)(2,1)S(1)}, bf16[256,512]{1,0:T(8,128)(2,1)S(1)}, u32[]{:S(2)}, u32[]{:S(2)}) collective-permute-start(bf16[256,512]{1,0:T(8,128)(2,1)S(1)} %get-tuple-element.71), channel_id=1, source_target_pairs={{0,2},{1,3},{2,0},{3,1},{4,6},{5,7},{6,4},{7,5},{8,10},{9,11},{10,... | collective-permute-start | bytes 786440 | tf_op jit(solution)/shard_map/ppermute | solution.py:278
  52.2 12.4 %collective-permute-start.15 = (bf16[256,512]{1,0:T(8,128)(2,1)S(1)}, bf16[256,512]{1,0:T(8,128)(2,1)S(1)}, u32[]{:S(2)}, u32[]{:S(2)}) collective-permute-start(bf16[256,512]{1,0:T(8,128)(2,1)S(1)} %get-tuple-element.70), channel_id=1, source_target_pairs={{0,1},{1,0},{2,3},{3,2},{4,5},{5,4},{6,7},{7,6},{8,9},{9,8},{10,11... | collective-permute-start | bytes 786440 | tf_op jit(solution)/shard_map/ppermute | solution.py:278
  53.1 11.9 %collective-permute-start.17 = (bf16[256,512]{1,0:T(8,128)(2,1)S(1)}, bf16[256,512]{1,0:T(8,128)(2,1)S(1)}, u32[]{:S(2)}, u32[]{:S(2)}) collective-permute-start(bf16[256,512]{1,0:T(8,128)(2,1)S(1)} %get-tuple-element.72), channel_id=1, source_target_pairs={{0,3},{1,2},{2,1},{3,0},{4,7},{5,6},{6,5},{7,4},{8,11},{9,10},{10,... | collective-permute-start | bytes 786440 | tf_op jit(solution)/shard_map/ppermute | solution.py:278
  (6 other events, 5.1 us)

commit v5 on v4

--- a/solution.py
+++ b/solution.py
@@ -31,6 +31,7 @@
 
 
 FLIPS = (0, 2, 1, 3)
+Y_FLIPS = (0, 1, 3, 2)
 
 
 def flip(index, bits):
@@ -175,14 +176,14 @@
     total = joined(load(other), load(mine))
     scratch[...] = total[0].astype(BF)
     meta = meta_of(*total[1:])
-    for d, ref in zip(FLIPS, (own, s1, s2, s3)):
+    for d, ref in zip(Y_FLIPS, (own, s1, s2, s3)):
         ref[0:QUARTER] = scratch[at(flip(y, d), QUARTER), :]
         ref[QUARTER:] = meta
 
 
 def stack_rows(parts, stack):
     _, y, _ = place()
-    for d, ref in zip(FLIPS, parts):
+    for d, ref in zip(Y_FLIPS, parts):
         stack[flip(y, d)] = ref[...]
     return [load(stack.at[i]) for i in range(4)]
 
@@ -212,13 +213,13 @@
     for i in range(4):
         save(stack.at[i], run)
         run = joined(run, chips[i])
-    for d, ref in zip(FLIPS, (own_o, s1, s2, s3)):
+    for d, ref in zip(Y_FLIPS, (own_o, s1, s2, s3)):
         ref[...] = stack[flip(y, d)]
 
 
 def unpair_kernel(own, far0, far2, r1, r2, r3, other, into, after):
     _, y, _ = place()
-    for d, ref in zip(FLIPS, (own, r1, r2, r3)):
+    for d, ref in zip(Y_FLIPS, (own, r1, r2, r3)):
         into[at(flip(y, d), QUARTER), :] = ref[0:QUARTER]
     into[V:] = own[QUARTER:]
     save(after, joined(load(into), load(other)))
@@ -311,7 +312,7 @@
 
 def over_y(blocks):
     return [
-        over_chips(b, lambda z, y, d=d: (z, y ^ d)) for d, b in zip(FLIPS[1:], blocks)
+        over_chips(b, lambda z, y, d=d: (z, y ^ d)) for d, b in zip(Y_FLIPS[1:], blocks)
     ]
 
 

time: 66.2 us -> 66.2 us (level)
  transfers between devices with their start and end apart: 18 -> 18, of which waited for: 15 -> 13; matrix products, arithmetic and copies ran while one was open for 1% -> 1% of each run, Pallas kernels for 4% -> 4%
where the time goes in v5:
time: 66.2 us; the launch traced here: 65.9 us
  waiting for transfers between devices  31.5 us (48%)
  starting transfers between devices  19.3 us (29%)
  local copies, waits for them, and re-layouts  7.5 us (11%)
  Pallas kernels  6.6 us (10%)
  other arithmetic  0.84 us (1%)
    ppermute x6, waiting for transfers between devices, over_tp(): return lax.ppermute(block, 'tp', [(i, i ^ bits) for i in range(4)])  15 us
    ppermute x8, waiting for transfers between devices, over_chips(): return lax.ppermute(block, ('seq', 'tp'), route)  13.2 us
    ppermute x8, starting transfers between devices, over_chips(): return lax.ppermute(block, ('seq', 'tp'), route)  7.5 us
    ppermute x6, starting transfers between devices, over_tp(): return lax.ppermute(block, 'tp', [(i, i ^ bits) for i in range(4)])  7.31 us
    unnamed x24, local copies, waits for them, and re-layouts  6.69 us
    pallas_call x12, Pallas kernels, call(): pl.pallas_call(kernel, out_shape=shapes, in_specs=specs or [VM] * len(arg...  6.6 us
    ppermute x2, starting transfers between devices, to_middle(): return lax.ppermute(block, ('seq', 'tp'), route)  3.48 us
    ppermute x2, waiting for transfers between devices, over_seq(): return lax.ppermute(block, 'seq', route)  2.71 us
  transfers between devices with their start and end apart: 18, of which 13 were waited for; matrix products, arithmetic and copies ran while one was open for 1% of the time, Pallas kernels for 4%

profile of v5, /device:TPU:97, one launch (start us, length us, event | category | flops | bytes accessed | tf_op | source)
XLA Modules:
  0.0 65.9 jit_solution(2303139338265721851)
XLA Ops:
  0.0 2.7 %collective-permute-start = (bf16[256,512]{1,0:T(8,128)(2,1)}, bf16[256,512]{1,0:T(8,128)(2,1)S(1)}, u32[]{:S(2)}, u32[]{:S(2)}) collective-permute-start(bf16[256,512]{1,0:T(8,128)(2,1)} %refs_0_.1), channel_id=1, source_target_pairs={{0,2},{1,3},{2,0},{3,1},{4,6},{5,7},{6,4},{7,5},{8,10},{9,11},{10,... | collective-permute-start | bytes 786440 | tf_op jit(solution)/shard_map/ppermute | solution.py:279
  4.4 1.6 %copy-done.2 = bf16[2048,512]{1,0:T(8,128)(2,1)S(1)} copy-done((bf16[2048,512]{1,0:T(8,128)(2,1)S(1)}, bf16[2048,512]{1,0:T(8,128)(2,1)}, u32[]{:S(2)}) %copy-start.2) | copy-done | bytes 2097176
  6.0 1.2 %copy-done.4 = bf16[2048,256]{1,0:T(8,128)(2,1)S(1)} copy-done((bf16[2048,256]{1,0:T(8,128)(2,1)S(1)}, bf16[2048,256]{1,0:T(8,128)(2,1)}, u32[]{:S(2)}) %copy-start.4) | copy-done | bytes 1048600
  7.2 0.9 %copy-done.5 = bf16[256,512]{1,0:T(8,128)(2,1)S(1)} copy-done((bf16[256,512]{1,0:T(8,128)(2,1)S(1)}, bf16[256,512]{1,0:T(8,128)(2,1)}, u32[]{:S(2)}) %copy-start.5) | copy-done | bytes 262168
  11.5 4.0 %collective-permute-done.2.t3 = bf16[256,512]{1,0:T(8,128)(2,1)S(1)} collective-permute-done((bf16[256,512]{1,0:T(8,128)(2,1)}, bf16[256,512]{1,0:T(8,128)(2,1)S(1)}, u32[]{:S(2)}, u32[]{:S(2)}) %collective-permute-start.2) | collective-permute-done | bytes 262176 | tf_op jit(solution)/shard_map/ppermute | solution.py:279
  15.6 2.5 %front.1 = (bf16[4,256,512]{2,1,0:T(8,128)(2,1)S(1)}, bf16[256,256]{1,0:T(8,128)(2,1)S(1)}, bf16[256,512]{1,0:T(8,128)(2,1)S(1)}, f32[256,256]{1,0:T(8,128)S(1)}, bf16[528,256]{1,0:T(8,128)(2,1)S(1)}) custom-call(bf16[256,512]{1,0:T(8,128)(2,1)S(1)} %get-tuple-element.39.t0, bf16[256,512]{1,0:T(8,128)(2,1)S(1)} %collective-permute-done.t1, ...), custom_call_target="tpu_custom_call" | custom-call | flops 822083584 | bytes 6252544 | tf_op jit(solution)/shard_map/front/pallas_call | solution.py:266
  18.8 1.2 %collective-permute-done.3.other = bf16[528,256]{1,0:T(8,128)(2,1)S(1)} collective-permute-done((bf16[528,256]{1,0:T(8,128)(2,1)S(1)}, bf16[528,256]{1,0:T(8,128)(2,1)S(1)}, u32[]{:S(2)}, u32[]{:S(2)}) %collective-permute-start.3) | collective-permute-done | bytes 270368 | tf_op jit(solution)/shard_map/ppermute | solution.py:287
  20.1 1.4 %collective-permute-start.4 = (bf16[144,256]{1,0:T(8,128)(2,1)S(1)}, bf16[144,256]{1,0:T(8,128)(2,1)S(1)}, u32[]{:S(2)}, u32[]{:S(2)}) collective-permute-start(bf16[144,256]{1,0:T(8,128)(2,1)S(1)} %get-tuple-element.48), channel_id=1, source_target_pairs={{0,1},{1,0},{2,3},{3,2},{4,12},{5,13},{6,14},{7,15},{8,9},{9,8},{1... | collective-permute-start | bytes 221192 | tf_op jit(solution)/shard_map/ppermute | solution.py:296
  21.5 1.9 %collective-permute-start.5 = (bf16[144,256]{1,0:T(8,128)(2,1)S(1)}, bf16[144,256]{1,0:T(8,128)(2,1)S(1)}, u32[]{:S(2)}, u32[]{:S(2)}) collective-permute-start(bf16[144,256]{1,0:T(8,128)(2,1)S(1)} %get-tuple-element.49), channel_id=1, source_target_pairs={{0,1},{1,0},{2,3},{3,2},{4,28},{5,29},{6,30},{7,31},{8,9},{9,8},{1... | collective-permute-start | bytes 221192 | tf_op jit(solution)/shard_map/ppermute | solution.py:296
  24.1 1.8 %collective-permute-done.5.r2 = bf16[144,256]{1,0:T(8,128)(2,1)S(1)} collective-permute-done((bf16[144,256]{1,0:T(8,128)(2,1)S(1)}, bf16[144,256]{1,0:T(8,128)(2,1)S(1)}, u32[]{:S(2)}, u32[]{:S(2)}) %collective-permute-start.5) | collective-permute-done | bytes 73760 | tf_op jit(solution)/shard_map/ppermute | solution.py:296
  25.9 2.2 %collective-permute-done.6.r3 = bf16[144,256]{1,0:T(8,128)(2,1)S(1)} collective-permute-done((bf16[144,256]{1,0:T(8,128)(2,1)S(1)}, bf16[144,256]{1,0:T(8,128)(2,1)S(1)}, u32[]{:S(2)}, u32[]{:S(2)}) %collective-permute-start.6) | collective-permute-done | bytes 73760 | tf_op jit(solution)/shard_map/ppermute | solution.py:296
  28.3 1.6 %inner.1 = (bf16[256,256]{1,0:T(8,128)(2,1)S(1)}, f32[256,512]{1,0:T(8,128)S(1)}, f32[256,512]{1,0:T(8,128)S(1)}) custom-call(bf16[4,256,512]{2,1,0:T(8,128)(2,1)S(1)} %get-tuple-element.51.normed, bf16[2048,256]{1,0:T(8,128)(2,1)S(1)} %copy-done.3, bf16[2048,512]{1,0:T(8,128)(2,1)S(1)} %copy-done.1, bf16[256,256]{1,0:T(8,128)(2,1)S(1)} %get-tuple-element.52.key_r, ...), custom_call_target="tpu_custom_call" | custom-call | flops 1073741824 | bytes 6033408 | tf_op jit(solution)/shard_map/inner/pallas_call | solution.py:266
  30.0 1.5 %collective-permute-done.7.beside.z1 = bf16[144,256]{1,0:T(8,128)(2,1)S(1)} collective-permute-done((bf16[144,256]{1,0:T(8,128)(2,1)S(1)}, bf16[144,256]{1,0:T(8,128)(2,1)S(1)}, u32[]{:S(2)}, u32[]{:S(2)}) %collective-permute-start.7) | collective-permute-done | bytes 73760 | tf_op jit(solution)/shard_map/ppermute | solution.py:296
  31.6 4.6 %collective-permute-done.8.z2 = bf16[144,256]{1,0:T(8,128)(2,1)S(1)} collective-permute-done((bf16[144,256]{1,0:T(8,128)(2,1)S(1)}, bf16[144,256]{1,0:T(8,128)(2,1)S(1)}, u32[]{:S(2)}, u32[]{:S(2)}) %collective-permute-start.8) | collective-permute-done | bytes 73760 | tf_op jit(solution)/shard_map/ppermute | solution.py:296
  36.5 3.4 %collective-permute-start.9 = (bf16[144,256]{1,0:T(8,128)(2,1)S(1)}, bf16[144,256]{1,0:T(8,128)(2,1)S(1)}, u32[]{:S(2)}, u32[]{:S(2)}) collective-permute-start(bf16[144,256]{1,0:T(8,128)(2,1)S(1)} %get-tuple-element.58), channel_id=1, source_target_pairs={{0,4},{1,5},{2,6},{3,7},{4,0},{5,1},{6,2},{7,3},{8,12},{9,13},{10,... | collective-permute-start | bytes 221192 | tf_op jit(solution)/shard_map/ppermute | solution.py:310
  39.9 1.0 %collective-permute-start.11 = (bf16[144,256]{1,0:T(8,128)(2,1)S(1)}, bf16[144,256]{1,0:T(8,128)(2,1)S(1)}, u32[]{:S(2)}, u32[]{:S(2)}) collective-permute-start(bf16[144,256]{1,0:T(8,128)(2,1)S(1)} %get-tuple-element.61), channel_id=1, source_target_pairs={{0,1},{1,0},{2,3},{3,2},{4,12},{5,13},{6,14},{7,15},{8,9},{9,8},{1... | collective-permute-start | bytes 221192 | tf_op jit(solution)/shard_map/ppermute | solution.py:296
  40.9 1.2 %collective-permute-start.12 = (bf16[144,256]{1,0:T(8,128)(2,1)S(1)}, bf16[144,256]{1,0:T(8,128)(2,1)S(1)}, u32[]{:S(2)}, u32[]{:S(2)}) collective-permute-start(bf16[144,256]{1,0:T(8,128)(2,1)S(1)} %get-tuple-element.62), channel_id=1, source_target_pairs={{0,1},{1,0},{2,3},{3,2},{4,28},{5,29},{6,30},{7,31},{8,9},{9,8},{1... | collective-permute-start | bytes 221192 | tf_op jit(solution)/shard_map/ppermute | solution.py:296
  42.2 1.1 %collective-permute-start.13 = (bf16[144,256]{1,0:T(8,128)(2,1)S(1)}, bf16[144,256]{1,0:T(8,128)(2,1)S(1)}, u32[]{:S(2)}, u32[]{:S(2)}) collective-permute-start(bf16[144,256]{1,0:T(8,128)(2,1)S(1)} %get-tuple-element.63), channel_id=1, source_target_pairs={{0,1},{1,0},{2,3},{3,2},{4,20},{5,21},{6,22},{7,23},{8,9},{9,8},{1... | collective-permute-start | bytes 221192 | tf_op jit(solution)/shard_map/ppermute | solution.py:296
  43.8 1.5 %collective-permute-done.12.r2 = bf16[144,256]{1,0:T(8,128)(2,1)S(1)} collective-permute-done((bf16[144,256]{1,0:T(8,128)(2,1)S(1)}, bf16[144,256]{1,0:T(8,128)(2,1)S(1)}, u32[]{:S(2)}, u32[]{:S(2)}) %collective-permute-start.12) | collective-permute-done | bytes 73760 | tf_op jit(solution)/shard_map/ppermute | solution.py:296
  45.4 1.5 %collective-permute-done.13.r3 = bf16[144,256]{1,0:T(8,128)(2,1)S(1)} collective-permute-done((bf16[144,256]{1,0:T(8,128)(2,1)S(1)}, bf16[144,256]{1,0:T(8,128)(2,1)S(1)}, u32[]{:S(2)}, u32[]{:S(2)}) %collective-permute-start.13) | collective-permute-done | bytes 73760 | tf_op jit(solution)/shard_map/ppermute | solution.py:296
  47.4 1.5 %collective-permute-done.14.into = bf16[528,256]{1,0:T(8,128)(2,1)S(1)} collective-permute-done((bf16[528,256]{1,0:T(8,128)(2,1)S(1)}, bf16[528,256]{1,0:T(8,128)(2,1)S(1)}, u32[]{:S(2)}, u32[]{:S(2)}) %collective-permute-start.14) | collective-permute-done | bytes 270368 | tf_op jit(solution)/shard_map/ppermute | solution.py:287
  49.6 2.5 %collective-permute-start.16 = (bf16[256,512]{1,0:T(8,128)(2,1)S(1)}, bf16[256,512]{1,0:T(8,128)(2,1)S(1)}, u32[]{:S(2)}, u32[]{:S(2)}) collective-permute-start(bf16[256,512]{1,0:T(8,128)(2,1)S(1)} %get-tuple-element.71), channel_id=1, source_target_pairs={{0,2},{1,3},{2,0},{3,1},{4,6},{5,7},{6,4},{7,5},{8,10},{9,11},{10,... | collective-permute-start | bytes 786440 | tf_op jit(solution)/shard_map/ppermute | solution.py:279
  54.0 5.0 %collective-permute-done.16 = bf16[256,512]{1,0:T(8,128)(2,1)S(1)} collective-permute-done((bf16[256,512]{1,0:T(8,128)(2,1)S(1)}, bf16[256,512]{1,0:T(8,128)(2,1)S(1)}, u32[]{:S(2)}, u32[]{:S(2)}) %collective-permute-start.16) | collective-permute-done | bytes 262176 | tf_op jit(solution)/shard_map/ppermute | solution.py:279
  59.0 5.5 %collective-permute-done.15 = bf16[256,512]{1,0:T(8,128)(2,1)S(1)} collective-permute-done((bf16[256,512]{1,0:T(8,128)(2,1)S(1)}, bf16[256,512]{1,0:T(8,128)(2,1)S(1)}, u32[]{:S(2)}, u32[]{:S(2)}) %collective-permute-start.15) | collective-permute-done | bytes 262176 | tf_op jit(solution)/shard_map/ppermute | solution.py:279
  (50 shorter events, 12.3 us)
Async XLA Ops:
  0.0 11.5 %collective-permute-start = (bf16[256,512]{1,0:T(8,128)(2,1)}, bf16[256,512]{1,0:T(8,128)(2,1)S(1)}, u32[]{:S(2)}, u32[]{:S(2)}) collective-permute-start(bf16[256,512]{1,0:T(8,128)(2,1)} %refs_0_.1), channel_id=1, source_target_pairs={{0,2},{1,3},{2,0},{3,1},{4,6},{5,7},{6,4},{7,5},{8,10},{9,11},{10,... | collective-permute-start | bytes 786440 | tf_op jit(solution)/shard_map/ppermute | solution.py:279
  2.7 12.8 %collective-permute-start.2 = (bf16[256,512]{1,0:T(8,128)(2,1)}, bf16[256,512]{1,0:T(8,128)(2,1)S(1)}, u32[]{:S(2)}, u32[]{:S(2)}) collective-permute-start(bf16[256,512]{1,0:T(8,128)(2,1)} %refs_0_.1), channel_id=1, source_target_pairs={{0,3},{1,2},{2,1},{3,0},{4,7},{5,6},{6,5},{7,4},{8,11},{9,10},{10,... | collective-permute-start | bytes 786440 | tf_op jit(solution)/shard_map/ppermute | solution.py:279
  3.6 12.0 %collective-permute-start.1 = (bf16[256,512]{1,0:T(8,128)(2,1)}, bf16[256,512]{1,0:T(8,128)(2,1)S(1)}, u32[]{:S(2)}, u32[]{:S(2)}) collective-permute-start(bf16[256,512]{1,0:T(8,128)(2,1)} %refs_0_.1), channel_id=1, source_target_pairs={{0,1},{1,0},{2,3},{3,2},{4,5},{5,4},{6,7},{7,6},{8,9},{9,8},{10,11... | collective-permute-start | bytes 786440 | tf_op jit(solution)/shard_map/ppermute | solution.py:279
  4.4 1.6 %copy-start.2 = (bf16[2048,512]{1,0:T(8,128)(2,1)S(1)}, bf16[2048,512]{1,0:T(8,128)(2,1)}, u32[]{:S(2)}) copy-start(bf16[2048,512]{1,0:T(8,128)(2,1)} %refs_3_.1) | copy-start | bytes 6291460
  15.6 12.7 %copy-start.1 = (bf16[2048,512]{1,0:T(8,128)(2,1)S(1)}, bf16[2048,512]{1,0:T(8,128)(2,1)}, u32[]{:S(2)}) copy-start(bf16[2048,512]{1,0:T(8,128)(2,1)} %wg.1) | copy-start | bytes 6291460
  15.6 12.7 %copy-start.3 = (bf16[2048,256]{1,0:T(8,128)(2,1)S(1)}, bf16[2048,256]{1,0:T(8,128)(2,1)}, u32[]{:S(2)}) copy-start(bf16[2048,256]{1,0:T(8,128)(2,1)} %wq.1) | copy-start | bytes 3145732
  15.6 12.8 %copy-start.9 = (s32[256]{0:T(256)S(1)}, s32[256]{0:T(256)}, u32[]{:S(2)}) copy-start(s32[256]{0:T(256)} %param.23) | copy-start | bytes 3076
  15.6 12.8 %copy-start.10 = (f32[512]{0:T(512)S(1)}, f32[512]{0:T(512)}, u32[]{:S(2)}) copy-start(f32[512]{0:T(512)} %param.21) | copy-start | bytes 6148
  18.1 1.9 %collective-permute-start.3 = (bf16[528,256]{1,0:T(8,128)(2,1)S(1)}, bf16[528,256]{1,0:T(8,128)(2,1)S(1)}, u32[]{:S(2)}, u32[]{:S(2)}) collective-permute-start(bf16[528,256]{1,0:T(8,128)(2,1)S(1)} %get-tuple-element.46.mine), channel_id=1, source_target_pairs={{0,4},{4,0},{8,12},{12,8},{16,20},{20,16},{24,28},{28,24},{32,36},... | collective-permute-start | bytes 811016 | tf_op jit(solution)/shard_map/ppermute | solution.py:287
  20.1 4.0 %collective-permute-start.4 = (bf16[144,256]{1,0:T(8,128)(2,1)S(1)}, bf16[144,256]{1,0:T(8,128)(2,1)S(1)}, u32[]{:S(2)}, u32[]{:S(2)}) collective-permute-start(bf16[144,256]{1,0:T(8,128)(2,1)S(1)} %get-tuple-element.48), channel_id=1, source_target_pairs={{0,1},{1,0},{2,3},{3,2},{4,12},{5,13},{6,14},{7,15},{8,9},{9,8},{1... | collective-permute-start | bytes 221192 | tf_op jit(solution)/shard_map/ppermute | solution.py:296
  21.5 4.4 %collective-permute-start.5 = (bf16[144,256]{1,0:T(8,128)(2,1)S(1)}, bf16[144,256]{1,0:T(8,128)(2,1)S(1)}, u32[]{:S(2)}, u32[]{:S(2)}) collective-permute-start(bf16[144,256]{1,0:T(8,128)(2,1)S(1)} %get-tuple-element.49), channel_id=1, source_target_pairs={{0,1},{1,0},{2,3},{3,2},{4,28},{5,29},{6,30},{7,31},{8,9},{9,8},{1... | collective-permute-start | bytes 221192 | tf_op jit(solution)/shard_map/ppermute | solution.py:296
  23.4 4.7 %collective-permute-start.6 = (bf16[144,256]{1,0:T(8,128)(2,1)S(1)}, bf16[144,256]{1,0:T(8,128)(2,1)S(1)}, u32[]{:S(2)}, u32[]{:S(2)}) collective-permute-start(bf16[144,256]{1,0:T(8,128)(2,1)S(1)} %get-tuple-element.50), channel_id=1, source_target_pairs={{0,1},{1,0},{2,3},{3,2},{4,20},{5,21},{6,22},{7,23},{8,9},{9,8},{1... | collective-permute-start | bytes 221192 | tf_op jit(solution)/shard_map/ppermute | solution.py:296
  28.2 3.3 %collective-permute-start.7 = (bf16[144,256]{1,0:T(8,128)(2,1)S(1)}, bf16[144,256]{1,0:T(8,128)(2,1)S(1)}, u32[]{:S(2)}, u32[]{:S(2)}) collective-permute-start(bf16[144,256]{1,0:T(8,128)(2,1)S(1)} %row.1), channel_id=1, source_target_pairs={{0,1},{1,0},{2,3},{3,2},{4,36},{5,37},{6,38},{7,39},{8,9},{9,8},{1... | collective-permute-start | bytes 221192 | tf_op jit(solution)/shard_map/ppermute | solution.py:296
  31.5 4.7 %collective-permute-start.8 = (bf16[144,256]{1,0:T(8,128)(2,1)S(1)}, bf16[144,256]{1,0:T(8,128)(2,1)S(1)}, u32[]{:S(2)}, u32[]{:S(2)}) collective-permute-start(bf16[144,256]{1,0:T(8,128)(2,1)S(1)} %two_rows.1.pair), channel_id=1, source_target_pairs={{0,1},{1,0},{2,3},{3,2},{4,68},{5,69},{6,70},{7,71},{8,9},{9,8},{1... | collective-permute-start | bytes 221192 | tf_op jit(solution)/shard_map/ppermute | solution.py:296
  36.4 6.8 %collective-permute-start.10 = (bf16[144,256]{1,0:T(8,128)(2,1)S(1)}, bf16[144,256]{1,0:T(8,128)(2,1)S(1)}, u32[]{:S(2)}, u32[]{:S(2)}) collective-permute-start(bf16[144,256]{1,0:T(8,128)(2,1)S(1)} %get-tuple-element.58), channel_id=1, source_target_pairs={{0,4},{1,5},{2,6},{3,7},{4,0},{5,1},{6,2},{7,3},{8,12},{9,13},{10,... | collective-permute-start | bytes 221192 | tf_op jit(solution)/shard_map/ppermute | solution.py:310
  36.5 7.3 %collective-permute-start.9 = (bf16[144,256]{1,0:T(8,128)(2,1)S(1)}, bf16[144,256]{1,0:T(8,128)(2,1)S(1)}, u32[]{:S(2)}, u32[]{:S(2)}) collective-permute-start(bf16[144,256]{1,0:T(8,128)(2,1)S(1)} %get-tuple-element.58), channel_id=1, source_target_pairs={{0,4},{1,5},{2,6},{3,7},{4,0},{5,1},{6,2},{7,3},{8,12},{9,13},{10,... | collective-permute-start | bytes 221192 | tf_op jit(solution)/shard_map/ppermute | solution.py:310
  39.9 3.9 %collective-permute-start.11 = (bf16[144,256]{1,0:T(8,128)(2,1)S(1)}, bf16[144,256]{1,0:T(8,128)(2,1)S(1)}, u32[]{:S(2)}, u32[]{:S(2)}) collective-permute-start(bf16[144,256]{1,0:T(8,128)(2,1)S(1)} %get-tuple-element.61), channel_id=1, source_target_pairs={{0,1},{1,0},{2,3},{3,2},{4,12},{5,13},{6,14},{7,15},{8,9},{9,8},{1... | collective-permute-start | bytes 221192 | tf_op jit(solution)/shard_map/ppermute | solution.py:296
  40.9 4.4 %collective-permute-start.12 = (bf16[144,256]{1,0:T(8,128)(2,1)S(1)}, bf16[144,256]{1,0:T(8,128)(2,1)S(1)}, u32[]{:S(2)}, u32[]{:S(2)}) collective-permute-start(bf16[144,256]{1,0:T(8,128)(2,1)S(1)} %get-tuple-element.62), channel_id=1, source_target_pairs={{0,1},{1,0},{2,3},{3,2},{4,28},{5,29},{6,30},{7,31},{8,9},{9,8},{1... | collective-permute-start | bytes 221192 | tf_op jit(solution)/shard_map/ppermute | solution.py:296
  42.2 6.7 %copy-start = (bf16[512,2048]{1,0:T(8,128)(2,1)S(1)}, bf16[512,2048]{1,0:T(8,128)(2,1)}, u32[]{:S(2)}) copy-start(bf16[512,2048]{1,0:T(8,128)(2,1)} %w_out.5) | copy-start | bytes 6291460
  42.2 4.7 %collective-permute-start.13 = (bf16[144,256]{1,0:T(8,128)(2,1)S(1)}, bf16[144,256]{1,0:T(8,128)(2,1)S(1)}, u32[]{:S(2)}, u32[]{:S(2)}) collective-permute-start(bf16[144,256]{1,0:T(8,128)(2,1)S(1)} %get-tuple-element.63), channel_id=1, source_target_pairs={{0,1},{1,0},{2,3},{3,2},{4,20},{5,21},{6,22},{7,23},{8,9},{9,8},{1... | collective-permute-start | bytes 221192 | tf_op jit(solution)/shard_map/ppermute | solution.py:296
  47.1 1.8 %collective-permute-start.14 = (bf16[528,256]{1,0:T(8,128)(2,1)S(1)}, bf16[528,256]{1,0:T(8,128)(2,1)S(1)}, u32[]{:S(2)}, u32[]{:S(2)}) collective-permute-start(bf16[528,256]{1,0:T(8,128)(2,1)S(1)} %get-tuple-element.65), channel_id=1, source_target_pairs={{0,4},{4,0},{8,12},{12,8},{16,20},{20,16},{24,28},{28,24},{32,36},... | collective-permute-start | bytes 811016 | tf_op jit(solution)/shard_map/ppermute | solution.py:287
  49.6 9.4 %collective-permute-start.16 = (bf16[256,512]{1,0:T(8,128)(2,1)S(1)}, bf16[256,512]{1,0:T(8,128)(2,1)S(1)}, u32[]{:S(2)}, u32[]{:S(2)}) collective-permute-start(bf16[256,512]{1,0:T(8,128)(2,1)S(1)} %get-tuple-element.71), channel_id=1, source_target_pairs={{0,2},{1,3},{2,0},{3,1},{4,6},{5,7},{6,4},{7,5},{8,10},{9,11},{10,... | collective-permute-start | bytes 786440 | tf_op jit(solution)/shard_map/ppermute | solution.py:279
  52.5 11.9 %collective-permute-start.15 = (bf16[256,512]{1,0:T(8,128)(2,1)S(1)}, bf16[256,512]{1,0:T(8,128)(2,1)S(1)}, u32[]{:S(2)}, u32[]{:S(2)}) collective-permute-start(bf16[256,512]{1,0:T(8,128)(2,1)S(1)} %get-tuple-element.70), channel_id=1, source_target_pairs={{0,1},{1,0},{2,3},{3,2},{4,5},{5,4},{6,7},{7,6},{8,9},{9,8},{10,11... | collective-permute-start | bytes 786440 | tf_op jit(solution)/shard_map/ppermute | solution.py:279
  53.0 12.0 %collective-permute-start.17 = (bf16[256,512]{1,0:T(8,128)(2,1)S(1)}, bf16[256,512]{1,0:T(8,128)(2,1)S(1)}, u32[]{:S(2)}, u32[]{:S(2)}) collective-permute-start(bf16[256,512]{1,0:T(8,128)(2,1)S(1)} %get-tuple-element.72), channel_id=1, source_target_pairs={{0,3},{1,2},{2,1},{3,0},{4,7},{5,6},{6,5},{7,4},{8,11},{9,10},{10,... | collective-permute-start | bytes 786440 | tf_op jit(solution)/shard_map/ppermute | solution.py:279
  (6 other events, 5.1 us)
